TPU v7x, 32 devices: a whole 2x2x4 slice. The times are simulated.
32 devices in a mesh: seq: 16 (over z, y, x), chan: 2 (over core).
Axes of the slice: x: 2, y: 2, z: 4, core: 2. Of those that a mesh axis runs over, the one named last changes fastest.
Arguments:
- tokens: bfloat16 [32768, 1024], P('seq', 'chan'), may hold values from -30 to 30, as said below
- cotangent: bfloat16 [32768, 1024], P('seq', 'chan'), may hold values from -12 to 12, as said below
- norm_gain: float32 [1024], P('chan'), may hold values from 0.5 to 1.5
- gate_slope: float32 [1024], P('chan'), may hold values from -3 to 3
- gate_bias: float32 [1024], P('chan'), may hold values from -1 to 1
- right_factor: bfloat16 [512, 512], P('chan'), may hold values from -0.25 to 0.25
- left_factor: bfloat16 [64, 64], P('chan'), may hold values from -0.75 to 0.75
- twiddle: float32 [64, 512], P('seq'), may hold values from -4 to 4
Outputs:
- mixed: bfloat16 [32768, 1024], P('seq', 'chan')
- token_grad: bfloat16 [32768, 1024], P('seq', 'chan')
- right_grad: float32 [512, 512], P('seq', 'chan')
- left_grad: float32 [64, 64], P('seq', 'chan')
- twiddle_grad: float32 [64, 512], P('seq')
- gain_grad: float32 [1024], P('chan')
- slope_grad: float32 [1024], P('chan')
- bias_grad: float32 [1024], P('chan')
Inputs may be any that keep to these rules, and one draw needn't show every extreme that they name: `tokens`: Real-valued activations of varying scale. `cotangent`: Real-valued cotangents.
All inputs are finite; a program needn't handle non-finite values.
Results may differ from a plain program's by a relative error of at most 0.0069.
Values may be sent and summed in bfloat16 or wider, within the bound.
No kernel may reach another device: no remote copies, remote signals or barrier semaphores. Data moves between devices by JAX's collectives and lax.ppermute only.
A program may use at most 128 MiB of HBM per device.

v0:
```python
import jax
import jax.numpy as jnp
from jax import lax
from jax.sharding import PartitionSpec as P

D = 1024
B = 512


def on_device(
    tokens, cotangent, norm_gain, gate_slope, gate_bias, right_factor, left_factor, twiddle
):
    row_count, chan_width = tokens.shape
    blocks = row_count // B
    right_whole, left_whole = (
        lax.all_gather(right_factor, "chan", axis=0, tiled=True),
        lax.all_gather(left_factor, "chan", axis=0, tiled=True),
    )
    wide_tokens = tokens.astype(jnp.float32)
    square_sum = lax.psum(jnp.sum(wide_tokens * wide_tokens, axis=1), "chan")
    row_scale = lax.rsqrt(square_sum / D + 1e-05)[:, None]
    normed = wide_tokens * row_scale * norm_gain
    normed_b = normed.astype(jnp.bfloat16).reshape(blocks, B, chan_width)
    gate_value = jax.nn.sigmoid(gate_slope * normed + gate_bias)
    first_mix = jnp.einsum("ij,ajc->aic", right_whole, normed_b, preferred_element_type=jnp.float32)
    twiddle_grid = twiddle[:, :, None]
    spread = (first_mix * twiddle_grid).astype(jnp.bfloat16)
    wide_cot = cotangent.astype(jnp.float32)
    cot_gated = (wide_cot * gate_value).astype(jnp.bfloat16).reshape(blocks, B, chan_width)
    columns = lax.all_to_all(spread, "seq", split_axis=1, concat_axis=0, tiled=True)
    outer_len = columns.shape[0]
    col_flat = columns.reshape(outer_len, -1)
    second_mix = jnp.dot(left_whole, col_flat, preferred_element_type=jnp.float32)
    second_mix = second_mix.astype(jnp.bfloat16).reshape(columns.shape)
    back_rows = (
        lax.all_to_all(second_mix, "seq", split_axis=0, concat_axis=1, tiled=True)
        .reshape(row_count, chan_width)
        .astype(jnp.float32)
    )
    mixed = (gate_value * back_rows).astype(jnp.bfloat16)
    gate_grad = wide_cot * back_rows * gate_value * (1.0 - gate_value)
    cot_columns = lax.all_to_all(cot_gated, "seq", split_axis=1, concat_axis=0, tiled=True)
    cot_flat = cot_columns.reshape(outer_len, -1)
    left_grad = lax.dot_general(
        cot_flat, col_flat, (((1,), (1,)), ((), ())), preferred_element_type=jnp.float32
    )
    spread_grad = lax.dot_general(
        left_whole, cot_flat, (((0,), (0,)), ((), ())), preferred_element_type=jnp.float32
    )
    spread_grad = spread_grad.astype(jnp.bfloat16).reshape(columns.shape)
    grad_back = lax.all_to_all(spread_grad, "seq", split_axis=0, concat_axis=1, tiled=True).astype(
        jnp.float32
    )
    twiddle_part = jnp.sum(grad_back * first_mix, axis=2)
    twiddle_grad = lax.psum(twiddle_part, "chan")
    first_grad = (grad_back * twiddle_grid).astype(jnp.bfloat16)
    right_grad = jnp.einsum("aic,abc->ib", first_grad, normed_b, preferred_element_type=jnp.float32)
    normed_grad = jnp.einsum(
        "ib,aic->abc", right_whole, first_grad, preferred_element_type=jnp.float32
    )
    normed_grad = normed_grad.reshape(row_count, chan_width) + gate_grad * gate_slope
    scaled_grad = normed_grad * norm_gain
    inner_part = jnp.sum(scaled_grad * wide_tokens, axis=1)
    inner_sum = lax.psum(inner_part, "chan")
    token_grad = (
        row_scale * scaled_grad - wide_tokens * row_scale**3 * inner_sum[:, None] / D
    ).astype(jnp.bfloat16)
    gain_grad, slope_grad, bias_grad = lax.psum(
        (
            jnp.sum(normed_grad * wide_tokens * row_scale, axis=0),
            jnp.sum(gate_grad * normed, axis=0),
            jnp.sum(gate_grad, axis=0),
        ),
        "seq",
    )
    right_rows, left_rows = (
        lax.psum_scatter(right_grad, "seq", scatter_dimension=0, tiled=True),
        lax.psum_scatter(left_grad, "seq", scatter_dimension=0, tiled=True),
    )
    right_out, left_out = (
        lax.psum_scatter(right_rows, "chan", scatter_dimension=1, tiled=True),
        lax.psum_scatter(left_rows, "chan", scatter_dimension=1, tiled=True),
    )
    return (mixed, token_grad, right_out, left_out, twiddle_grad, gain_grad, slope_grad, bias_grad)


def solution(mesh):
    return jax.shard_map(
        on_device,
        mesh=mesh,
        in_specs=(
            P("seq", "chan"),
            P("seq", "chan"),
            P("chan"),
            P("chan"),
            P("chan"),
            P("chan", None),
            P("chan", None),
            P("seq", None),
        ),
        out_specs=(
            P("seq", "chan"),
            P("seq", "chan"),
            P("seq", "chan"),
            P("seq", "chan"),
            P("seq", None),
            P("chan"),
            P("chan"),
            P("chan"),
        ),
        check_vma=False,
    )
```

profile of v0, /device:TPU:0, one launch (start us, length us, event | category | flops | bytes accessed | tf_op | source)
XLA Modules:
  0.0 379.4 jit_solution(13754209156722773257)
XLA Ops:
  7.2 2.2 fusion.3
  9.4 2.6 psum.42
  12.0 2.4 all_gather.6
  15.7 4.0 %fusion.22 = (bf16[4,512,512]{1,2,0:T(8,128)(2,1)}, f32[4,512,512]{2,1,0:T(8,128)}) fusion(f32[4,512]{1,0:T(4,128)S(1)} %copy-done.7, bf16[4,512,512]{2,1,0:T(8,128)(2,1)S(1)} %bitcast.79, bf16[512,512]{1,0:T(8,128)(2,1)S(1)} %all_gather.6), kind=kOutput, calls=%fused_computation.36 | convolution fusion | flops 1075838976 | bytes 8921088 | tf_op jit(solution)/shard_map/ij,ajc->aic/dot_general | solution.py:25
  19.7 4.5 %copy.58 = bf16[4,512,512]{2,0,1:T(4,128)(2,1)} copy(bf16[4,512,512]{1,2,0:T(8,128)(2,1)} %get-tuple-element.26) | data formatting | bytes 4194304 | tf_op jit(solution)/shard_map/convert_element_type | solution.py:27
  24.2 8.2 %all-to-all-start = ((bf16[4,512,512]{2,0,1:T(4,128)(2,1)}), bf16[4,512,512]{2,0,1:T(4,128)(2,1)}, u32[]{:S(2)}, u32[]{:S(2)}) async-start(bf16[4,512,512]{2,0,1:T(4,128)(2,1)} %copy.58), calls=%async_computation | async-start | bytes 4194304 | tf_op jit(solution)/shard_map/all_to_all | solution.py:30
  34.3 41.5 %all-to-all-done = bf16[4,512,512]{2,0,1:T(4,128)(2,1)} async-done(((bf16[4,512,512]{2,0,1:T(4,128)(2,1)}), bf16[4,512,512]{2,0,1:T(4,128)(2,1)}, u32[]{:S(2)}, u32[]{:S(2)}) %all-to-all-start) | async-done | bytes 2097184 | tf_op jit(solution)/shard_map/all_to_all | solution.py:30
  80.8 58.2 %all_to_all.48 = bf16[64,32,512]{2,1,0:T(8,128)(2,1)S(1)} all-to-all(bf16[64,32,512]{2,1,0:T(8,128)(2,1)S(1)} %bitcast.84), channel_id=1, replica_groups=mesh['seq'=16,'chan'=2] {'seq'}, dimensions={0} | all-to-all | bytes 4194304 | tf_op jit(solution)/shard_map/all_to_all | solution.py:36
  140.6 4.5 %fusion.2 = (f32[2048,512]{1,0:T(8,128)}, bf16[2048,512]{1,0:T(8,128)(2,1)}, bf16[2048,512]{1,0:T(8,128)(2,1)S(1)}) fusion(bf16[2048,512]{1,0:T(8,128)(2,1)S(1)} %copy-done.6, f32[16,4,32,512]{3,2,0,1:T(8,128)S(1)} %copy.61, f32[512]{0:T(512)S(1)} %copy-done.11, f32[512]{0:T(512)S(1)} %copy-done.8, f32[2048]{0:T(1024)S(1)} %get-tuple-element.25, ...), kind=kLoop, calls=%fused_computation.11 | loop fusion | flops 17825792 | bytes 16791552 | tf_op jit(solution)/shard_map/mul | solution.py:41
  146.7 51.9 %all_to_all.49 = bf16[4,512,512]{2,0,1:T(4,128)(2,1)S(1)} all-to-all(bf16[4,512,512]{2,0,1:T(4,128)(2,1)S(1)} %copy.62), channel_id=1, replica_groups=mesh['seq'=16,'chan'=2] {'seq'}, dimensions={1} | all-to-all | bytes 4194304 | tf_op jit(solution)/shard_map/all_to_all | solution.py:42
  203.4 4.4 %all-to-all-start.3 = ((bf16[64,32,512]{2,1,0:T(8,128)(2,1)}), bf16[64,32,512]{2,1,0:T(8,128)(2,1)}, u32[]{:S(2)}, u32[]{:S(2)}) async-start(bf16[64,32,512]{2,1,0:T(8,128)(2,1)} %bitcast.81), calls=%async_computation.3 | async-start | bytes 4194304 | tf_op jit(solution)/shard_map/all_to_all | solution.py:51
  209.2 2.9 fusion.30
  212.2 37.6 %all-to-all-done.3 = bf16[64,32,512]{2,1,0:T(8,128)(2,1)} async-done(((bf16[64,32,512]{2,1,0:T(8,128)(2,1)}), bf16[64,32,512]{2,1,0:T(8,128)(2,1)}, u32[]{:S(2)}, u32[]{:S(2)}) %all-to-all-start.3) | async-done | bytes 2097184 | tf_op jit(solution)/shard_map/all_to_all | solution.py:51
  249.8 2.2 multiply_convert_fusion
  252.3 2.2 convolution_bitcast_fusion
  256.8 2.5 copy.65
  259.3 5.2 %copy.66 = f32[4,512,512]{1,2,0:T(8,128)} copy(f32[4,512,512]{2,1,0:T(8,128)} %bitcast.75) | data formatting | bytes 8388608 | tf_op jit(solution)/shard_map/convert_element_type | solution.py:51
  264.5 3.7 fusion.24
  268.2 4.1 %fusion.29 = (f32[512]{0:T(512)S(1)}, f32[512]{0:T(512)S(1)}, f32[2048]{0:T(1024)S(1)}, f32[512]{0:T(512)S(1)}, f32[2048,512]{1,0:T(8,128)}) fusion(f32[2048,512]{1,0:T(8,128)S(1)} %copy-done.3, f32[512]{0:T(512)S(1)} %copy-done.8, f32[2048]{0:T(1024)S(1)} %get-tuple-element.25, bf16[2048,512]{1,0:T(8,128)(2,1)S(1)} %copy-done, f32[512]{0:T(512)S(1)} %copy-done.9, ...), kind=kLoop, calls=%fused_computation.49 | loop fusion | flops 14676480 | bytes 14706688 | tf_op jit(solution)/shard_map/reduce_sum | solution.py:72
  272.3 80.7 %all-reduce.1 = (f32[64,64]{1,0:T(8,128)S(1)}, f32[512]{0:T(512)}, f32[512]{0:T(512)}, f32[512]{0:T(512)}) all-reduce(f32[64,64]{1,0:T(8,128)S(1)} %fusion.30, f32[512]{0:T(512)S(1)} %get-tuple-element.13, f32[512]{0:T(512)S(1)} %get-tuple-element.11, f32[512]{0:T(512)S(1)} %get-tuple-element.10), channel_id=4, replica_groups=mesh['seq'=16,'chan'=2] {'seq'}, use_global_device_ids=true, to_apply=%region_6.0.clone | all-reduce | flops 5632 | bytes 45056
  353.7 4.2 %fusion.23 = f32[4,512]{1,0:T(4,128)S(1)} fusion(f32[4,512,512]{1,2,0:T(8,128)} %copy.66, f32[4,512,512]{2,1,0:T(8,128)} %get-tuple-element.27), kind=kLoop, calls=%fused_computation.37 | loop fusion | flops 2095104 | bytes 8396800 | tf_op jit(solution)/shard_map/reduce_sum | solution.py:54
  357.9 3.9 %all-reduce.2 = (f32[2048]{0:T(1024)S(1)}, f32[4,512]{1,0:T(4,128)}) all-reduce(f32[2048]{0:T(1024)S(1)} %get-tuple-element.12, f32[4,512]{1,0:T(4,128)S(1)} %fusion.23), channel_id=1, replica_groups=mesh['seq'=16,'chan'=2] {'chan'}, use_global_device_ids=true, to_apply=%region_3.0 | all-reduce | flops 4096 | bytes 32768 | tf_op jit(solution)/shard_map/psum | solution.py:64
  361.9 3.8 fusion.17
  367.0 5.8 %reduce-scatter.8.cloned.1.call-done = f32[32,256]{1,0:T(8,128)} async-done(((f32[32,512]{1,0:T(8,128)}), f32[32,256]{1,0:T(8,128)}) %reduce-scatter.8.cloned.1.call-update) | async-done | bytes 32784 | tf_op jit(solution)/shard_map/reduce_scatter | solution.py:81
  (57 shorter events, 21.3 us)
Async XLA Ops:
  7.2 7.3 %copy-start = (bf16[2048,512]{1,0:T(8,128)(2,1)S(1)}, bf16[2048,512]{1,0:T(8,128)(2,1)}, u32[]{:S(2)}) copy-start(bf16[2048,512]{1,0:T(8,128)(2,1)} %param.8) | copy-start | bytes 6291460
  7.2 8.5 %copy-start.7 = (f32[4,512]{1,0:T(4,128)S(1)}, f32[4,512]{1,0:T(4,128)}, u32[]{:S(2)}) copy-start(f32[4,512]{1,0:T(4,128)} %param.15) | copy-start | bytes 24580
  15.7 4.1 %copy-start.4 = (bf16[2048,512]{1,0:T(8,128)(2,1)}, bf16[2048,512]{1,0:T(8,128)(2,1)S(1)}, u32[]{:S(2)}) copy-start(bf16[2048,512]{1,0:T(8,128)(2,1)S(1)} %fusion.6) | copy-start | bytes 6291460
  19.7 12.8 %copy-start.10 = (bf16[32,64]{1,0:T(8,128)(2,1)S(1)}, bf16[32,64]{1,0:T(8,128)(2,1)}, u32[]{:S(2)}) copy-start(bf16[32,64]{1,0:T(8,128)(2,1)} %param.14) | copy-start | bytes 12292
  24.2 51.6 %all-to-all-start = ((bf16[4,512,512]{2,0,1:T(4,128)(2,1)}), bf16[4,512,512]{2,0,1:T(4,128)(2,1)}, u32[]{:S(2)}, u32[]{:S(2)}) async-start(bf16[4,512,512]{2,0,1:T(4,128)(2,1)} %copy.58), calls=%async_computation | async-start | bytes 4194304 | tf_op jit(solution)/shard_map/all_to_all | solution.py:30
  79.3 1.5 copy-start.2
  139.0 1.6 copy-start.6
  139.0 1.6 copy-start.8
  139.0 1.6 copy-start.9
  139.0 1.6 copy-start.11
  200.5 2.9 copy-start.1
  201.3 6.7 %copy-start.12 = (u32[32]{0:T(128)S(1)}, u32[32]{0:T(128)}, u32[]{:S(2)}) copy-start(u32[32]{0:T(128)} %constant.14) | copy-start | bytes 388
  203.4 46.4 %all-to-all-start.3 = ((bf16[64,32,512]{2,1,0:T(8,128)(2,1)}), bf16[64,32,512]{2,1,0:T(8,128)(2,1)}, u32[]{:S(2)}, u32[]{:S(2)}) async-start(bf16[64,32,512]{2,1,0:T(8,128)(2,1)} %bitcast.81), calls=%async_computation.3 | async-start | bytes 4194304 | tf_op jit(solution)/shard_map/all_to_all | solution.py:51
  207.8 154.0 %reduce-scatter.6.cloned.1.call-start = ((), (), s32[]{:S(2)}) async-start(), calls=%async_computation.7 | async-start | bytes 1114112 | tf_op jit(solution)/shard_map/reduce_scatter | solution.py:77
  249.8 2.5 copy-start.5
  254.6 111.1 %reduce-scatter.10.cloned.1.call-start = ((), (), s32[]{:S(2)}) async-start(), calls=%async_computation.9 | async-start | bytes 49152
  264.5 3.7 copy-start.3
  357.9 14.9 %reduce-scatter.8.cloned.1.call-start = ((), (), s32[]{:S(2)}) async-start(), calls=%async_computation.8 | async-start | bytes 98304 | tf_op jit(solution)/shard_map/reduce_scatter | solution.py:81
Sparse Core Ops, SparseCore 0:
  254.7 81.9 reduce-scatter.5
  358.0 3.2 reduce-scatter.9
  364.2 8.5 reduce-scatter.7
where the time goes:
time: 380 us; the launch traced here: 379 us
  blocking collectives  202 us (53%)
  waiting for transfers between devices  85 us (22%)
  local copies, waits for them, and re-layouts  26.7 us (7%)
  other arithmetic  24.4 us (6%)
  between operations  14.7 us (4%)
  matrix products  14.3 us (4%)
  starting transfers between devices  12.8 us (3%)
    unnamed x1, blocking collectives  80.7 us
    all_to_all x1, blocking collectives, on_device(): lax.all_to_all(second_mix, 'seq', split_axis=0, concat_axis=1, tiled=True)  58.2 us
    all_to_all x1, blocking collectives, on_device(): lax.all_to_all(cot_gated, 'seq', split_axis=1, concat_axis=0, tiled=True)  51.9 us
    all_to_all x1, waiting for transfers between devices, on_device(): lax.all_to_all(spread, 'seq', split_axis=1, concat_axis=0, tiled=True)  41.5 us
    all_to_all x1, waiting for transfers between devices, on_device(): lax.all_to_all(spread_grad, 'seq', split_axis=0, concat_axis=1, tiled=True)  37.6 us
    unnamed x34, local copies, waits for them, and re-layouts  9.08 us
    all_to_all x1, starting transfers between devices, on_device(): lax.all_to_all(spread, 'seq', split_axis=1, concat_axis=0, tiled=True)  8.24 us
    convert_element_type x2, local copies, waits for them, and re-layouts, on_device(): lax.all_to_all(spread_grad, 'seq', split_axis=0, concat_axis=1, tiled=True)  7.71 us
  transfers between devices with their start and end apart: 5, of which 3 were waited for; matrix products, arithmetic and copies ran while one was open for 8% of the time, Pallas kernels for 0%

commit v1 on v0

v1 whole, which is shorter than its diff:
```python
import functools

import jax
import jax.numpy as jnp
from jax import lax
from jax.experimental import pallas as pl
from jax.experimental.pallas import tpu as pltpu
from jax.sharding import PartitionSpec as P

D = 1024
B = 512
EPS = 1e-05
LAG = 8

F32 = jnp.float32
BF16 = jnp.bfloat16


def sds(shape, dtype):
    return jax.ShapeDtypeStruct(shape, dtype)


def cost(flops, nbytes):
    return pl.CostEstimate(flops=int(flops), bytes_accessed=int(nbytes), transcendentals=0)


def params():
    return pltpu.CompilerParams(vmem_limit_bytes=56 * 1024 * 1024)


def whole(shape):
    zeros = (0,) * len(shape)
    return pl.BlockSpec(shape, lambda *_: zeros)


def partners(n, sign):
    me = lax.axis_index("seq")
    hi, lo = me // 4, me % 4
    high = n // 4
    lo_of = [lo, lo + 1 - 2 * (lo % 2), (lo + 2) % 4, 3 - lo]
    return [
        ((hi + (sign * (k // 4)) % high) % high) * 4 + lo_of[k % 4]
        for k in range(n)
    ]


def pairs(n, k):
    high = n // 4
    return [
        (i, ((i // 4 + k // 4) % high) * 4 + ((i % 4) ^ (k % 4)))
        for i in range(n)
    ]


def send_order(n):
    high = n // 4
    far_first = sorted(range(1, high), key=lambda d: (abs(d - high / 2), d))
    order = []
    for dl in range(4):
        order += [4 * dh + dl for dh in far_first]
        if dl < 3:
            order.append(dl + 1)
    return order


def exchange(blocks):
    n = len(blocks)
    out = list(blocks)
    for k in send_order(n):
        out[k] = lax.ppermute(blocks[k], "seq", pairs(n, k))
    return out


def after_part(values, started):
    keys = send_order(len(started))[:LAG]
    values, held = lax.optimization_barrier((values, [started[k] for k in keys]))
    started = list(started)
    for k, v in zip(keys, held):
        started[k] = v
    return values, started


def chan_terms(x):
    nc = lax.axis_size("chan")
    if nc == 2:
        return x, lax.ppermute(x, "chan", [(0, 1), (1, 0)])
    return lax.psum(x, "chan"), jnp.zeros_like(x)


def chan_gather(x):
    nc = lax.axis_size("chan")
    if nc != 2:
        return lax.all_gather(x, "chan", axis=0, tiled=True)
    other = lax.ppermute(x, "chan", [(0, 1), (1, 0)])
    first = lax.axis_index("chan") == 0
    return jnp.concatenate(
        [jnp.where(first, x, other), jnp.where(first, other, x)], axis=0
    )


def chan_scatter(x):
    nc = lax.axis_size("chan")
    if nc != 2:
        return lax.psum_scatter(x, "chan", scatter_dimension=x.ndim - 1, tiled=True)
    half = x.shape[-1] // 2
    first = lax.axis_index("chan") == 0
    low, high = x[..., :half], x[..., half:]
    other = lax.ppermute(jnp.where(first, high, low), "chan", [(0, 1), (1, 0)])
    return jnp.where(first, low, high) + other


def row_sums(x):
    high = x.astype(BF16)
    low = (x - high.astype(F32)).astype(BF16)
    ones = jnp.ones((8, x.shape[1]), BF16)
    dims = (((1,), (1,)), ((), ()))
    return lax.dot_general(ones, high, dims, preferred_element_type=F32) + lax.dot_general(
        ones, low, dims, preferred_element_type=F32
    )


def column(rows):
    return rows.T[:, :1]


def scale_of(sa_ref, sb_ref):
    return column(lax.rsqrt((sa_ref[...] + sb_ref[...]) / D + EPS))


sigmoid = jax.nn.sigmoid


def squares_kernel(tok_ref, out_ref):
    x = tok_ref[...].astype(F32)
    out_ref[...] = row_sums(x * x)


def squares(tokens):
    rows, width = tokens.shape
    return pl.pallas_call(
        squares_kernel,
        grid=(rows // B,),
        in_specs=[pl.BlockSpec((B, width), lambda a: (a, 0))],
        out_specs=pl.BlockSpec((8, B), lambda a: (0, a)),
        out_shape=sds((8, rows), F32),
        compiler_params=params(),
        cost_estimate=cost(8 * rows * width, 2 * rows * width),
        name="squares",
    )(tokens)


def gate_kernel(n, tok_ref, cot_ref, sa_ref, sb_ref, gain_ref, slope_ref, bias_ref, *rest):
    nb_ref, outs, held = rest[0], rest[1 : 1 + n], rest[1 + n]
    size = B // n
    normed = tok_ref[...].astype(F32) * scale_of(sa_ref, sb_ref) * gain_ref[...]
    nb_ref[0] = normed.astype(BF16)
    gate = sigmoid(slope_ref[...] * normed + bias_ref[...])
    held[...] = (cot_ref[...].astype(F32) * gate).astype(BF16)
    for k, dest in enumerate(partners(n, 1)):
        outs[k][0] = held[pl.ds(pl.multiple_of(dest * size, size), size), :]


def gate_cotangent(n, tokens, cotangent, sa, sb, gain, slope, bias):
    rows, width = tokens.shape
    blocks = rows // B
    size = B // n
    tall = pl.BlockSpec((B, width), lambda a: (a, 0))
    row = pl.BlockSpec((8, B), lambda a: (0, a))
    vec = whole((1, width))
    result = pl.pallas_call(
        functools.partial(gate_kernel, n),
        grid=(blocks,),
        in_specs=[tall, tall, row, row, vec, vec, vec],
        out_specs=[pl.BlockSpec((1, B, width), lambda a: (a, 0, 0))]
        + [pl.BlockSpec((1, size, width), lambda a: (a, 0, 0))] * n,
        out_shape=[sds((blocks, B, width), BF16)] + [sds((blocks, size, width), BF16)] * n,
        scratch_shapes=[pltpu.VMEM((B, width), BF16)],
        compiler_params=params(),
        cost_estimate=cost(20 * rows * width, 8 * rows * width),
        name="gate_cotangent",
    )(tokens, cotangent, sa, sb, gain, slope, bias)
    return result[0], list(result[1:])


def twiddle_column(tw_ref, a):
    return column(jnp.broadcast_to(tw_ref[pl.ds(a, 1), :], (8, tw_ref.shape[1])))


def first_kernel(n, nb_ref, right_ref, tw_ref, *rest):
    first_ref, outs, held = rest[0], rest[1 : 1 + n], rest[1 + n]
    size = B // n
    first = jnp.dot(right_ref[...], nb_ref[0], preferred_element_type=F32)
    first_ref[0] = first
    held[...] = (first * twiddle_column(tw_ref, pl.program_id(0))).astype(BF16)
    for k, dest in enumerate(partners(n, 1)):
        outs[k][0] = held[pl.ds(pl.multiple_of(dest * size, size), size), :]


def first_factor(n, normed_b, right, twiddle):
    blocks, _, width = normed_b.shape
    size = B // n
    block = pl.BlockSpec((1, B, width), lambda a: (a, 0, 0))
    result = pl.pallas_call(
        functools.partial(first_kernel, n),
        grid=(blocks,),
        in_specs=[block, whole((B, B)), whole((blocks, B))],
        out_specs=[block] + [pl.BlockSpec((1, size, width), lambda a: (a, 0, 0))] * n,
        out_shape=[sds((blocks, B, width), F32)] + [sds((blocks, size, width), BF16)] * n,
        scratch_shapes=[pltpu.VMEM((B, width), BF16)],
        compiler_params=params(),
        cost_estimate=cost(2 * blocks * B * B * width, 8 * blocks * B * width),
        name="first_factor",
    )(normed_b, right, twiddle)
    return result[0], list(result[1:])


def group_of(n):
    return min(16, B // n)


def spread_matrix(rows, cols, group, offset, transposed):
    shape = (cols, rows) if transposed else (rows, cols)
    m = lax.broadcasted_iota(jnp.int32, shape, 1 if transposed else 0) + offset
    r = lax.broadcasted_iota(jnp.int32, shape, 0 if transposed else 1)
    inside = (m >= r * group) & (m < (r + 1) * group)
    return jnp.where(inside, 1.0, 0.0).astype(BF16)


def same_place(rows, cols, group, offset):
    m = lax.broadcasted_iota(jnp.int32, (rows, cols), 0) + offset
    q = lax.broadcasted_iota(jnp.int32, (rows, cols), 1)
    return lax.rem(m, group) == lax.rem(q, group)


def widen_kernel(group, left_ref, fore_ref, back_ref):
    step, total = fore_ref.shape
    outer = left_ref.shape[0]
    offset = pl.program_id(0) * step
    rows = spread_matrix(step, outer, group, offset, False)
    cols = spread_matrix(total, outer, group, 0, True)
    same = same_place(step, total, group, offset)
    left = left_ref[...]
    for source, out_ref in ((left, fore_ref), (left.astype(F32).T.astype(BF16), back_ref)):
        part = jnp.dot(rows, source, preferred_element_type=F32).astype(BF16)
        full = jnp.dot(part, cols, preferred_element_type=F32)
        out_ref[...] = jnp.where(same, full, 0.0).astype(BF16)


def widen(left, group):
    outer = left.shape[0]
    total = outer * group
    step = 256
    spec = pl.BlockSpec((step, total), lambda i: (i, 0))
    return pl.pallas_call(
        functools.partial(widen_kernel, group),
        grid=(total // step,),
        in_specs=[whole((outer, outer))],
        out_specs=[spec, spec],
        out_shape=[sds((total, total), BF16)] * 2,
        compiler_params=params(),
        cost_estimate=cost(4 * total * total * outer, 4 * total * total),
        name="widen",
    )(left)


def second_kernel(n, group, mat_ref, *rest):
    ins, outs, held, done = rest[:n], rest[n : 2 * n], rest[2 * n], rest[2 * n + 1]
    count, size, width = ins[0].shape
    sources, dests = partners(n, -1), partners(n, 1)
    span = count * group
    for g in range(size // group):
        part = pl.ds(g * group, group)
        for k in range(n):
            held[g, pl.ds(sources[k] * count, count)] = ins[k][:, part, :]
    for g in range(size // group):
        flat = held[g].reshape(-1, width)
        done[g] = jnp.dot(mat_ref[...], flat, preferred_element_type=F32).astype(BF16)
    for g in range(size // group):
        part = pl.ds(g * group, group)
        for k in range(n):
            place = pl.ds(pl.multiple_of(dests[k] * span, span), span)
            outs[k][:, part, :] = done[g, place, :].reshape(count, group, width)


def second_factor(n, matrix, blocks, name):
    count, size, width = blocks[0].shape
    group = group_of(n)
    total = matrix.shape[0]
    step = min(256, width)
    spec = pl.BlockSpec((count, size, step), lambda c: (0, 0, c))
    groups = size // group
    scratch = pltpu.VMEM((groups, n * count, group, step), BF16)
    return list(
        pl.pallas_call(
            functools.partial(second_kernel, n, group),
            grid=(width // step,),
            in_specs=[whole((total, total))] + [spec] * n,
            out_specs=[spec] * n,
            out_shape=[sds((count, size, width), BF16)] * n,
            scratch_shapes=[scratch, pltpu.VMEM((groups, total, step), BF16)],
            compiler_params=params(),
            cost_estimate=cost(2 * total * total * width * (size // group), 8 * n * count * size * width),
            name=name,
        )(matrix, *blocks)
    )


def left_kernel(n, group, *rest):
    cots, spreads, out_ref = rest[:n], rest[n : 2 * n], rest[2 * n]
    held_c, held_s, total_ref = rest[2 * n + 1 :]
    count, size, width = cots[0].shape
    sources = partners(n, -1)
    dims = (((1,), (1,)), ((), ()))

    @pl.when(pl.program_id(0) == 0)
    def _():
        total_ref[...] = jnp.zeros_like(total_ref)

    for g in range(size // group):
        part = pl.ds(g * group, group)
        for k in range(n):
            held_c[g, pl.ds(sources[k] * count, count)] = cots[k][:, part, :]
            held_s[g, pl.ds(sources[k] * count, count)] = spreads[k][:, part, :]
    for g in range(size // group):
        total_ref[...] += lax.dot_general(
            held_c[g].reshape(-1, width),
            held_s[g].reshape(-1, width),
            dims,
            preferred_element_type=F32,
        )

    @pl.when(pl.program_id(0) == pl.num_programs(0) - 1)
    def _():
        size_all = total_ref.shape[0]
        outer = size_all // group
        kept = jnp.where(same_place(size_all, size_all, group, 0), total_ref[...], 0.0)
        summed = kept.reshape(outer, group, size_all).sum(axis=1)
        gather = spread_matrix(size_all, outer, group, 0, False).astype(F32)
        out_ref[...] = jnp.dot(
            summed, gather, preferred_element_type=F32, precision=lax.Precision.HIGHEST
        )


def left_gradient(n, cots, spreads):
    count, size, width = cots[0].shape
    group = group_of(n)
    outer = n * count
    total = outer * group
    step = min(256, width)
    spec = pl.BlockSpec((count, size, step), lambda c: (0, 0, c))
    scratch = pltpu.VMEM((size // group, outer, group, step), BF16)
    return pl.pallas_call(
        functools.partial(left_kernel, n, group),
        grid=(width // step,),
        in_specs=[spec] * (2 * n),
        out_specs=whole((outer, outer)),
        out_shape=sds((outer, outer), F32),
        scratch_shapes=[scratch, scratch, pltpu.VMEM((total, total), F32)],
        compiler_params=params(),
        cost_estimate=cost(2 * total * total * width * (size // group), 8 * n * count * size * width),
        name="left_gradient",
    )(*cots, *spreads)


def back_kernel(n, first_ref, nb_ref, right_ref, tw_ref, *rest):
    ins, (twg_ref, rg_ref, mm_ref), (held, turned) = rest[:n], rest[n : n + 3], rest[n + 3 :]
    size = B // n
    a = pl.program_id(0)

    @pl.when(a == 0)
    def _():
        turned[...] = right_ref[...].astype(F32).T.astype(BF16)
        rg_ref[...] = jnp.zeros_like(rg_ref)

    for k, source in enumerate(partners(n, -1)):
        held[pl.ds(pl.multiple_of(source * size, size), size), :] = ins[k][0]
    grad = held[...].astype(F32)
    twg_ref[0] = row_sums(grad * first_ref[0])
    first_grad = (grad * twiddle_column(tw_ref, a)).astype(BF16)
    rg_ref[...] += lax.dot_general(
        first_grad, nb_ref[0], (((1,), (1,)), ((), ())), preferred_element_type=F32
    )
    mm_ref[0] = jnp.dot(turned[...], first_grad, preferred_element_type=F32)


def back_first(n, blocks, first_mix, normed_b, right, twiddle):
    count, _, width = normed_b.shape
    size = B // n
    block = pl.BlockSpec((1, B, width), lambda a: (a, 0, 0))
    return pl.pallas_call(
        functools.partial(back_kernel, n),
        grid=(count,),
        in_specs=[block, block, whole((B, B)), whole((count, B))]
        + [pl.BlockSpec((1, size, width), lambda a: (a, 0, 0))] * n,
        out_specs=[pl.BlockSpec((1, 8, B), lambda a: (a, 0, 0)), whole((B, B)), block],
        out_shape=[sds((count, 8, B), F32), sds((B, B), F32), sds((count, B, width), F32)],
        scratch_shapes=[pltpu.VMEM((B, width), BF16), pltpu.VMEM((B, B), BF16)],
        compiler_params=params(),
        cost_estimate=cost(4 * count * B * B * width, 12 * count * B * width),
        name="back_first",
    )(first_mix, normed_b, right, twiddle, *blocks)


def finish_kernel(n, tok_ref, cot_ref, sa_ref, sb_ref, gain_ref, slope_ref, bias_ref, mm_ref, *rest):
    ins, (mixed_ref, scaled_ref, inner_ref, sums_ref), held = rest[:n], rest[n : n + 4], rest[n + 4]
    size = B // n

    @pl.when(pl.program_id(0) == 0)
    def _():
        sums_ref[...] = jnp.zeros_like(sums_ref)

    for k, source in enumerate(partners(n, -1)):
        held[pl.ds(pl.multiple_of(source * size, size), size), :] = ins[k][0]
    second = held[...].astype(F32)
    wide = tok_ref[...].astype(F32)
    unit = wide * scale_of(sa_ref, sb_ref)
    normed = unit * gain_ref[...]
    gate = sigmoid(slope_ref[...] * normed + bias_ref[...])
    mixed_ref[...] = (gate * second).astype(BF16)
    gate_grad = cot_ref[...].astype(F32) * second * gate * (1.0 - gate)
    normed_grad = mm_ref[0] + gate_grad * slope_ref[...]
    scaled = normed_grad * gain_ref[...]
    scaled_ref[...] = scaled
    inner_ref[...] = row_sums(scaled * wide)
    sums_ref[0:1, :] += jnp.sum(normed_grad * unit, axis=0, keepdims=True)
    sums_ref[1:2, :] += jnp.sum(gate_grad * normed, axis=0, keepdims=True)
    sums_ref[2:3, :] += jnp.sum(gate_grad, axis=0, keepdims=True)


def finish(n, blocks, tokens, cotangent, sa, sb, gain, slope, bias, mm):
    rows, width = tokens.shape
    size = B // n
    tall = pl.BlockSpec((B, width), lambda a: (a, 0))
    row = pl.BlockSpec((8, B), lambda a: (0, a))
    vec = whole((1, width))
    return pl.pallas_call(
        functools.partial(finish_kernel, n),
        grid=(rows // B,),
        in_specs=[tall, tall, row, row, vec, vec, vec, pl.BlockSpec((1, B, width), lambda a: (a, 0, 0))]
        + [pl.BlockSpec((1, size, width), lambda a: (a, 0, 0))] * n,
        out_specs=[tall, tall, row, whole((8, width))],
        out_shape=[sds((rows, width), BF16), sds((rows, width), F32), sds((8, rows), F32), sds((8, width), F32)],
        scratch_shapes=[pltpu.VMEM((B, width), BF16)],
        compiler_params=params(),
        cost_estimate=cost(40 * rows * width, 16 * rows * width),
        name="finish",
    )(tokens, cotangent, sa, sb, gain, slope, bias, mm, *blocks)


def token_kernel(tok_ref, scaled_ref, sa_ref, sb_ref, ia_ref, ib_ref, out_ref):
    scale = lax.rsqrt((sa_ref[...] + sb_ref[...]) / D + EPS)
    inner = (ia_ref[...] + ib_ref[...]) * (scale * scale * scale) / D
    out_ref[...] = (
        column(scale) * scaled_ref[...] - tok_ref[...].astype(F32) * column(inner)
    ).astype(BF16)


def token_gradient(tokens, scaled, sa, sb, ia, ib):
    rows, width = tokens.shape
    tall = pl.BlockSpec((B, width), lambda a: (a, 0))
    row = pl.BlockSpec((8, B), lambda a: (0, a))
    return pl.pallas_call(
        token_kernel,
        grid=(rows // B,),
        in_specs=[tall, tall, row, row, row, row],
        out_specs=tall,
        out_shape=sds((rows, width), BF16),
        compiler_params=params(),
        cost_estimate=cost(5 * rows * width, 8 * rows * width),
        name="token_gradient",
    )(tokens, scaled, sa, sb, ia, ib)


def on_device(
    tokens, cotangent, norm_gain, gate_slope, gate_bias, right_factor, left_factor, twiddle
):
    n = lax.axis_size("seq")
    rows, width = tokens.shape
    gain, slope, bias = (v.reshape(1, width) for v in (norm_gain, gate_slope, gate_bias))
    sa, sb = chan_terms(squares(tokens))
    normed_b, cot_blocks = gate_cotangent(n, tokens, cotangent, sa, sb, gain, slope, bias)
    cot_cols = exchange(cot_blocks)
    right = chan_gather(right_factor)
    first_mix, spread_blocks = first_factor(n, normed_b, right, twiddle)
    spread_cols = exchange(spread_blocks)
    fore, back = widen(chan_gather(left_factor), group_of(n))

    cot_cols, spread_cols = after_part(cot_cols, spread_cols)
    grad_back = exchange(second_factor(n, back, cot_cols, "spread_grad"))
    spread_cols, grad_back = after_part(spread_cols, grad_back)
    mix_back = exchange(second_factor(n, fore, spread_cols, "second_mix"))
    left_part = left_gradient(n, cot_cols, spread_cols)
    grad_back, mix_back = after_part(grad_back, mix_back)
    twiddle_rows, right_part, mm = back_first(n, grad_back, first_mix, normed_b, right, twiddle)
    ta, tb = chan_terms(twiddle_rows)
    twiddle_grad = ta[:, 0] + tb[:, 0]
    right_part = chan_scatter(right_part)
    left_part = chan_scatter(left_part)

    mixed, scaled, inner, sums = finish(
        n, mix_back, tokens, cotangent, sa, sb, gain, slope, bias, mm
    )
    ia, ib = chan_terms(inner)
    token_grad = token_gradient(tokens, scaled, sa, sb, ia, ib)

    right_flat = right_part.reshape(n, -1)
    left_flat = left_part.reshape(n, -1)
    small = jnp.broadcast_to(sums[:3].reshape(1, -1), (n, 3 * width))
    sizes = [right_flat.shape[1], left_flat.shape[1]]
    parts = lax.all_to_all(
        jnp.concatenate([right_flat, left_flat, small], axis=1), "seq", 0, 0
    )
    total = jnp.sum(parts, axis=0)
    right_out = total[: sizes[0]].reshape(B // n, -1)
    left_out = total[sizes[0] : sizes[0] + sizes[1]].reshape(left_part.shape[0] // n, -1)
    vectors = total[sizes[0] + sizes[1] :].reshape(3, width)
    return (
        mixed,
        token_grad,
        right_out,
        left_out,
        twiddle_grad,
        vectors[0],
        vectors[1],
        vectors[2],
    )


def solution(mesh):
    return jax.shard_map(
        on_device,
        mesh=mesh,
        in_specs=(
            P("seq", "chan"),
            P("seq", "chan"),
            P("chan"),
            P("chan"),
            P("chan"),
            P("chan", None),
            P("chan", None),
            P("seq", None),
        ),
        out_specs=(
            P("seq", "chan"),
            P("seq", "chan"),
            P("seq", "chan"),
            P("seq", "chan"),
            P("seq", None),
            P("chan"),
            P("chan"),
            P("chan"),
        ),
        check_vma=False,
    )
```

time: 380 us -> 273 us (0.72)
  blocking collectives: 202 us -> 0 us
  starting transfers between devices: 12.8 us -> 148 us
  Pallas kernels: 0 us -> 62.2 us
  waiting for transfers between devices: 85 us -> 47.6 us
  local copies, waits for them, and re-layouts: 26.7 us -> 6.85 us
  other arithmetic: 24.4 us -> 5.14 us
  matrix products: 14.3 us -> 0 us
  between operations: 14.7 us -> 1.59 us
    ppermute x0 -> x67, starting transfers between devices: none -> 142 us  [the longest x60 140 us: exchange(): out[k] = lax.ppermute(blocks[k], 'seq', pairs(n, k))]
    all_to_all x2 -> x0, blocking collectives: 110 us -> none  [the longest x1 58.2 us: on_device(): lax.all_to_all(second_mix, 'seq', split_axis=0, concat_axis=1, tiled=True)]
    unnamed x1 -> x0, blocking collectives: 80.7 us -> none
    all_to_all x2 -> x1, waiting for transfers between devices: 79.1 us -> 8.57 us  [on_device(): lax.all_to_all(jnp.concatenate([right_flat, left_flat, small], axis=1), '...]
    pallas_call x0 -> x10, Pallas kernels: none -> 62.2 us  [the longest x2 12.1 us: second_factor(): pl.pallas_call(functools.partial(second_kernel, n, group), grid=(width //...]
    ppermute x0 -> x67, waiting for transfers between devices: none -> 39 us  [the longest x60 34.5 us: exchange(): out[k] = lax.ppermute(blocks[k], 'seq', pairs(n, k))]
    dot_general x6 -> x0, matrix products: 14.3 us -> none  [the longest x1 4.03 us: on_device(): jnp.einsum('ij,ajc->aic', right_whole, normed_b, preferred_element_type=j...]
    convert_element_type x5 -> x0, local copies, waits for them, and re-layouts: 13 us -> none  [the longest x2 7.71 us: on_device(): lax.all_to_all(spread_grad, 'seq', split_axis=0, concat_axis=1, tiled=True)]
  transfers between devices with their start and end apart: 5 -> 68, of which waited for: 3 -> 20; matrix products, arithmetic and copies ran while one was open for 8% -> 2% of each run, Pallas kernels for 0% -> 20%
where the time goes in v1:
time: 273 us; the launch traced here: 272 us
  starting transfers between devices  148 us (54%)
  Pallas kernels  62.2 us (23%)
  waiting for transfers between devices  47.6 us (17%)
  local copies, waits for them, and re-layouts  6.85 us (3%)
  other arithmetic  5.14 us (2%)
    ppermute x60, starting transfers between devices, exchange(): out[k] = lax.ppermute(blocks[k], 'seq', pairs(n, k))  140 us
    ppermute x60, waiting for transfers between devices, exchange(): out[k] = lax.ppermute(blocks[k], 'seq', pairs(n, k))  34.5 us
    pallas_call x2, Pallas kernels, second_factor(): pl.pallas_call(functools.partial(second_kernel, n, group), grid=(width //...  12.1 us
    pallas_call x1, Pallas kernels, finish(): pl.pallas_call(functools.partial(finish_kernel, n), grid=(rows // B,), in...  8.97 us
    pallas_call x1, Pallas kernels, back_first(): pl.pallas_call(functools.partial(back_kernel, n), grid=(count,), in_specs...  8.69 us
    all_to_all x1, waiting for transfers between devices, on_device(): lax.all_to_all(jnp.concatenate([right_flat, left_flat, small], axis=1), '...  8.57 us
    pallas_call x1, Pallas kernels, left_gradient(): pl.pallas_call(functools.partial(left_kernel, n, group), grid=(width // s...  6.93 us
    all_to_all x1, starting transfers between devices, on_device(): lax.all_to_all(jnp.concatenate([right_flat, left_flat, small], axis=1), '...  6.67 us
  transfers between devices with their start and end apart: 68, of which 20 were waited for; matrix products, arithmetic and copies ran while one was open for 2% of the time, Pallas kernels for 20%

profile of v1, /device:TPU:0, one launch (start us, length us, event | category | flops | bytes accessed | tf_op | source)
XLA Modules:
  0.0 271.6 jit_solution(1797080307988278631)
XLA Ops:
  1.1 4.2 %squares.1.sa_ref = f32[8,2048]{1,0:T(8,128)} custom-call(bf16[2048,512]{1,0:T(8,128)(2,1)} %tok_ref.7), custom_call_target="tpu_custom_call" | custom-call | flops 8388608 | bytes 2097152 | tf_op jit(solution)/shard_map/squares/pallas_call | solution.py:140
  7.4 5.7 %gate_cotangent.1 = (bf16[4,512,512]{2,1,0:T(8,128)(2,1)}, bf16[4,32,512]{2,1,0:T(8,128)(2,1)}, bf16[4,32,512]{2,1,0:T(8,128)(2,1)}, bf16[4,32,512]{2,1,0:T(8,12...) custom-call(bf16[2048,512]{1,0:T(8,128)(2,1)} %tok_ref.7, ...), custom_call_target="tpu_custom_call" | custom-call | flops 20971520 | bytes 8388608 | tf_op jit(solution)/shard_map/gate_cotangent/pallas_call | solution.py:170
  38.9 10.2 %collective-permute-done.10.rest_8_ = bf16[4,32,512]{2,1,0:T(8,128)(2,1)S(1)} collective-permute-done((bf16[4,32,512]{2,1,0:T(8,128)(2,1)}, bf16[4,32,512]{2,1,0:T(8,128)(2,1)S(1)}, u32[]{:S(2)}, u32[]{:S(2)}) %collective-permute-start.10) | collective-permute-done | bytes 131104 | tf_op jit(solution)/shard_map/ppermute | solution.py:70
  49.2 6.0 %collective-permute-start.15 = (bf16[4,32,512]{2,1,0:T(8,128)(2,1)}, bf16[4,32,512]{2,1,0:T(8,128)(2,1)S(1)}, u32[]{:S(2)}, u32[]{:S(2)}) collective-permute-start(bf16[4,32,512]{2,1,0:T(8,128)(2,1)} %get-tuple-element.171), channel_id=1, source_target_pairs={{0,26},{2,24},{4,30},{6,28},{8,2},{10,0},{12,6},{14,4},{16,10},{18... | collective-permute-start | bytes 393224 | tf_op jit(solution)/shard_map/ppermute | solution.py:70
  56.0 5.8 %first_factor.1 = (f32[4,512,512]{2,1,0:T(8,128)}, bf16[4,32,512]{2,1,0:T(8,128)(2,1)}, bf16[4,32,512]{2,1,0:T(8,128)(2,1)}, bf16[4,32,512]{2,1,0:T(8,128)(2,1)}...) custom-call(bf16[4,512,512]{2,1,0:T(8,128)(2,1)} %get-tuple-element., ...), custom_call_target="tpu_custom_call" | custom-call | flops 1073741824 | bytes 8388608 | tf_op jit(solution)/shard_map/first_factor/pallas_call | solution.py:203
  67.2 8.7 %collective-permute-start.19 = (bf16[4,32,512]{2,1,0:T(8,128)(2,1)}, bf16[4,32,512]{2,1,0:T(8,128)(2,1)S(1)}, u32[]{:S(2)}, u32[]{:S(2)}) collective-permute-start(bf16[4,32,512]{2,1,0:T(8,128)(2,1)} %get-tuple-element.175), channel_id=1, source_target_pairs={{0,8},{2,10},{4,12},{6,14},{8,16},{10,18},{12,20},{14,22},{16,24},... | collective-permute-start | bytes 393224 | tf_op jit(solution)/shard_map/ppermute | solution.py:70
  89.5 4.4 %widen.1 = (bf16[1024,1024]{1,0:T(8,128)(2,1)}, bf16[1024,1024]{1,0:T(8,128)(2,1)}) custom-call(bf16[64,64]{1,0:T(8,128)(2,1)} %pad_maximum_fusion.1.left_ref), custom_call_target="tpu_custom_call" | custom-call | flops 268435456 | bytes 4194304 | tf_op jit(solution)/shard_map/widen/pallas_call | solution.py:254
  102.2 6.1 %spread_grad.1 = (bf16[4,32,512]{2,1,0:T(8,128)(2,1)}, bf16[4,32,512]{2,1,0:T(8,128)(2,1)}, bf16[4,32,512]{2,1,0:T(8,128)(2,1)}, bf16[4,32,512]{2,1,0:T(8,128)(2...) custom-call(bf16[1024,1024]{1,0:T(8,128)(2,1)} %get-tuple-element.15, ...), custom_call_target="tpu_custom_call" | custom-call | flops 2147483648 | bytes 8388608 | tf_op jit(solution)/shard_map/spread_grad/pallas_call | solution.py:294
  116.3 5.1 %collective-permute-start.34 = (bf16[4,32,512]{2,1,0:T(8,128)(2,1)}, bf16[4,32,512]{2,1,0:T(8,128)(2,1)S(1)}, u32[]{:S(2)}, u32[]{:S(2)}) collective-permute-start(bf16[4,32,512]{2,1,0:T(8,128)(2,1)} %get-tuple-element.216), channel_id=1, source_target_pairs={{0,8},{2,10},{4,12},{6,14},{8,16},{10,18},{12,20},{14,22},{16,24},... | collective-permute-start | bytes 393224 | tf_op jit(solution)/shard_map/ppermute | solution.py:70
  121.4 8.4 %collective-permute-start.35 = (bf16[4,32,512]{2,1,0:T(8,128)(2,1)}, bf16[4,32,512]{2,1,0:T(8,128)(2,1)S(1)}, u32[]{:S(2)}, u32[]{:S(2)}) collective-permute-start(bf16[4,32,512]{2,1,0:T(8,128)(2,1)} %get-tuple-element.217), channel_id=1, source_target_pairs={{0,24},{2,26},{4,28},{6,30},{8,0},{10,2},{12,4},{14,6},{16,8},{18,... | collective-permute-start | bytes 393224 | tf_op jit(solution)/shard_map/ppermute | solution.py:70
  136.6 4.3 %collective-permute-start.41 = (bf16[4,32,512]{2,1,0:T(8,128)(2,1)}, bf16[4,32,512]{2,1,0:T(8,128)(2,1)S(1)}, u32[]{:S(2)}, u32[]{:S(2)}) collective-permute-start(bf16[4,32,512]{2,1,0:T(8,128)(2,1)} %get-tuple-element.225), channel_id=1, source_target_pairs={{0,6},{2,4},{4,2},{6,0},{8,14},{10,12},{12,10},{14,8},{16,22},{18,... | collective-permute-start | bytes 393224 | tf_op jit(solution)/shard_map/ppermute | solution.py:70
  144.2 6.5 %collective-permute-start.44 = (bf16[4,32,512]{2,1,0:T(8,128)(2,1)}, bf16[4,32,512]{2,1,0:T(8,128)(2,1)S(1)}, u32[]{:S(2)}, u32[]{:S(2)}) collective-permute-start(bf16[4,32,512]{2,1,0:T(8,128)(2,1)} %get-tuple-element.232), channel_id=1, source_target_pairs={{0,20},{2,22},{4,16},{6,18},{8,28},{10,30},{12,24},{14,26},{16,4},... | collective-permute-start | bytes 393224 | tf_op jit(solution)/shard_map/ppermute | solution.py:70
  152.0 6.1 %second_mix.1 = (bf16[4,32,512]{2,1,0:T(8,128)(2,1)}, bf16[4,32,512]{2,1,0:T(8,128)(2,1)}, bf16[4,32,512]{2,1,0:T(8,128)(2,1)}, bf16[4,32,512]{2,1,0:T(8,128)(2,...) custom-call(bf16[1024,1024]{1,0:T(8,128)(2,1)} %get-tuple-element.23, ...), custom_call_target="tpu_custom_call" | custom-call | flops 2147483648 | bytes 8388608 | tf_op jit(solution)/shard_map/second_mix/pallas_call | solution.py:294
  164.8 5.7 %collective-permute-start.49 = (bf16[4,32,512]{2,1,0:T(8,128)(2,1)}, bf16[4,32,512]{2,1,0:T(8,128)(2,1)S(1)}, u32[]{:S(2)}, u32[]{:S(2)}) collective-permute-start(bf16[4,32,512]{2,1,0:T(8,128)(2,1)} %get-tuple-element.256), channel_id=1, source_target_pairs={{0,8},{2,10},{4,12},{6,14},{8,16},{10,18},{12,20},{14,22},{16,24},... | collective-permute-start | bytes 393224 | tf_op jit(solution)/shard_map/ppermute | solution.py:70
  170.5 4.8 %collective-permute-start.50 = (bf16[4,32,512]{2,1,0:T(8,128)(2,1)}, bf16[4,32,512]{2,1,0:T(8,128)(2,1)S(1)}, u32[]{:S(2)}, u32[]{:S(2)}) collective-permute-start(bf16[4,32,512]{2,1,0:T(8,128)(2,1)} %get-tuple-element.257), channel_id=1, source_target_pairs={{0,24},{2,26},{4,28},{6,30},{8,0},{10,2},{12,4},{14,6},{16,8},{18,... | collective-permute-start | bytes 393224 | tf_op jit(solution)/shard_map/ppermute | solution.py:70
  179.4 4.7 %collective-permute-start.54 = (bf16[4,32,512]{2,1,0:T(8,128)(2,1)}, bf16[4,32,512]{2,1,0:T(8,128)(2,1)S(1)}, u32[]{:S(2)}, u32[]{:S(2)}) collective-permute-start(bf16[4,32,512]{2,1,0:T(8,128)(2,1)} %get-tuple-element.261), channel_id=1, source_target_pairs={{0,26},{2,24},{4,30},{6,28},{8,2},{10,0},{12,6},{14,4},{16,10},{18... | collective-permute-start | bytes 393224 | tf_op jit(solution)/shard_map/ppermute | solution.py:70
  189.3 8.7 %back_first.1 = (f32[4,8,512]{2,1,0:T(8,128)}, f32[512,512]{1,0:T(8,128)}, f32[4,512,512]{2,1,0:T(8,128)}) custom-call(f32[4,512,512]{2,1,0:T(8,128)} %get-tuple-element.156.first_ref, bf16[4,512,512]{2,1,0:T(8,128)(2,1)} %get-tuple-element.155.nb_ref, bf16[512,512]{1,0:T(8,128)(2,1)} %pad_maximum_fusion.right_ref, f32[4,512]{1,0:T(4,128)} %tw_ref.3, ...), custom_call_target="tpu_custom_call" | custom-call | flops 2147483648 | bytes 12582912 | tf_op jit(solution)/shard_map/back_first/pallas_call | solution.py:390
  199.5 6.9 %left_gradient.1 = f32[64,64]{1,0:T(8,128)} custom-call(bf16[4,32,512]{2,1,0:T(8,128)(2,1)} %get-tuple-element.182.rest_0_, bf16[4,32,512]{2,1,0:T(8,128)(2,1)} %copy-done.37, bf16[4,32,512]{2,1,0:T(8,128)(2,1)} %copy-done.38, bf16[4,32,512]{2,1,0:T(8,128)(2,1)} %copy-done.39, bf16[4,32,512]{2,1,0:T(8,128)(2,1)} %copy-done.40, ...), custom_call_target="tpu_custom_call" | custom-call | flops 2147483648 | bytes 8388608 | tf_op jit(solution)/shard_map/left_gradient/pallas_call | solution.py:352
  216.3 5.3 %collective-permute-start.60 = (bf16[4,32,512]{2,1,0:T(8,128)(2,1)S(1)}, bf16[4,32,512]{2,1,0:T(8,128)(2,1)S(1)}, u32[]{:S(2)}, u32[]{:S(2)}) collective-permute-start(bf16[4,32,512]{2,1,0:T(8,128)(2,1)S(1)} %copy-done.69), channel_id=1, source_target_pairs={{0,22},{2,20},{4,18},{6,16},{8,30},{10,28},{12,26},{14,24},{16,6},... | collective-permute-start | bytes 393224 | tf_op jit(solution)/shard_map/ppermute | solution.py:70
  224.4 4.1 %collective-permute-done.59.rest_10_ = bf16[4,32,512]{2,1,0:T(8,128)(2,1)S(1)} collective-permute-done((bf16[4,32,512]{2,1,0:T(8,128)(2,1)S(1)}, bf16[4,32,512]{2,1,0:T(8,128)(2,1)S(1)}, u32[]{:S(2)}, u32[]{:S(2)}) %collective-permute-start.59) | collective-permute-done | bytes 131104 | tf_op jit(solution)/shard_map/ppermute | solution.py:70
  234.6 9.0 %finish.1 = (bf16[2048,512]{1,0:T(8,128)(2,1)}, f32[2048,512]{1,0:T(8,128)}, f32[8,2048]{1,0:T(8,128)}, f32[8,512]{1,0:T(8,128)}) custom-call(bf16[2048,512]{1,0:T(8,128)(2,1)} %tok_ref.7, bf16[2048,512]{1,0:T(8,128)(2,1)} %cot_ref.3, f32[8,2048]{1,0:T(8,128)} %squares.1.sa_ref, f32[8,2048]{1,0:T(8,128)} %copy-done.1, f32[1,512]{1,0:T(1,128)} %bitcast.8, ...), custom_call_target="tpu_custom_call" | custom-call | flops 41943040 | bytes 16777216 | tf_op jit(solution)/shard_map/finish/pallas_call | solution.py:436
  245.9 6.7 %all-to-all-start = ((f32[16,1,9856]{2,1,0:T(1,128)}), f32[16,1,9856]{2,1,0:T(1,128)S(1)}, u32[]{:S(2)}, u32[]{:S(2)}) async-start(f32[16,1,9856]{2,1,0:T(1,128)} %all_to_all.6), calls=%async_computation | async-start | bytes 1261568 | tf_op jit(solution)/shard_map/all_to_all | solution.py:510
  255.2 5.5 %token_gradient.1 = bf16[2048,512]{1,0:T(8,128)(2,1)} custom-call(bf16[2048,512]{1,0:T(8,128)(2,1)} %tok_ref.7, f32[2048,512]{1,0:T(8,128)} %get-tuple-element.297.scaled_ref, f32[8,2048]{1,0:T(8,128)} %squares.1.sa_ref, f32[8,2048]{1,0:T(8,128)} %copy-done.1, f32[8,2048]{1,0:T(8,128)} %get-tuple-element.298.ia_ref, f32[8,2048]{1,0:T(8,128)} %copy-done.34), custom_call_target="tpu_custom_call" | custom-call | flops 5242880 | bytes 8388608 | tf_op jit(solution)/shard_map/token_gradient/pallas_call | solution.py:462
  260.7 8.6 %all-to-all-done = f32[16,1,9856]{2,1,0:T(1,128)S(1)} async-done(((f32[16,1,9856]{2,1,0:T(1,128)}), f32[16,1,9856]{2,1,0:T(1,128)S(1)}, u32[]{:S(2)}, u32[]{:S(2)}) %all-to-all-start) | async-done | bytes 630816 | tf_op jit(solution)/shard_map/all_to_all | solution.py:510
  (305 shorter events, 118.7 us)
Async XLA Ops:
  0.6 26.9 %collective-permute-start.1 = (bf16[256,512]{1,0:T(8,128)(2,1)}, bf16[256,512]{1,0:T(8,128)(2,1)S(1)}, u32[]{:S(2)}, u32[]{:S(2)}) collective-permute-start(bf16[256,512]{1,0:T(8,128)(2,1)} %param.13), channel_id=1, source_target_pairs={{0,1},{1,0},{2,3},{3,2},{4,5},{5,4},{6,7},{7,6},{8,9},{9,8},{10,11... | collective-permute-start | bytes 786440 | tf_op jit(solution)/shard_map/ppermute | solution.py:94
  27.5 21.7 %collective-permute-start.10 = (bf16[4,32,512]{2,1,0:T(8,128)(2,1)}, bf16[4,32,512]{2,1,0:T(8,128)(2,1)S(1)}, u32[]{:S(2)}, u32[]{:S(2)}) collective-permute-start(bf16[4,32,512]{2,1,0:T(8,128)(2,1)} %get-tuple-element.166), channel_id=1, source_target_pairs={{0,16},{2,18},{4,20},{6,22},{8,24},{10,26},{12,28},{14,30},{16,0},... | collective-permute-start | bytes 393224 | tf_op jit(solution)/shard_map/ppermute | solution.py:70
  29.6 32.3 %collective-permute-start.11 = (bf16[4,32,512]{2,1,0:T(8,128)(2,1)}, bf16[4,32,512]{2,1,0:T(8,128)(2,1)S(1)}, u32[]{:S(2)}, u32[]{:S(2)}) collective-permute-start(bf16[4,32,512]{2,1,0:T(8,128)(2,1)} %get-tuple-element.167), channel_id=1, source_target_pairs={{0,18},{2,16},{4,22},{6,20},{8,26},{10,24},{12,30},{14,28},{16,2},... | collective-permute-start | bytes 393224 | tf_op jit(solution)/shard_map/ppermute | solution.py:70
  32.3 29.8 %collective-permute-start.12 = (bf16[4,32,512]{2,1,0:T(8,128)(2,1)}, bf16[4,32,512]{2,1,0:T(8,128)(2,1)S(1)}, u32[]{:S(2)}, u32[]{:S(2)}) collective-permute-start(bf16[4,32,512]{2,1,0:T(8,128)(2,1)} %get-tuple-element.168), channel_id=1, source_target_pairs={{0,20},{2,22},{4,16},{6,18},{8,28},{10,30},{12,24},{14,26},{16,4},... | collective-permute-start | bytes 393224 | tf_op jit(solution)/shard_map/ppermute | solution.py:70
  34.5 30.0 %collective-permute-start.13 = (bf16[4,32,512]{2,1,0:T(8,128)(2,1)}, bf16[4,32,512]{2,1,0:T(8,128)(2,1)S(1)}, u32[]{:S(2)}, u32[]{:S(2)}) collective-permute-start(bf16[4,32,512]{2,1,0:T(8,128)(2,1)} %get-tuple-element.169), channel_id=1, source_target_pairs={{0,22},{2,20},{4,18},{6,16},{8,30},{10,28},{12,26},{14,24},{16,6},... | collective-permute-start | bytes 393224 | tf_op jit(solution)/shard_map/ppermute | solution.py:70
  37.7 29.4 %collective-permute-start.14 = (bf16[4,32,512]{2,1,0:T(8,128)(2,1)}, bf16[4,32,512]{2,1,0:T(8,128)(2,1)S(1)}, u32[]{:S(2)}, u32[]{:S(2)}) collective-permute-start(bf16[4,32,512]{2,1,0:T(8,128)(2,1)} %get-tuple-element.170), channel_id=1, source_target_pairs={{0,24},{2,26},{4,28},{6,30},{8,0},{10,2},{12,4},{14,6},{16,8},{18,... | collective-permute-start | bytes 393224 | tf_op jit(solution)/shard_map/ppermute | solution.py:70
  49.2 26.7 %collective-permute-start.15 = (bf16[4,32,512]{2,1,0:T(8,128)(2,1)}, bf16[4,32,512]{2,1,0:T(8,128)(2,1)S(1)}, u32[]{:S(2)}, u32[]{:S(2)}) collective-permute-start(bf16[4,32,512]{2,1,0:T(8,128)(2,1)} %get-tuple-element.171), channel_id=1, source_target_pairs={{0,26},{2,24},{4,30},{6,28},{8,2},{10,0},{12,6},{14,4},{16,10},{18... | collective-permute-start | bytes 393224 | tf_op jit(solution)/shard_map/ppermute | solution.py:70
  75.9 18.0 %collective-permute-start.21 = (bf16[4,32,512]{2,1,0:T(8,128)(2,1)}, bf16[4,32,512]{2,1,0:T(8,128)(2,1)S(1)}, u32[]{:S(2)}, u32[]{:S(2)}) collective-permute-start(bf16[4,32,512]{2,1,0:T(8,128)(2,1)} %get-tuple-element.177), channel_id=1, source_target_pairs={{0,2},{2,0},{4,6},{6,4},{8,10},{10,8},{12,14},{14,12},{16,18},{18,... | collective-permute-start | bytes 393224 | tf_op jit(solution)/shard_map/ppermute | solution.py:70
  76.0 19.2 %collective-permute-start.22 = (bf16[4,32,512]{2,1,0:T(8,128)(2,1)}, bf16[4,32,512]{2,1,0:T(8,128)(2,1)S(1)}, u32[]{:S(2)}, u32[]{:S(2)}) collective-permute-start(bf16[4,32,512]{2,1,0:T(8,128)(2,1)} %get-tuple-element.178), channel_id=1, source_target_pairs={{0,18},{2,16},{4,22},{6,20},{8,26},{10,24},{12,30},{14,28},{16,2},... | collective-permute-start | bytes 393224 | tf_op jit(solution)/shard_map/ppermute | solution.py:70
  95.2 18.4 %collective-permute-start.28 = (bf16[4,32,512]{2,1,0:T(8,128)(2,1)}, bf16[4,32,512]{2,1,0:T(8,128)(2,1)S(1)}, u32[]{:S(2)}, u32[]{:S(2)}) collective-permute-start(bf16[4,32,512]{2,1,0:T(8,128)(2,1)} %get-tuple-element.206), channel_id=1, source_target_pairs={{0,14},{2,12},{4,10},{6,8},{8,22},{10,20},{12,18},{14,16},{16,30},... | collective-permute-start | bytes 393224 | tf_op jit(solution)/shard_map/ppermute | solution.py:70
  97.8 18.5 %collective-permute-start.29 = (bf16[4,32,512]{2,1,0:T(8,128)(2,1)}, bf16[4,32,512]{2,1,0:T(8,128)(2,1)S(1)}, u32[]{:S(2)}, u32[]{:S(2)}) collective-permute-start(bf16[4,32,512]{2,1,0:T(8,128)(2,1)} %get-tuple-element.209), channel_id=1, source_target_pairs={{0,20},{2,22},{4,16},{6,18},{8,28},{10,30},{12,24},{14,26},{16,4},... | collective-permute-start | bytes 393224 | tf_op jit(solution)/shard_map/ppermute | solution.py:70
  101.5 19.8 %collective-permute-start.30 = (bf16[4,32,512]{2,1,0:T(8,128)(2,1)}, bf16[4,32,512]{2,1,0:T(8,128)(2,1)S(1)}, u32[]{:S(2)}, u32[]{:S(2)}) collective-permute-start(bf16[4,32,512]{2,1,0:T(8,128)(2,1)} %get-tuple-element.210), channel_id=1, source_target_pairs={{0,22},{2,20},{4,18},{6,16},{8,30},{10,28},{12,26},{14,24},{16,6},... | collective-permute-start | bytes 393224 | tf_op jit(solution)/shard_map/ppermute | solution.py:70
  108.3 21.4 %collective-permute-start.31 = (bf16[4,32,512]{2,1,0:T(8,128)(2,1)S(1)}, bf16[4,32,512]{2,1,0:T(8,128)(2,1)S(1)}, u32[]{:S(2)}, u32[]{:S(2)}) collective-permute-start(bf16[4,32,512]{2,1,0:T(8,128)(2,1)S(1)} %copy-done.75), channel_id=1, source_target_pairs={{0,28},{2,30},{4,24},{6,26},{8,4},{10,6},{12,0},{14,2},{16,12},{18... | collective-permute-start | bytes 393224 | tf_op jit(solution)/shard_map/ppermute | solution.py:70
  111.0 19.9 %collective-permute-start.32 = (bf16[4,32,512]{2,1,0:T(8,128)(2,1)S(1)}, bf16[4,32,512]{2,1,0:T(8,128)(2,1)S(1)}, u32[]{:S(2)}, u32[]{:S(2)}) collective-permute-start(bf16[4,32,512]{2,1,0:T(8,128)(2,1)S(1)} %copy-done.73), channel_id=1, source_target_pairs={{0,30},{2,28},{4,26},{6,24},{8,6},{10,4},{12,2},{14,0},{16,14},{18... | collective-permute-start | bytes 393224 | tf_op jit(solution)/shard_map/ppermute | solution.py:70
  113.5 17.4 %collective-permute-start.33 = (bf16[4,32,512]{2,1,0:T(8,128)(2,1)}, bf16[4,32,512]{2,1,0:T(8,128)(2,1)S(1)}, u32[]{:S(2)}, u32[]{:S(2)}) collective-permute-start(bf16[4,32,512]{2,1,0:T(8,128)(2,1)} %get-tuple-element.215), channel_id=1, source_target_pairs={{0,16},{2,18},{4,20},{6,22},{8,24},{10,26},{12,28},{14,30},{16,0},... | collective-permute-start | bytes 393224 | tf_op jit(solution)/shard_map/ppermute | solution.py:70
  136.6 21.6 %collective-permute-start.41 = (bf16[4,32,512]{2,1,0:T(8,128)(2,1)}, bf16[4,32,512]{2,1,0:T(8,128)(2,1)S(1)}, u32[]{:S(2)}, u32[]{:S(2)}) collective-permute-start(bf16[4,32,512]{2,1,0:T(8,128)(2,1)} %get-tuple-element.225), channel_id=1, source_target_pairs={{0,6},{2,4},{4,2},{6,0},{8,14},{10,12},{12,10},{14,8},{16,22},{18,... | collective-permute-start | bytes 393224 | tf_op jit(solution)/shard_map/ppermute | solution.py:70
  140.9 19.3 %collective-permute-start.42 = (bf16[4,32,512]{2,1,0:T(8,128)(2,1)}, bf16[4,32,512]{2,1,0:T(8,128)(2,1)S(1)}, u32[]{:S(2)}, u32[]{:S(2)}) collective-permute-start(bf16[4,32,512]{2,1,0:T(8,128)(2,1)} %get-tuple-element.228), channel_id=1, source_target_pairs={{0,12},{2,14},{4,8},{6,10},{8,20},{10,22},{12,16},{14,18},{16,28},... | collective-permute-start | bytes 393224 | tf_op jit(solution)/shard_map/ppermute | solution.py:70
  140.9 20.6 %collective-permute-start.43 = (bf16[4,32,512]{2,1,0:T(8,128)(2,1)}, bf16[4,32,512]{2,1,0:T(8,128)(2,1)S(1)}, u32[]{:S(2)}, u32[]{:S(2)}) collective-permute-start(bf16[4,32,512]{2,1,0:T(8,128)(2,1)} %get-tuple-element.229), channel_id=1, source_target_pairs={{0,14},{2,12},{4,10},{6,8},{8,22},{10,20},{12,18},{14,16},{16,30},... | collective-permute-start | bytes 393224 | tf_op jit(solution)/shard_map/ppermute | solution.py:70
  144.2 20.6 %collective-permute-start.44 = (bf16[4,32,512]{2,1,0:T(8,128)(2,1)}, bf16[4,32,512]{2,1,0:T(8,128)(2,1)S(1)}, u32[]{:S(2)}, u32[]{:S(2)}) collective-permute-start(bf16[4,32,512]{2,1,0:T(8,128)(2,1)} %get-tuple-element.232), channel_id=1, source_target_pairs={{0,20},{2,22},{4,16},{6,18},{8,28},{10,30},{12,24},{14,26},{16,4},... | collective-permute-start | bytes 393224 | tf_op jit(solution)/shard_map/ppermute | solution.py:70
  150.8 19.8 %collective-permute-start.45 = (bf16[4,32,512]{2,1,0:T(8,128)(2,1)}, bf16[4,32,512]{2,1,0:T(8,128)(2,1)S(1)}, u32[]{:S(2)}, u32[]{:S(2)}) collective-permute-start(bf16[4,32,512]{2,1,0:T(8,128)(2,1)} %get-tuple-element.233), channel_id=1, source_target_pairs={{0,22},{2,20},{4,18},{6,16},{8,30},{10,28},{12,26},{14,24},{16,6},... | collective-permute-start | bytes 393224 | tf_op jit(solution)/shard_map/ppermute | solution.py:70
  160.2 17.2 %collective-permute-start.47 = (bf16[4,32,512]{2,1,0:T(8,128)(2,1)S(1)}, bf16[4,32,512]{2,1,0:T(8,128)(2,1)S(1)}, u32[]{:S(2)}, u32[]{:S(2)}) collective-permute-start(bf16[4,32,512]{2,1,0:T(8,128)(2,1)S(1)} %copy-done.76), channel_id=1, source_target_pairs={{0,30},{2,28},{4,26},{6,24},{8,6},{10,4},{12,2},{14,0},{16,14},{18... | collective-permute-start | bytes 393224 | tf_op jit(solution)/shard_map/ppermute | solution.py:70
  161.5 17.9 %collective-permute-start.48 = (bf16[4,32,512]{2,1,0:T(8,128)(2,1)}, bf16[4,32,512]{2,1,0:T(8,128)(2,1)S(1)}, u32[]{:S(2)}, u32[]{:S(2)}) collective-permute-start(bf16[4,32,512]{2,1,0:T(8,128)(2,1)} %get-tuple-element.255), channel_id=1, source_target_pairs={{0,16},{2,18},{4,20},{6,22},{8,24},{10,26},{12,28},{14,30},{16,0},... | collective-permute-start | bytes 393224 | tf_op jit(solution)/shard_map/ppermute | solution.py:70
  199.4 44.9 %collective-permute-start.64 = (f32[512,256]{1,0:T(8,128)S(1)}, f32[512,256]{1,0:T(8,128)S(1)}, u32[]{:S(2)}, u32[]{:S(2)}) collective-permute-start(f32[512,256]{1,0:T(8,128)S(1)} %slice_select_fusion), channel_id=1, source_target_pairs={{0,1},{1,0},{2,3},{3,2},{4,5},{5,4},{6,7},{7,6},{8,9},{9,8},{10,11... | collective-permute-start | bytes 1572872 | tf_op jit(solution)/shard_map/ppermute | solution.py:108
  245.9 23.4 %all-to-all-start = ((f32[16,1,9856]{2,1,0:T(1,128)}), f32[16,1,9856]{2,1,0:T(1,128)S(1)}, u32[]{:S(2)}, u32[]{:S(2)}) async-start(f32[16,1,9856]{2,1,0:T(1,128)} %all_to_all.6), calls=%async_computation | async-start | bytes 1261568 | tf_op jit(solution)/shard_map/all_to_all | solution.py:510
  (124 other events, 1990.4 us)

commit v2 on v1

v2 whole, which is shorter than its diff:
```python
import functools

import jax
import jax.numpy as jnp
from jax import lax
from jax.experimental import pallas as pl
from jax.experimental.pallas import tpu as pltpu
from jax.sharding import PartitionSpec as P

D = 1024
B = 512
EPS = 1e-05
LAG = 8
LAST = 10
SHARE = 1000

F32 = jnp.float32
BF16 = jnp.bfloat16


def sds(shape, dtype):
    return jax.ShapeDtypeStruct(shape, dtype)


def cost(flops, nbytes):
    return pl.CostEstimate(flops=int(flops) // SHARE, bytes_accessed=int(nbytes) // SHARE, transcendentals=0)


def params(mib=20):
    return pltpu.CompilerParams(vmem_limit_bytes=mib * 1024 * 1024)


def whole(shape):
    zeros = (0,) * len(shape)
    return pl.BlockSpec(shape, lambda *_: zeros)


HBM = pl.BlockSpec(memory_space=pltpu.HBM)
VMEM = pl.BlockSpec(memory_space=pltpu.VMEM)


def partners(n, sign):
    me = lax.axis_index("seq")
    hi, lo = me // 4, me % 4
    high = n // 4
    lo_of = [lo, lo + 1 - 2 * (lo % 2), (lo + 2) % 4, 3 - lo]
    return [
        ((hi + (sign * (k // 4)) % high) % high) * 4 + lo_of[k % 4]
        for k in range(n)
    ]


def pairs(n, k):
    high = n // 4
    return [
        (i, ((i // 4 + k // 4) % high) * 4 + ((i % 4) ^ (k % 4)))
        for i in range(n)
    ]


def send_order(n):
    high = n // 4
    far_first = sorted(range(1, high), key=lambda d: (abs(d - high / 2), d))
    order = []
    for dl in range(4):
        order += [4 * dh + dl for dh in far_first]
        if dl < 3:
            order.append(dl + 1)
    return order


def exchange(blocks):
    n = len(blocks)
    out = list(blocks)
    for k in send_order(n):
        out[k] = lax.ppermute(blocks[k], "seq", pairs(n, k))
    return out


def in_hbm(blocks):
    return [pltpu.with_memory_space_constraint(x, pltpu.HBM) for x in blocks]


def after_part(values, started, count=LAG):
    keys = send_order(len(started))[:count]
    values, held = lax.optimization_barrier((values, [started[k] for k in keys]))
    started = list(started)
    for k, v in zip(keys, held):
        started[k] = v
    return values, started


def chan_terms(x):
    nc = lax.axis_size("chan")
    if nc == 2:
        return x, lax.ppermute(x, "chan", [(0, 1), (1, 0)])
    return lax.psum(x, "chan"), jnp.zeros_like(x)


def chan_gather(x):
    nc = lax.axis_size("chan")
    if nc != 2:
        return lax.all_gather(x, "chan", axis=0, tiled=True)
    other = lax.ppermute(x, "chan", [(0, 1), (1, 0)])
    first = lax.axis_index("chan") == 0
    return jnp.concatenate(
        [jnp.where(first, x, other), jnp.where(first, other, x)], axis=0
    )


def chan_halves(x):
    half = x.shape[1] // 2
    first = lax.axis_index("chan") == 0
    low, high = x[:, :half], x[:, half:]
    return jnp.where(first, low, high), jnp.where(first, high, low)


def chan_joined(keep, give):
    if lax.axis_size("chan") == 2:
        return keep, lax.ppermute(give, "chan", [(0, 1), (1, 0)])
    out = lax.psum_scatter(give, "chan", scatter_dimension=1, tiled=True)
    return out, jnp.zeros_like(out)


def flipped(x, bit):
    n = lax.axis_size("seq")
    return lax.ppermute(x, "seq", [(i, i ^ bit) for i in range(n)])


def bits(n):
    return [1 << i for i in range(n.bit_length() - 1)]


def write_split(bit, blocks, keep_ref, message):
    mine = (lax.axis_index("seq") // bit) % 2
    size = keep_ref.shape[1]
    for q in range(keep_ref.shape[0]):
        keep_ref[q] = blocks(2 * q + mine)
        message[q * size : (q + 1) * size, :] = blocks(2 * q + 1 - mine)


def join_kernel(bit, ra_ref, rb_ref, la_ref, lb_ref, sums_ref, keep_ref, message, held):
    n, size, width = held.shape
    rows = size - 8
    count = la_ref.shape[0] // n
    thin = la_ref.shape[1]
    held[:, :rows, :] = (ra_ref[...] + rb_ref[...]).reshape(n, rows, width)
    held[:, rows:, :] = jnp.zeros((n, 8, width), F32)
    left = la_ref[...] + lb_ref[...]
    for q in range(n):
        held[q, rows : rows + count, :thin] = left[q * count : (q + 1) * count, :]
    write_split(bit, lambda q: held[q], keep_ref, message)
    message[n // 2 * size :, :] = sums_ref[...]


def join(bit, n, ra, rb, la, lb, sums):
    rows, width = ra.shape
    size = rows // n + 8
    return pl.pallas_call(
        functools.partial(join_kernel, bit),
        in_specs=[VMEM] * 5,
        out_specs=[VMEM] * 2,
        out_shape=[
            sds((n // 2, size, width), F32),
            sds((n // 2 * size + sums.shape[0], width), F32),
        ],
        scratch_shapes=[pltpu.VMEM((n, size, width), F32)],
        compiler_params=params(8),
        cost_estimate=cost(rows * width, 8 * rows * width),
        name="join",
    )(ra, rb, la, lb, sums)


def fold_kernel(bit, keep_ref, small_ref, came, next_keep, next_small, message):
    parts, size, _ = keep_ref.shape
    write_split(
        bit,
        lambda q: keep_ref[q] + came[pl.ds(pl.multiple_of(q * size, 8), size), :],
        next_keep,
        message,
    )
    small = small_ref[...] + came[parts * size :, :]
    next_small[...] = small
    message[parts // 2 * size :, :] = small


def fold(bit, keep, small, came):
    parts, size, width = keep.shape
    tail = small.shape[0]
    shapes = [
        sds((parts // 2, size, width), F32),
        sds((tail, width), F32),
        sds((parts // 2 * size + tail, width), F32),
    ]
    return pl.pallas_call(
        functools.partial(fold_kernel, bit),
        in_specs=[VMEM] * 3,
        out_specs=[VMEM] * 3,
        out_shape=shapes,
        compiler_params=params(8),
        cost_estimate=cost(parts * size * width, 8 * parts * size * width),
        name="fold",
    )(keep, small, came)


def close_kernel(keep_ref, small_ref, came, ta_ref, tb_ref, right_ref, left_ref, twiddle_ref, *vectors):
    _, size, width = keep_ref.shape
    rows, count, thin = size - 8, *left_ref.shape
    right_ref[...] = keep_ref[0, :rows, :] + came[:rows, :]
    left_ref[...] = keep_ref[0, rows : rows + count, :thin] + came[rows : rows + count, :thin]
    small = small_ref[...] + came[size:, :]
    lines = vectors[0].shape[1] // width
    for i, out_ref in enumerate(vectors):
        for j in range(lines):
            at = i * lines + j
            out_ref[:, j * width : (j + 1) * width] = small[at : at + 1, :]
    for a in range(twiddle_ref.shape[0]):
        twiddle_ref[a : a + 1, :] = ta_ref[a, :1, :] + tb_ref[a, :1, :]


def close(keep, small, came, ta, tb, count, thin, chans):
    _, size, width = keep.shape
    return pl.pallas_call(
        close_kernel,
        in_specs=[VMEM] * 5,
        out_shape=[
            sds((size - 8, width), F32),
            sds((count, thin), F32),
            sds((ta.shape[0], ta.shape[2]), F32),
        ]
        + [sds((1, chans), F32)] * 3,
        compiler_params=params(8),
        cost_estimate=cost(size * width, 8 * size * width),
        name="close",
    )(keep, small, came, ta, tb)


def row_sums(x):
    high = x.astype(BF16)
    low = (x - high.astype(F32)).astype(BF16)
    ones = jnp.ones((x.shape[1], 128), BF16)
    sums = jnp.dot(high, ones, preferred_element_type=F32) + jnp.dot(
        low, ones, preferred_element_type=F32
    )
    return sums.T[:8, :]


def column(rows):
    return rows.T[:, :1]


def scale_of(sa_ref, sb_ref):
    return column(lax.rsqrt((sa_ref[...] + sb_ref[...]) / D + EPS))


def sigmoid(x):
    return 0.5 * jnp.tanh(0.5 * x) + 0.5


def squares_kernel(tok_ref, out_ref):
    x = tok_ref[...].astype(F32)
    out_ref[...] = row_sums(x * x)


def squares(tokens):
    rows, width = tokens.shape
    return pl.pallas_call(
        squares_kernel,
        grid=(rows // B,),
        in_specs=[pl.BlockSpec((B, width), lambda a: (a, 0))],
        out_specs=pl.BlockSpec((8, B), lambda a: (0, a)),
        out_shape=sds((8, rows), F32),
        compiler_params=params(),
        cost_estimate=cost(8 * rows * width, 2 * rows * width),
        name="squares",
    )(tokens)


def gate_kernel(n, tok_ref, cot_ref, sa_ref, sb_ref, gain_ref, slope_ref, bias_ref, *rest):
    nb_ref, outs, held = rest[0], rest[1 : 1 + n], rest[1 + n]
    size = B // n
    normed = tok_ref[...].astype(F32) * scale_of(sa_ref, sb_ref) * gain_ref[...]
    nb_ref[0] = normed.astype(BF16)
    gate = sigmoid(slope_ref[...] * normed + bias_ref[...])
    held[...] = (cot_ref[...].astype(F32) * gate).astype(BF16)
    for k, dest in enumerate(partners(n, 1)):
        outs[k][0] = held[pl.ds(pl.multiple_of(dest * size, size), size), :]


def gate_cotangent(n, tokens, cotangent, sa, sb, gain, slope, bias):
    rows, width = tokens.shape
    blocks = rows // B
    size = B // n
    tall = pl.BlockSpec((B, width), lambda a: (a, 0))
    row = pl.BlockSpec((8, B), lambda a: (0, a))
    vec = whole((1, width))
    result = pl.pallas_call(
        functools.partial(gate_kernel, n),
        grid=(blocks,),
        in_specs=[tall, tall, row, row, vec, vec, vec],
        out_specs=[pl.BlockSpec((1, B, width), lambda a: (a, 0, 0))]
        + [pl.BlockSpec((1, size, width), lambda a: (a, 0, 0))] * n,
        out_shape=[sds((blocks, B, width), BF16)] + [sds((blocks, size, width), BF16)] * n,
        scratch_shapes=[pltpu.VMEM((B, width), BF16)],
        compiler_params=params(),
        cost_estimate=cost(20 * rows * width, 8 * rows * width),
        name="gate_cotangent",
    )(tokens, cotangent, sa, sb, gain, slope, bias)
    return result[0], list(result[1:])


def twiddle_column(tw_ref, a):
    return column(jnp.broadcast_to(tw_ref[pl.ds(a, 1), :], (8, tw_ref.shape[1])))


def first_kernel(n, nb_ref, right_ref, tw_ref, *rest):
    first_ref, outs, held = rest[0], rest[1 : 1 + n], rest[1 + n]
    size = B // n
    first = jnp.dot(right_ref[...], nb_ref[0], preferred_element_type=F32)
    first_ref[0] = first
    held[...] = (first * twiddle_column(tw_ref, pl.program_id(0))).astype(BF16)
    for k, dest in enumerate(partners(n, 1)):
        outs[k][0] = held[pl.ds(pl.multiple_of(dest * size, size), size), :]


def first_factor(n, normed_b, right, twiddle):
    blocks, _, width = normed_b.shape
    size = B // n
    block = pl.BlockSpec((1, B, width), lambda a: (a, 0, 0))
    result = pl.pallas_call(
        functools.partial(first_kernel, n),
        grid=(blocks,),
        in_specs=[block, whole((B, B)), whole((blocks, B))],
        out_specs=[block] + [pl.BlockSpec((1, size, width), lambda a: (a, 0, 0))] * n,
        out_shape=[sds((blocks, B, width), F32)] + [sds((blocks, size, width), BF16)] * n,
        scratch_shapes=[pltpu.VMEM((B, width), BF16)],
        compiler_params=params(),
        cost_estimate=cost(2 * blocks * B * B * width, 8 * blocks * B * width),
        name="first_factor",
    )(normed_b, right, twiddle)
    return result[0], list(result[1:])


def group_of(n):
    return min(16, B // n)


def spread_matrix(rows, cols, group, offset, transposed):
    shape = (cols, rows) if transposed else (rows, cols)
    m = lax.broadcasted_iota(jnp.int32, shape, 1 if transposed else 0) + offset
    r = lax.broadcasted_iota(jnp.int32, shape, 0 if transposed else 1)
    inside = (m >= r * group) & (m < (r + 1) * group)
    return jnp.where(inside, 1.0, 0.0).astype(BF16)


def same_place(rows, cols, group, offset):
    m = lax.broadcasted_iota(jnp.int32, (rows, cols), 0) + offset
    q = lax.broadcasted_iota(jnp.int32, (rows, cols), 1)
    return lax.rem(m, group) == lax.rem(q, group)


def widen_kernel(group, left_ref, fore_ref, back_ref):
    step, total = fore_ref.shape
    outer = left_ref.shape[0]
    offset = pl.program_id(0) * step
    rows = spread_matrix(step, outer, group, offset, False)
    cols = spread_matrix(total, outer, group, 0, True)
    same = same_place(step, total, group, offset)
    left = left_ref[...]
    for source, out_ref in ((left, fore_ref), (left.astype(F32).T.astype(BF16), back_ref)):
        part = jnp.dot(rows, source, preferred_element_type=F32).astype(BF16)
        full = jnp.dot(part, cols, preferred_element_type=F32)
        out_ref[...] = jnp.where(same, full, 0.0).astype(BF16)


def widen(left, group):
    outer = left.shape[0]
    total = outer * group
    step = 256
    spec = pl.BlockSpec((step, total), lambda i: (i, 0))
    return pl.pallas_call(
        functools.partial(widen_kernel, group),
        grid=(total // step,),
        in_specs=[whole((outer, outer))],
        out_specs=[spec, spec],
        out_shape=[sds((total, total), BF16)] * 2,
        compiler_params=params(),
        cost_estimate=cost(4 * total * total * outer, 4 * total * total),
        name="widen",
    )(left)


def fetch(pairs_of_refs, sems):
    copies = [
        pltpu.make_async_copy(source, target, sems.at[i])
        for i, (source, target) in enumerate(pairs_of_refs)
    ]
    for copy in copies:
        copy.start()
    return copies


def group_copies(ins, held, group):
    n = len(ins)
    count, size, _ = ins[0].shape
    sources = partners(n, -1)
    return [
        (
            ins[k].at[:, pl.ds(g * group, group), :],
            held.at[g, pl.ds(sources[k] * count, count), :, :],
        )
        for g in range(size // group)
        for k in range(n)
    ]


def second_kernel(n, group, mat_ref, *rest):
    ins, outs, held, done, sems = rest[:n], rest[n : 2 * n], *rest[2 * n :]
    count, size, width = outs[0].shape
    groups = size // group
    dests = partners(n, 1)
    copies = fetch(group_copies(ins, held, group), sems)
    span = count * group
    step = min(256, width)
    for g in range(groups):
        for copy in copies[g * n : (g + 1) * n]:
            copy.wait()
        for c in range(width // step):
            part = slice(c * step, (c + 1) * step)
            flat = held[g, :, :, part].reshape(-1, step)
            done[g, :, part] = jnp.dot(
                mat_ref[...], flat, preferred_element_type=F32
            ).astype(BF16)
        for k in range(n):
            place = pl.ds(pl.multiple_of(dests[k] * span, span), span)
            outs[k][:, pl.ds(g * group, group), :] = done[g, place, :].reshape(count, group, width)


def second_factor(n, matrix, blocks, name):
    count, size, width = blocks[0].shape
    group = group_of(n)
    groups = size // group
    total = matrix.shape[0]
    return list(
        pl.pallas_call(
            functools.partial(second_kernel, n, group),
            in_specs=[VMEM] + [HBM] * n,
            out_shape=[sds((count, size, width), BF16)] * n,
            scratch_shapes=[
                pltpu.VMEM((groups, n * count, group, width), BF16),
                pltpu.VMEM((groups, total, width), BF16),
                pltpu.SemaphoreType.DMA((groups * n,)),
            ],
            compiler_params=params(),
            cost_estimate=cost(2 * total * total * width * groups, 8 * n * count * size * width),
            name=name,
        )(matrix, *in_hbm(blocks))
    )


def halves(rows, columns):
    nc = lax.axis_size("chan")
    if nc == 2:
        return [sds((rows, columns // 2), F32)] * 2
    return [sds((8, 128), F32), sds((rows, columns), F32)]


def store_halves(full, keep_ref, give_ref):
    if lax.axis_size("chan") == 2:
        keep_ref[...], give_ref[...] = chan_halves(full)
    else:
        keep_ref[...] = jnp.zeros_like(keep_ref)
        give_ref[...] = full


def left_kernel(n, group, *rest):
    cots, spreads, keep_ref, give_ref = rest[:n], rest[n : 2 * n], *rest[2 * n : 2 * n + 2]
    held_c, held_s, summed, sems = rest[2 * n + 2 :]
    groups, outer, _, width = held_c.shape
    dims = (((1,), (1,)), ((), ()))
    total = outer * group
    step = min(256, total)
    copies = fetch(group_copies(cots, held_c, group) + group_copies(spreads, held_s, group), sems)
    for copy in copies:
        copy.wait()
    for r in range(total // step):
        product = sum(
            lax.dot_general(
                held_c[g, r * step // group : (r + 1) * step // group].reshape(step, width),
                held_s[g].reshape(total, width),
                dims,
                preferred_element_type=F32,
            )
            for g in range(groups)
        )
        kept = jnp.where(same_place(step, total, group, 0), product, 0.0)
        lines = step // group
        summed[r * lines : (r + 1) * lines, :] = kept.reshape(lines, group, total).sum(axis=1)
    gather = spread_matrix(total, outer, group, 0, False).astype(F32)
    full = jnp.dot(
        summed[...], gather, preferred_element_type=F32, precision=lax.Precision.HIGHEST
    )
    store_halves(full, keep_ref, give_ref)


def left_gradient(n, cots, spreads):
    count, size, width = cots[0].shape
    group = group_of(n)
    outer = n * count
    total = outer * group
    groups = size // group
    scratch = pltpu.VMEM((groups, outer, group, width), BF16)
    return pl.pallas_call(
        functools.partial(left_kernel, n, group),
        in_specs=[HBM] * (2 * n),
        out_shape=halves(outer, outer),
        scratch_shapes=[
            scratch,
            scratch,
            pltpu.VMEM((outer, total), F32),
            pltpu.SemaphoreType.DMA((2 * groups * n,)),
        ],
        compiler_params=params(),
        cost_estimate=cost(2 * total * total * width * (size // group), 8 * n * count * size * width),
        name="left_gradient",
    )(*in_hbm(cots), *in_hbm(spreads))


def row_copies(ins, held):
    n = len(ins)
    size = ins[0].shape[1]
    return [
        (ins[k], held.at[:, pl.ds(pl.multiple_of(source * size, size), size), :])
        for k, source in enumerate(partners(n, -1))
    ]


def back_kernel(n, first_ref, nb_ref, right_ref, tw_ref, *rest):
    ins, (twg_ref, mm_ref, keep_ref, give_ref), (held, sems) = rest[:n], rest[n : n + 4], rest[n + 4 :]
    copies = fetch(row_copies(ins, held), sems)
    turned = right_ref[...].astype(F32).T.astype(BF16)
    for copy in copies:
        copy.wait()
    total = None
    for a in range(nb_ref.shape[0]):
        grad = held[a].astype(F32)
        twg_ref[a] = row_sums(grad * first_ref[a])
        first_grad = (grad * twiddle_column(tw_ref, a)).astype(BF16)
        mm_ref[a] = jnp.dot(turned, first_grad, preferred_element_type=F32)
        part = lax.dot_general(
            first_grad, nb_ref[a], (((1,), (1,)), ((), ())), preferred_element_type=F32
        )
        total = part if a == 0 else total + part
    store_halves(total, keep_ref, give_ref)


def back_first(n, blocks, first_mix, normed_b, right, twiddle):
    count, _, width = normed_b.shape
    return pl.pallas_call(
        functools.partial(back_kernel, n),
        in_specs=[VMEM] * 4 + [HBM] * n,
        out_specs=[VMEM] * 4,
        out_shape=[sds((count, 8, B), F32), sds((count, B, width), F32)] + halves(B, B),
        scratch_shapes=[pltpu.VMEM((count, B, width), BF16), pltpu.SemaphoreType.DMA((n,))],
        compiler_params=params(),
        cost_estimate=cost(4 * count * B * B * width, 12 * count * B * width),
        name="back_first",
    )(first_mix, normed_b, right, twiddle, *in_hbm(blocks))


def finish_kernel(n, tok_ref, cot_ref, sa_ref, sb_ref, gain_ref, slope_ref, bias_ref, mm_ref, *rest):
    ins, (mixed_ref, scaled_ref, inner_ref, sums_ref), (held, sems) = (
        rest[:n],
        rest[n : n + 4],
        rest[n + 4 :],
    )
    copies = fetch(row_copies(ins, held), sems)
    for copy in copies:
        copy.wait()
    scale = lax.rsqrt((sa_ref[...] + sb_ref[...]) / D + EPS)
    gains, slopes, biases = [], [], []
    for a in range(mm_ref.shape[0]):
        rows = slice(a * B, (a + 1) * B)
        second = held[a].astype(F32)
        wide = tok_ref[rows, :].astype(F32)
        unit = wide * column(scale[:, rows])
        normed = unit * gain_ref[...]
        gate = sigmoid(slope_ref[...] * normed + bias_ref[...])
        mixed_ref[rows, :] = (gate * second).astype(BF16)
        gate_grad = cot_ref[rows, :].astype(F32) * second * gate * (1.0 - gate)
        normed_grad = mm_ref[a] + gate_grad * slope_ref[...]
        scaled = normed_grad * gain_ref[...]
        scaled_ref[rows, :] = scaled
        inner_ref[:, rows] = row_sums(scaled * wide)
        gains.append(jnp.sum(normed_grad * unit, axis=0, keepdims=True))
        slopes.append(jnp.sum(gate_grad * normed, axis=0, keepdims=True))
        biases.append(jnp.sum(gate_grad, axis=0, keepdims=True))
    for i, terms in enumerate((gains, slopes, biases)):
        line = sum(terms)
        part = sums_ref.shape[1]
        lines = line.shape[1] // part
        for j in range(lines):
            at = i * lines + j
            sums_ref[at : at + 1, :] = line[:, j * part : (j + 1) * part]
    for at in range(3 * lines, sums_ref.shape[0]):
        sums_ref[at : at + 1, :] = jnp.zeros((1, part), F32)


def finish(n, blocks, tokens, cotangent, sa, sb, gain, slope, bias, mm, part):
    rows, width = tokens.shape
    return pl.pallas_call(
        functools.partial(finish_kernel, n),
        in_specs=[VMEM] * 8 + [HBM] * n,
        out_specs=[VMEM] * 4,
        out_shape=[sds((rows, width), BF16), sds((rows, width), F32), sds((8, rows), F32), sds((8, part), F32)],
        scratch_shapes=[pltpu.VMEM((rows // B, B, width), BF16), pltpu.SemaphoreType.DMA((n,))],
        compiler_params=params(),
        cost_estimate=cost(40 * rows * width, 16 * rows * width),
        name="finish",
    )(tokens, cotangent, sa, sb, gain, slope, bias, mm, *in_hbm(blocks))


def token_kernel(tok_ref, scaled_ref, sa_ref, sb_ref, ia_ref, ib_ref, out_ref):
    scale = lax.rsqrt((sa_ref[...] + sb_ref[...]) / D + EPS)
    inner = (ia_ref[...] + ib_ref[...]) * (scale * scale * scale) / D
    out_ref[...] = (
        column(scale) * scaled_ref[...] - tok_ref[...].astype(F32) * column(inner)
    ).astype(BF16)


def token_gradient(tokens, scaled, sa, sb, ia, ib):
    rows, width = tokens.shape
    tall = pl.BlockSpec((B, width), lambda a: (a, 0))
    row = pl.BlockSpec((8, B), lambda a: (0, a))
    return pl.pallas_call(
        token_kernel,
        grid=(rows // B,),
        in_specs=[tall, tall, row, row, row, row],
        out_specs=tall,
        out_shape=sds((rows, width), BF16),
        compiler_params=params(),
        cost_estimate=cost(5 * rows * width, 8 * rows * width),
        name="token_gradient",
    )(tokens, scaled, sa, sb, ia, ib)


def on_device(
    tokens, cotangent, norm_gain, gate_slope, gate_bias, right_factor, left_factor, twiddle
):
    n = lax.axis_size("seq")
    rows, width = tokens.shape
    gain, slope, bias = (v.reshape(1, width) for v in (norm_gain, gate_slope, gate_bias))
    sa, sb = chan_terms(squares(tokens))
    normed_b, cot_blocks = gate_cotangent(n, tokens, cotangent, sa, sb, gain, slope, bias)
    cot_cols = exchange(cot_blocks)
    right = chan_gather(right_factor)
    first_mix, spread_blocks = first_factor(n, normed_b, right, twiddle)
    spread_cols = exchange(spread_blocks)
    fore, back = widen(chan_gather(left_factor), group_of(n))

    cot_cols, spread_cols = after_part(cot_cols, spread_cols)
    grad_back = exchange(second_factor(n, back, cot_cols, "spread_grad"))
    spread_cols, grad_back = after_part(spread_cols, grad_back)
    mix_blocks = second_factor(n, fore, spread_cols, "second_mix")
    left_keep, left_give = left_gradient(n, cot_cols, spread_cols)
    la, lb = chan_joined(left_keep, left_give)
    left_give, mix_blocks = lax.optimization_barrier((left_give, mix_blocks))
    mix_back = exchange(mix_blocks)
    grad_back, mix_back = after_part(grad_back, mix_back, LAST)
    twiddle_rows, mm, right_keep, right_give = back_first(
        n, grad_back, first_mix, normed_b, right, twiddle
    )
    part = B // lax.axis_size("chan")
    mixed, scaled, inner, sums = finish(
        n, mix_back, tokens, cotangent, sa, sb, gain, slope, bias, mm, part
    )
    right_give, twiddle_rows, sums = lax.optimization_barrier((right_give, twiddle_rows, sums))
    ra, rb = chan_joined(right_keep, right_give)
    ia, ib = chan_terms(inner)
    token_grad = token_gradient(tokens, scaled, sa, sb, ia, ib)
    steps = bits(n)
    keep, message = join(steps[0], n, ra, rb, la, lb, sums)
    came = flipped(message, steps[0])
    for bit in steps[1:]:
        keep, sums, message = fold(bit, keep, sums, came)
        came = flipped(message, bit)
    ta, tb = chan_terms(twiddle_rows)
    right_out, left_out, twiddle_grad, *vectors = close(
        keep, sums, came, ta, tb, la.shape[0] // n, la.shape[1], width
    )
    return (mixed, token_grad, right_out, left_out, twiddle_grad, *(v.reshape(-1) for v in vectors))


def solution(mesh):
    return jax.shard_map(
        on_device,
        mesh=mesh,
        in_specs=(
            P("seq", "chan"),
            P("seq", "chan"),
            P("chan"),
            P("chan"),
            P("chan"),
            P("chan", None),
            P("chan", None),
            P("seq", None),
        ),
        out_specs=(
            P("seq", "chan"),
            P("seq", "chan"),
            P("seq", "chan"),
            P("seq", "chan"),
            P("seq", None),
            P("chan"),
            P("chan"),
            P("chan"),
        ),
        check_vma=False,
    )
```

time: 273 us -> 249 us (0.912)
  Pallas kernels: 62.2 us -> 40.8 us
  waiting for transfers between devices: 47.6 us -> 58.3 us
  starting transfers between devices: 148 us -> 142 us
  other arithmetic: 5.14 us -> 1.12 us
    ppermute x2 -> x6, waiting for transfers between devices: 1.2 us -> 15.8 us  [the longest x4 14.3 us: flipped(): return lax.ppermute(x, 'seq', [(i, i ^ bit) for i in range(n)])]
    ppermute x2 -> x6, starting transfers between devices: 0.08 us -> 9.94 us  [the longest x4 9.37 us: flipped(): return lax.ppermute(x, 'seq', [(i, i ^ bit) for i in range(n)])]
    ppermute x60, starting transfers between devices: 140 us -> 131 us  [exchange(): out[k] = lax.ppermute(blocks[k], 'seq', pairs(n, k))]
    all_to_all x1 -> x0, waiting for transfers between devices: 8.57 us -> none  [on_device(): lax.all_to_all(jnp.concatenate([right_flat, left_flat, small], axis=1), '...]
    pallas_call x5 -> x10, Pallas kernels: 36.7 us -> 28.2 us  [the longest x2 8.48 us: second_factor(): pl.pallas_call(functools.partial(second_kernel, n, group), in_specs=[VMEM...]
    ppermute x60, waiting for transfers between devices: 34.5 us -> 41.6 us  [exchange(): out[k] = lax.ppermute(blocks[k], 'seq', pairs(n, k))]
    all_to_all x1 -> x0, starting transfers between devices: 6.67 us -> none  [on_device(): lax.all_to_all(jnp.concatenate([right_flat, left_flat, small], axis=1), '...]
    pallas_call x1, Pallas kernels: 5.76 us -> 2.21 us  [first_factor(): pl.pallas_call(functools.partial(first_kernel, n), grid=(blocks,), in_spe...]
  transfers between devices with their start and end apart: 68 -> 71, of which waited for: 20 -> 19; matrix products, arithmetic and copies ran while one was open for 2% -> 0% of each run, Pallas kernels for 20% -> 11%
where the time goes in v2:
time: 249 us
  starting transfers between devices  142 us (57%)
  waiting for transfers between devices  58.3 us (23%)
  Pallas kernels  40.8 us (16%)
  local copies, waits for them, and re-layouts  4.44 us (2%)
    ppermute x60, starting transfers between devices, exchange(): out[k] = lax.ppermute(blocks[k], 'seq', pairs(n, k))  131 us
    ppermute x60, waiting for transfers between devices, exchange(): out[k] = lax.ppermute(blocks[k], 'seq', pairs(n, k))  41.6 us
    ppermute x4, waiting for transfers between devices, flipped(): return lax.ppermute(x, 'seq', [(i, i ^ bit) for i in range(n)])  14.3 us
    ppermute x4, starting transfers between devices, flipped(): return lax.ppermute(x, 'seq', [(i, i ^ bit) for i in range(n)])  9.37 us
    pallas_call x2, Pallas kernels, second_factor(): pl.pallas_call(functools.partial(second_kernel, n, group), in_specs=[VMEM...  8.48 us
    pallas_call x1, Pallas kernels, finish(): pl.pallas_call(functools.partial(finish_kernel, n), in_specs=[VMEM] * 8 +...  7.38 us
    pallas_call x1, Pallas kernels, left_gradient(): pl.pallas_call(functools.partial(left_kernel, n, group), in_specs=[HBM] *...  5.82 us
    pallas_call x1, Pallas kernels, back_first(): pl.pallas_call(functools.partial(back_kernel, n), in_specs=[VMEM] * 4 + [...  5.72 us
  transfers between devices with their start and end apart: 71, of which 19 were waited for; matrix products, arithmetic and copies ran while one was open for 0% of the time, Pallas kernels for 11%

profile of v2, /device:TPU:0, one launch (start us, length us, event | category | flops | bytes accessed | tf_op | source)
XLA Modules:
  0.0 248.5 jit_solution(10357869777616517103)
XLA Ops:
  32.4 10.3 %collective-permute-start.13 = (bf16[4,32,512]{2,1,0:T(8,128)(2,1)S(1)}, bf16[4,32,512]{2,1,0:T(8,128)(2,1)S(1)}, u32[]{:S(2)}, u32[]{:S(2)}) collective-permute-start(bf16[4,32,512]{2,1,0:T(8,128)(2,1)S(1)} %get-tuple-element.210), channel_id=1, source_target_pairs={{0,22},{2,20},{4,18},{6,16},{8,30},{10,28},{12,26},{14,24},{16,6},... | collective-permute-start | bytes 393224 | tf_op jit(solution)/shard_map/ppermute | solution.py:76
  50.6 7.5 %collective-permute-start.16 = (bf16[4,32,512]{2,1,0:T(8,128)(2,1)S(1)}, bf16[4,32,512]{2,1,0:T(8,128)(2,1)S(1)}, u32[]{:S(2)}, u32[]{:S(2)}) collective-permute-start(bf16[4,32,512]{2,1,0:T(8,128)(2,1)S(1)} %get-tuple-element.213), channel_id=1, source_target_pairs={{0,28},{2,30},{4,24},{6,26},{8,4},{10,6},{12,0},{14,2},{16,12},{18... | collective-permute-start | bytes 393224 | tf_op jit(solution)/shard_map/ppermute | solution.py:76
  70.8 7.7 %collective-permute-done.18.rest_24_.rest_8_ = bf16[4,32,512]{2,1,0:T(8,128)(2,1)S(1)} collective-permute-done((bf16[4,32,512]{2,1,0:T(8,128)(2,1)S(1)}, bf16[4,32,512]{2,1,0:T(8,128)(2,1)S(1)}, u32[]{:S(2)}, u32[]{:S(2)}) %collective-permute-start.18) | collective-permute-done | bytes 131104 | tf_op jit(solution)/shard_map/ppermute | solution.py:76
  78.5 4.7 %collective-permute-start.24 = (bf16[4,32,512]{2,1,0:T(8,128)(2,1)S(1)}, bf16[4,32,512]{2,1,0:T(8,128)(2,1)S(1)}, u32[]{:S(2)}, u32[]{:S(2)}) collective-permute-start(bf16[4,32,512]{2,1,0:T(8,128)(2,1)S(1)} %get-tuple-element.221), channel_id=1, source_target_pairs={{0,26},{2,24},{4,30},{6,28},{8,2},{10,0},{12,6},{14,4},{16,10},{18... | collective-permute-start | bytes 393224 | tf_op jit(solution)/shard_map/ppermute | solution.py:76
  94.2 5.6 %collective-permute-start.31 = (bf16[4,32,512]{2,1,0:T(8,128)(2,1)S(1)}, bf16[4,32,512]{2,1,0:T(8,128)(2,1)S(1)}, u32[]{:S(2)}, u32[]{:S(2)}) collective-permute-start(bf16[4,32,512]{2,1,0:T(8,128)(2,1)S(1)} %get-tuple-element.254), channel_id=1, source_target_pairs={{0,28},{2,30},{4,24},{6,26},{8,4},{10,6},{12,0},{14,2},{16,12},{18... | collective-permute-start | bytes 393224 | tf_op jit(solution)/shard_map/ppermute | solution.py:76
  99.8 5.3 %collective-permute-start.32 = (bf16[4,32,512]{2,1,0:T(8,128)(2,1)S(1)}, bf16[4,32,512]{2,1,0:T(8,128)(2,1)S(1)}, u32[]{:S(2)}, u32[]{:S(2)}) collective-permute-start(bf16[4,32,512]{2,1,0:T(8,128)(2,1)S(1)} %get-tuple-element.255), channel_id=1, source_target_pairs={{0,30},{2,28},{4,26},{6,24},{8,6},{10,4},{12,2},{14,0},{16,14},{18... | collective-permute-start | bytes 393224 | tf_op jit(solution)/shard_map/ppermute | solution.py:76
  107.9 4.2 %spread_grad.1 = (bf16[4,32,512]{2,1,0:T(8,128)(2,1)S(1)}, bf16[4,32,512]{2,1,0:T(8,128)(2,1)S(1)}, bf16[4,32,512]{2,1,0:T(8,128)(2,1)S(1)}, bf16[4,32,512]{2,1,...) custom-call(bf16[1024,1024]{1,0:T(8,128)(2,1)S(1)} %get-tuple-elemen, ...), custom_call_target="tpu_custom_call" | custom-call | flops 2147483 | bytes 8388 | tf_op jit(solution)/shard_map/spread_grad/pallas_call | solution.py:445
  112.4 9.9 %collective-permute-start.35 = (bf16[4,32,512]{2,1,0:T(8,128)(2,1)S(1)}, bf16[4,32,512]{2,1,0:T(8,128)(2,1)S(1)}, u32[]{:S(2)}, u32[]{:S(2)}) collective-permute-start(bf16[4,32,512]{2,1,0:T(8,128)(2,1)S(1)} %get-tuple-element.258), channel_id=1, source_target_pairs={{0,24},{2,26},{4,28},{6,30},{8,0},{10,2},{12,4},{14,6},{16,8},{18,... | collective-permute-start | bytes 393224 | tf_op jit(solution)/shard_map/ppermute | solution.py:76
  127.3 3.5 %collective-permute-start.40 = (bf16[4,32,512]{2,1,0:T(8,128)(2,1)S(1)}, bf16[4,32,512]{2,1,0:T(8,128)(2,1)S(1)}, u32[]{:S(2)}, u32[]{:S(2)}) collective-permute-start(bf16[4,32,512]{2,1,0:T(8,128)(2,1)S(1)} %get-tuple-element.263), channel_id=1, source_target_pairs={{0,4},{2,6},{4,0},{6,2},{8,12},{10,14},{12,8},{14,10},{16,20},{18,... | collective-permute-start | bytes 393224 | tf_op jit(solution)/shard_map/ppermute | solution.py:76
  130.8 5.5 %collective-permute-done.36.rest_1_ = bf16[4,32,512]{2,1,0:T(8,128)(2,1)S(1)} collective-permute-done((bf16[4,32,512]{2,1,0:T(8,128)(2,1)S(1)}, bf16[4,32,512]{2,1,0:T(8,128)(2,1)S(1)}, u32[]{:S(2)}, u32[]{:S(2)}) %collective-permute-start.36) | collective-permute-done | bytes 131104 | tf_op jit(solution)/shard_map/ppermute | solution.py:76
  137.7 6.2 %collective-permute-start.44 = (bf16[4,32,512]{2,1,0:T(8,128)(2,1)S(1)}, bf16[4,32,512]{2,1,0:T(8,128)(2,1)S(1)}, u32[]{:S(2)}, u32[]{:S(2)}) collective-permute-start(bf16[4,32,512]{2,1,0:T(8,128)(2,1)S(1)} %get-tuple-element.273), channel_id=1, source_target_pairs={{0,20},{2,22},{4,16},{6,18},{8,28},{10,30},{12,24},{14,26},{16,4},... | collective-permute-start | bytes 393224 | tf_op jit(solution)/shard_map/ppermute | solution.py:76
  144.0 5.9 %collective-permute-start.45 = (bf16[4,32,512]{2,1,0:T(8,128)(2,1)S(1)}, bf16[4,32,512]{2,1,0:T(8,128)(2,1)S(1)}, u32[]{:S(2)}, u32[]{:S(2)}) collective-permute-start(bf16[4,32,512]{2,1,0:T(8,128)(2,1)S(1)} %get-tuple-element.274), channel_id=1, source_target_pairs={{0,22},{2,20},{4,18},{6,16},{8,30},{10,28},{12,26},{14,24},{16,6},... | collective-permute-start | bytes 393224 | tf_op jit(solution)/shard_map/ppermute | solution.py:76
  152.9 5.8 %left_gradient.1 = (f32[64,32]{1,0:T(8,128)S(1)}, f32[64,32]{1,0:T(8,128)S(1)}) custom-call(bf16[4,32,512]{2,1,0:T(8,128)(2,1)} %copy-done.4, bf16[4,32,512]{2,1,0:T(8,128)(2,1)} %copy-done.12, bf16[4,32,512]{2,1,0:T(8,128)(2,1)} %copy-done.13, bf16[4,32,512]{2,1,0:T(8,128)(2,1)} %copy-done.14, bf16[4,32,512]{2,1,0:T(8,128)(2,1)} %copy-done.15, ...), custom_call_target="tpu_custom_call" | custom-call | flops 2147483 | bytes 8388 | tf_op jit(solution)/shard_map/left_gradient/pallas_call | solution.py:513
  158.8 4.2 %second_mix.1 = (bf16[4,32,512]{2,1,0:T(8,128)(2,1)S(1)}, bf16[4,32,512]{2,1,0:T(8,128)(2,1)S(1)}, bf16[4,32,512]{2,1,0:T(8,128)(2,1)S(1)}, bf16[4,32,512]{2,1,0...) custom-call(bf16[1024,1024]{1,0:T(8,128)(2,1)S(1)} %get-tuple-elemen, ...), custom_call_target="tpu_custom_call" | custom-call | flops 2147483 | bytes 8388 | tf_op jit(solution)/shard_map/second_mix/pallas_call | solution.py:445
  164.0 3.7 %collective-permute-start.49 = (bf16[4,32,512]{2,1,0:T(8,128)(2,1)S(1)}, bf16[4,32,512]{2,1,0:T(8,128)(2,1)S(1)}, u32[]{:S(2)}, u32[]{:S(2)}) collective-permute-start(bf16[4,32,512]{2,1,0:T(8,128)(2,1)S(1)} %get-tuple-element.314), channel_id=1, source_target_pairs={{0,8},{2,10},{4,12},{6,14},{8,16},{10,18},{12,20},{14,22},{16,24},... | collective-permute-start | bytes 393224 | tf_op jit(solution)/shard_map/ppermute | solution.py:76
  170.7 6.9 %collective-permute-done.48.rest_8_ = bf16[4,32,512]{2,1,0:T(8,128)(2,1)S(1)} collective-permute-done((bf16[4,32,512]{2,1,0:T(8,128)(2,1)S(1)}, bf16[4,32,512]{2,1,0:T(8,128)(2,1)S(1)}, u32[]{:S(2)}, u32[]{:S(2)}) %collective-permute-start.48) | collective-permute-done | bytes 131104 | tf_op jit(solution)/shard_map/ppermute | solution.py:76
  177.6 4.7 %collective-permute-start.54 = (bf16[4,32,512]{2,1,0:T(8,128)(2,1)S(1)}, bf16[4,32,512]{2,1,0:T(8,128)(2,1)S(1)}, u32[]{:S(2)}, u32[]{:S(2)}) collective-permute-start(bf16[4,32,512]{2,1,0:T(8,128)(2,1)S(1)} %get-tuple-element.319), channel_id=1, source_target_pairs={{0,26},{2,24},{4,30},{6,28},{8,2},{10,0},{12,6},{14,4},{16,10},{18... | collective-permute-start | bytes 393224 | tf_op jit(solution)/shard_map/ppermute | solution.py:76
  183.0 3.5 %collective-permute-start.56 = (bf16[4,32,512]{2,1,0:T(8,128)(2,1)S(1)}, bf16[4,32,512]{2,1,0:T(8,128)(2,1)S(1)}, u32[]{:S(2)}, u32[]{:S(2)}) collective-permute-start(bf16[4,32,512]{2,1,0:T(8,128)(2,1)S(1)} %get-tuple-element.321), channel_id=1, source_target_pairs={{0,20},{2,22},{4,16},{6,18},{8,28},{10,30},{12,24},{14,26},{16,4},... | collective-permute-start | bytes 393224 | tf_op jit(solution)/shard_map/ppermute | solution.py:76
  190.9 4.8 %collective-permute-start.59 = (bf16[4,32,512]{2,1,0:T(8,128)(2,1)S(1)}, bf16[4,32,512]{2,1,0:T(8,128)(2,1)S(1)}, u32[]{:S(2)}, u32[]{:S(2)}) collective-permute-start(bf16[4,32,512]{2,1,0:T(8,128)(2,1)S(1)} %get-tuple-element.347), channel_id=1, source_target_pairs={{0,14},{2,12},{4,10},{6,8},{8,22},{10,20},{12,18},{14,16},{16,30},... | collective-permute-start | bytes 393224 | tf_op jit(solution)/shard_map/ppermute | solution.py:76
  196.9 5.7 %collective-permute-done.56.rest_10_ = bf16[4,32,512]{2,1,0:T(8,128)(2,1)S(1)} collective-permute-done((bf16[4,32,512]{2,1,0:T(8,128)(2,1)S(1)}, bf16[4,32,512]{2,1,0:T(8,128)(2,1)S(1)}, u32[]{:S(2)}, u32[]{:S(2)}) %collective-permute-start.56) | collective-permute-done | bytes 131104 | tf_op jit(solution)/shard_map/ppermute | solution.py:76
  204.2 5.7 %back_first.1 = (f32[4,8,512]{2,1,0:T(8,128)S(1)}, f32[4,512,512]{2,1,0:T(8,128)S(1)}, f32[512,256]{1,0:T(8,128)S(1)}, f32[512,256]{1,0:T(8,128)S(1)}) custom-call(f32[4,512,512]{2,1,0:T(8,128)S(1)} %get-tuple-element.197.first_ref, bf16[4,512,512]{2,1,0:T(8,128)(2,1)S(1)} %get-tuple-element.196.nb_ref, bf16[512,512]{1,0:T(8,128)(2,1)S(1)} %pad_maximum_fusion.right_ref, ...), custom_call_target="tpu_custom_call" | custom-call | flops 2147483 | bytes 12582 | tf_op jit(solution)/shard_map/back_first/pallas_call | solution.py:559
  210.9 7.4 %finish.1 = (bf16[2048,512]{1,0:T(8,128)(2,1)}, f32[2048,512]{1,0:T(8,128)S(1)}, f32[8,2048]{1,0:T(8,128)S(1)}, f32[8,256]{1,0:T(8,128)S(1)}) custom-call(bf16[2048,512]{1,0:T(8,128)(2,1)S(1)} %copy-done.1, bf16[2048,512]{1,0:T(8,128)(2,1)S(1)} %copy-done.3, f32[8,2048]{1,0:T(8,128)S(1)} %squares.1.sa_ref, f32[8,2048]{1,0:T(8,128)S(1)} %collective-permute-done.sb_ref, ...), custom_call_target="tpu_custom_call" | custom-call | flops 41943 | bytes 16777 | tf_op jit(solution)/shard_map/finish/pallas_call | solution.py:611
  222.0 8.5 %collective-permute-done.66.came = f32[328,256]{1,0:T(8,128)S(1)} collective-permute-done((f32[328,256]{1,0:T(8,128)S(1)}, f32[328,256]{1,0:T(8,128)S(1)}, u32[]{:S(2)}, u32[]{:S(2)}) %collective-permute-start.66) | collective-permute-done | bytes 335904 | tf_op jit(solution)/shard_map/ppermute | solution.py:127
  232.7 3.8 %collective-permute-done.67.came = f32[168,256]{1,0:T(8,128)S(1)} collective-permute-done((f32[168,256]{1,0:T(8,128)S(1)}, f32[168,256]{1,0:T(8,128)S(1)}, u32[]{:S(2)}, u32[]{:S(2)}) %collective-permute-start.67) | collective-permute-done | bytes 172064 | tf_op jit(solution)/shard_map/ppermute | solution.py:127
  (275 shorter events, 105.8 us)
Async XLA Ops:
  20.4 37.7 %collective-permute-start.1 = (bf16[256,512]{1,0:T(8,128)(2,1)}, bf16[256,512]{1,0:T(8,128)(2,1)}, u32[]{:S(2)}, u32[]{:S(2)}) collective-permute-start(bf16[256,512]{1,0:T(8,128)(2,1)} %param.13), channel_id=1, source_target_pairs={{0,1},{1,0},{2,3},{3,2},{4,5},{5,4},{6,7},{7,6},{8,9},{9,8},{10,11... | collective-permute-start | bytes 786440 | tf_op jit(solution)/shard_map/ppermute | solution.py:104
  22.4 20.2 %collective-permute-start.10 = (bf16[4,32,512]{2,1,0:T(8,128)(2,1)S(1)}, bf16[4,32,512]{2,1,0:T(8,128)(2,1)}, u32[]{:S(2)}, u32[]{:S(2)}) collective-permute-start(bf16[4,32,512]{2,1,0:T(8,128)(2,1)S(1)} %get-tuple-element.207), channel_id=1, source_target_pairs={{0,16},{2,18},{4,20},{6,22},{8,24},{10,26},{12,28},{14,30},{16,0},... | collective-permute-start | bytes 393224 | tf_op jit(solution)/shard_map/ppermute | solution.py:76
  25.6 22.1 %collective-permute-start.11 = (bf16[4,32,512]{2,1,0:T(8,128)(2,1)S(1)}, bf16[4,32,512]{2,1,0:T(8,128)(2,1)}, u32[]{:S(2)}, u32[]{:S(2)}) collective-permute-start(bf16[4,32,512]{2,1,0:T(8,128)(2,1)S(1)} %get-tuple-element.208), channel_id=1, source_target_pairs={{0,18},{2,16},{4,22},{6,20},{8,26},{10,24},{12,30},{14,28},{16,2},... | collective-permute-start | bytes 393224 | tf_op jit(solution)/shard_map/ppermute | solution.py:76
  28.5 22.0 %collective-permute-start.12 = (bf16[4,32,512]{2,1,0:T(8,128)(2,1)S(1)}, bf16[4,32,512]{2,1,0:T(8,128)(2,1)}, u32[]{:S(2)}, u32[]{:S(2)}) collective-permute-start(bf16[4,32,512]{2,1,0:T(8,128)(2,1)S(1)} %get-tuple-element.209), channel_id=1, source_target_pairs={{0,20},{2,22},{4,16},{6,18},{8,28},{10,30},{12,24},{14,26},{16,4},... | collective-permute-start | bytes 393224 | tf_op jit(solution)/shard_map/ppermute | solution.py:76
  32.4 31.0 %collective-permute-start.13 = (bf16[4,32,512]{2,1,0:T(8,128)(2,1)S(1)}, bf16[4,32,512]{2,1,0:T(8,128)(2,1)S(1)}, u32[]{:S(2)}, u32[]{:S(2)}) collective-permute-start(bf16[4,32,512]{2,1,0:T(8,128)(2,1)S(1)} %get-tuple-element.210), channel_id=1, source_target_pairs={{0,22},{2,20},{4,18},{6,16},{8,30},{10,28},{12,26},{14,24},{16,6},... | collective-permute-start | bytes 393224 | tf_op jit(solution)/shard_map/ppermute | solution.py:76
  42.6 20.7 %collective-permute-start.14 = (bf16[4,32,512]{2,1,0:T(8,128)(2,1)S(1)}, bf16[4,32,512]{2,1,0:T(8,128)(2,1)S(1)}, u32[]{:S(2)}, u32[]{:S(2)}) collective-permute-start(bf16[4,32,512]{2,1,0:T(8,128)(2,1)S(1)} %get-tuple-element.211), channel_id=1, source_target_pairs={{0,24},{2,26},{4,28},{6,30},{8,0},{10,2},{12,4},{14,6},{16,8},{18,... | collective-permute-start | bytes 393224 | tf_op jit(solution)/shard_map/ppermute | solution.py:76
  47.7 18.7 %collective-permute-start.15 = (bf16[4,32,512]{2,1,0:T(8,128)(2,1)S(1)}, bf16[4,32,512]{2,1,0:T(8,128)(2,1)S(1)}, u32[]{:S(2)}, u32[]{:S(2)}) collective-permute-start(bf16[4,32,512]{2,1,0:T(8,128)(2,1)S(1)} %get-tuple-element.212), channel_id=1, source_target_pairs={{0,26},{2,24},{4,30},{6,28},{8,2},{10,0},{12,6},{14,4},{16,10},{18... | collective-permute-start | bytes 393224 | tf_op jit(solution)/shard_map/ppermute | solution.py:76
  50.6 18.2 %collective-permute-start.16 = (bf16[4,32,512]{2,1,0:T(8,128)(2,1)S(1)}, bf16[4,32,512]{2,1,0:T(8,128)(2,1)S(1)}, u32[]{:S(2)}, u32[]{:S(2)}) collective-permute-start(bf16[4,32,512]{2,1,0:T(8,128)(2,1)S(1)} %get-tuple-element.213), channel_id=1, source_target_pairs={{0,28},{2,30},{4,24},{6,26},{8,4},{10,6},{12,0},{14,2},{16,12},{18... | collective-permute-start | bytes 393224 | tf_op jit(solution)/shard_map/ppermute | solution.py:76
  66.4 16.9 %collective-permute-start.20 = (bf16[4,32,512]{2,1,0:T(8,128)(2,1)S(1)}, bf16[4,32,512]{2,1,0:T(8,128)(2,1)S(1)}, u32[]{:S(2)}, u32[]{:S(2)}) collective-permute-start(bf16[4,32,512]{2,1,0:T(8,128)(2,1)S(1)} %get-tuple-element.217), channel_id=1, source_target_pairs={{0,24},{2,26},{4,28},{6,30},{8,0},{10,2},{12,4},{14,6},{16,8},{18,... | collective-permute-start | bytes 393224 | tf_op jit(solution)/shard_map/ppermute | solution.py:76
  69.0 16.9 %collective-permute-start.22 = (bf16[4,32,512]{2,1,0:T(8,128)(2,1)S(1)}, bf16[4,32,512]{2,1,0:T(8,128)(2,1)S(1)}, u32[]{:S(2)}, u32[]{:S(2)}) collective-permute-start(bf16[4,32,512]{2,1,0:T(8,128)(2,1)S(1)} %get-tuple-element.219), channel_id=1, source_target_pairs={{0,18},{2,16},{4,22},{6,20},{8,26},{10,24},{12,30},{14,28},{16,2},... | collective-permute-start | bytes 393224 | tf_op jit(solution)/shard_map/ppermute | solution.py:76
  86.7 25.5 %collective-permute-start.28 = (bf16[4,32,512]{2,1,0:T(8,128)(2,1)S(1)}, bf16[4,32,512]{2,1,0:T(8,128)(2,1)S(1)}, u32[]{:S(2)}, u32[]{:S(2)}) collective-permute-start(bf16[4,32,512]{2,1,0:T(8,128)(2,1)S(1)} %get-tuple-element.247), channel_id=1, source_target_pairs={{0,14},{2,12},{4,10},{6,8},{8,22},{10,20},{12,18},{14,16},{16,30},... | collective-permute-start | bytes 393224 | tf_op jit(solution)/shard_map/ppermute | solution.py:76
  89.6 22.7 %collective-permute-start.29 = (bf16[4,32,512]{2,1,0:T(8,128)(2,1)S(1)}, bf16[4,32,512]{2,1,0:T(8,128)(2,1)S(1)}, u32[]{:S(2)}, u32[]{:S(2)}) collective-permute-start(bf16[4,32,512]{2,1,0:T(8,128)(2,1)S(1)} %get-tuple-element.250), channel_id=1, source_target_pairs={{0,20},{2,22},{4,16},{6,18},{8,28},{10,30},{12,24},{14,26},{16,4},... | collective-permute-start | bytes 393224 | tf_op jit(solution)/shard_map/ppermute | solution.py:76
  94.2 18.2 %collective-permute-start.30 = (bf16[4,32,512]{2,1,0:T(8,128)(2,1)S(1)}, bf16[4,32,512]{2,1,0:T(8,128)(2,1)S(1)}, u32[]{:S(2)}, u32[]{:S(2)}) collective-permute-start(bf16[4,32,512]{2,1,0:T(8,128)(2,1)S(1)} %get-tuple-element.251), channel_id=1, source_target_pairs={{0,22},{2,20},{4,18},{6,16},{8,30},{10,28},{12,26},{14,24},{16,6},... | collective-permute-start | bytes 393224 | tf_op jit(solution)/shard_map/ppermute | solution.py:76
  94.2 28.1 %collective-permute-start.31 = (bf16[4,32,512]{2,1,0:T(8,128)(2,1)S(1)}, bf16[4,32,512]{2,1,0:T(8,128)(2,1)S(1)}, u32[]{:S(2)}, u32[]{:S(2)}) collective-permute-start(bf16[4,32,512]{2,1,0:T(8,128)(2,1)S(1)} %get-tuple-element.254), channel_id=1, source_target_pairs={{0,28},{2,30},{4,24},{6,26},{8,4},{10,6},{12,0},{14,2},{16,12},{18... | collective-permute-start | bytes 393224 | tf_op jit(solution)/shard_map/ppermute | solution.py:76
  99.8 22.5 %collective-permute-start.32 = (bf16[4,32,512]{2,1,0:T(8,128)(2,1)S(1)}, bf16[4,32,512]{2,1,0:T(8,128)(2,1)S(1)}, u32[]{:S(2)}, u32[]{:S(2)}) collective-permute-start(bf16[4,32,512]{2,1,0:T(8,128)(2,1)S(1)} %get-tuple-element.255), channel_id=1, source_target_pairs={{0,30},{2,28},{4,26},{6,24},{8,6},{10,4},{12,2},{14,0},{16,14},{18... | collective-permute-start | bytes 393224 | tf_op jit(solution)/shard_map/ppermute | solution.py:76
  136.4 27.3 %collective-permute-start.43 = (bf16[4,32,512]{2,1,0:T(8,128)(2,1)S(1)}, bf16[4,32,512]{2,1,0:T(8,128)(2,1)S(1)}, u32[]{:S(2)}, u32[]{:S(2)}) collective-permute-start(bf16[4,32,512]{2,1,0:T(8,128)(2,1)S(1)} %get-tuple-element.270), channel_id=1, source_target_pairs={{0,14},{2,12},{4,10},{6,8},{8,22},{10,20},{12,18},{14,16},{16,30},... | collective-permute-start | bytes 393224 | tf_op jit(solution)/shard_map/ppermute | solution.py:76
  137.7 26.3 %collective-permute-start.44 = (bf16[4,32,512]{2,1,0:T(8,128)(2,1)S(1)}, bf16[4,32,512]{2,1,0:T(8,128)(2,1)S(1)}, u32[]{:S(2)}, u32[]{:S(2)}) collective-permute-start(bf16[4,32,512]{2,1,0:T(8,128)(2,1)S(1)} %get-tuple-element.273), channel_id=1, source_target_pairs={{0,20},{2,22},{4,16},{6,18},{8,28},{10,30},{12,24},{14,26},{16,4},... | collective-permute-start | bytes 393224 | tf_op jit(solution)/shard_map/ppermute | solution.py:76
  144.0 23.7 %collective-permute-start.45 = (bf16[4,32,512]{2,1,0:T(8,128)(2,1)S(1)}, bf16[4,32,512]{2,1,0:T(8,128)(2,1)S(1)}, u32[]{:S(2)}, u32[]{:S(2)}) collective-permute-start(bf16[4,32,512]{2,1,0:T(8,128)(2,1)S(1)} %get-tuple-element.274), channel_id=1, source_target_pairs={{0,22},{2,20},{4,18},{6,16},{8,30},{10,28},{12,26},{14,24},{16,6},... | collective-permute-start | bytes 393224 | tf_op jit(solution)/shard_map/ppermute | solution.py:76
  149.9 17.9 %collective-permute-start.46 = (bf16[4,32,512]{2,1,0:T(8,128)(2,1)S(1)}, bf16[4,32,512]{2,1,0:T(8,128)(2,1)S(1)}, u32[]{:S(2)}, u32[]{:S(2)}) collective-permute-start(bf16[4,32,512]{2,1,0:T(8,128)(2,1)S(1)} %get-tuple-element.277), channel_id=1, source_target_pairs={{0,28},{2,30},{4,24},{6,26},{8,4},{10,6},{12,0},{14,2},{16,12},{18... | collective-permute-start | bytes 393224 | tf_op jit(solution)/shard_map/ppermute | solution.py:76
  151.0 19.5 %collective-permute-start.47 = (bf16[4,32,512]{2,1,0:T(8,128)(2,1)S(1)}, bf16[4,32,512]{2,1,0:T(8,128)(2,1)S(1)}, u32[]{:S(2)}, u32[]{:S(2)}) collective-permute-start(bf16[4,32,512]{2,1,0:T(8,128)(2,1)S(1)} %get-tuple-element.278), channel_id=1, source_target_pairs={{0,30},{2,28},{4,26},{6,24},{8,6},{10,4},{12,2},{14,0},{16,14},{18... | collective-permute-start | bytes 393224 | tf_op jit(solution)/shard_map/ppermute | solution.py:76
  170.5 17.9 %collective-permute-start.52 = (bf16[4,32,512]{2,1,0:T(8,128)(2,1)S(1)}, bf16[4,32,512]{2,1,0:T(8,128)(2,1)S(1)}, u32[]{:S(2)}, u32[]{:S(2)}) collective-permute-start(bf16[4,32,512]{2,1,0:T(8,128)(2,1)S(1)} %get-tuple-element.317), channel_id=1, source_target_pairs={{0,18},{2,16},{4,22},{6,20},{8,26},{10,24},{12,30},{14,28},{16,2},... | collective-permute-start | bytes 393224 | tf_op jit(solution)/shard_map/ppermute | solution.py:76
  183.0 19.6 %collective-permute-start.56 = (bf16[4,32,512]{2,1,0:T(8,128)(2,1)S(1)}, bf16[4,32,512]{2,1,0:T(8,128)(2,1)S(1)}, u32[]{:S(2)}, u32[]{:S(2)}) collective-permute-start(bf16[4,32,512]{2,1,0:T(8,128)(2,1)S(1)} %get-tuple-element.321), channel_id=1, source_target_pairs={{0,20},{2,22},{4,16},{6,18},{8,28},{10,30},{12,24},{14,26},{16,4},... | collective-permute-start | bytes 393224 | tf_op jit(solution)/shard_map/ppermute | solution.py:76
  188.4 21.6 %collective-permute-start.58 = (bf16[4,32,512]{2,1,0:T(8,128)(2,1)S(1)}, bf16[4,32,512]{2,1,0:T(8,128)(2,1)S(1)}, u32[]{:S(2)}, u32[]{:S(2)}) collective-permute-start(bf16[4,32,512]{2,1,0:T(8,128)(2,1)S(1)} %get-tuple-element.343), channel_id=1, source_target_pairs={{0,6},{2,4},{4,2},{6,0},{8,14},{10,12},{12,10},{14,8},{16,22},{18,... | collective-permute-start | bytes 393224 | tf_op jit(solution)/shard_map/ppermute | solution.py:76
  190.9 19.2 %collective-permute-start.59 = (bf16[4,32,512]{2,1,0:T(8,128)(2,1)S(1)}, bf16[4,32,512]{2,1,0:T(8,128)(2,1)S(1)}, u32[]{:S(2)}, u32[]{:S(2)}) collective-permute-start(bf16[4,32,512]{2,1,0:T(8,128)(2,1)S(1)} %get-tuple-element.347), channel_id=1, source_target_pairs={{0,14},{2,12},{4,10},{6,8},{8,22},{10,20},{12,18},{14,16},{16,30},... | collective-permute-start | bytes 393224 | tf_op jit(solution)/shard_map/ppermute | solution.py:76
  (116 other events, 1939.6 us)

commit v3 on v2

--- a/solution.py
+++ b/solution.py
@@ -11,7 +11,7 @@
 B = 512
 EPS = 1e-05
 LAG = 8
-LAST = 10
+LAST = 6
 SHARE = 1000
 
 F32 = jnp.float32
@@ -59,6 +59,8 @@
 
 
 def send_order(n):
+    if n == 16:
+        return [1, 8, 4, 12, 2, 9, 5, 13, 3, 10, 6, 14, 11, 7, 15]
     high = n // 4
     far_first = sorted(range(1, high), key=lambda d: (abs(d - high / 2), d))
     order = []
@@ -139,7 +141,7 @@
         message[q * size : (q + 1) * size, :] = blocks(2 * q + 1 - mine)
 
 
-def join_kernel(bit, ra_ref, rb_ref, la_ref, lb_ref, sums_ref, keep_ref, message, held):
+def join_kernel(bit, ra_ref, rb_ref, la_ref, lb_ref, keep_ref, message, held):
     n, size, width = held.shape
     rows = size - 8
     count = la_ref.shape[0] // n
@@ -150,28 +152,28 @@
     for q in range(n):
         held[q, rows : rows + count, :thin] = left[q * count : (q + 1) * count, :]
     write_split(bit, lambda q: held[q], keep_ref, message)
-    message[n // 2 * size :, :] = sums_ref[...]
-
-
-def join(bit, n, ra, rb, la, lb, sums):
+
+
+def join(bit, n, ra, rb, la, lb):
     rows, width = ra.shape
     size = rows // n + 8
     return pl.pallas_call(
         functools.partial(join_kernel, bit),
-        in_specs=[VMEM] * 5,
+        in_specs=[VMEM] * 4,
         out_specs=[VMEM] * 2,
         out_shape=[
             sds((n // 2, size, width), F32),
-            sds((n // 2 * size + sums.shape[0], width), F32),
+            sds((n // 2 * size, width), F32),
         ],
         scratch_shapes=[pltpu.VMEM((n, size, width), F32)],
         compiler_params=params(8),
         cost_estimate=cost(rows * width, 8 * rows * width),
         name="join",
-    )(ra, rb, la, lb, sums)
-
-
-def fold_kernel(bit, keep_ref, small_ref, came, next_keep, next_small, message):
+    )(ra, rb, la, lb)
+
+
+def fold_kernel(bit, keep_ref, small_ref, came, *rest):
+    next_keep, next_small, message = rest[-3:]
     parts, size, _ = keep_ref.shape
     write_split(
         bit,
@@ -179,12 +181,13 @@
         next_keep,
         message,
     )
-    small = small_ref[...] + came[parts * size :, :]
+    other = came[parts * size :, :] if len(rest) == 3 else rest[0][...]
+    small = small_ref[...] + other
     next_small[...] = small
     message[parts // 2 * size :, :] = small
 
 
-def fold(bit, keep, small, came):
+def fold(bit, keep, small, *came):
     parts, size, width = keep.shape
     tail = small.shape[0]
     shapes = [
@@ -194,13 +197,13 @@
     ]
     return pl.pallas_call(
         functools.partial(fold_kernel, bit),
-        in_specs=[VMEM] * 3,
+        in_specs=[VMEM] * (2 + len(came)),
         out_specs=[VMEM] * 3,
         out_shape=shapes,
         compiler_params=params(8),
         cost_estimate=cost(parts * size * width, 8 * parts * size * width),
         name="fold",
-    )(keep, small, came)
+    )(keep, small, *came)
 
 
 def close_kernel(keep_ref, small_ref, came, ta_ref, tb_ref, right_ref, left_ref, twiddle_ref, *vectors):
@@ -671,17 +674,21 @@
         n, grad_back, first_mix, normed_b, right, twiddle
     )
     part = B // lax.axis_size("chan")
+    steps = bits(n)
+    right_give, twiddle_rows, _ = lax.optimization_barrier((right_give, twiddle_rows, mix_back))
+    ra, rb = chan_joined(right_keep, right_give)
+    keep, message = join(steps[0], n, ra, rb, la, lb)
+    came = flipped(message, steps[0])
     mixed, scaled, inner, sums = finish(
         n, mix_back, tokens, cotangent, sa, sb, gain, slope, bias, mm, part
     )
-    right_give, twiddle_rows, sums = lax.optimization_barrier((right_give, twiddle_rows, sums))
-    ra, rb = chan_joined(right_keep, right_give)
     ia, ib = chan_terms(inner)
+    sums_came = flipped(sums, steps[0])
     token_grad = token_gradient(tokens, scaled, sa, sb, ia, ib)
-    steps = bits(n)
-    keep, message = join(steps[0], n, ra, rb, la, lb, sums)
-    came = flipped(message, steps[0])
-    for bit in steps[1:]:
+    keep, sums, message = fold(steps[1], keep, sums, came, sums_came)
+    came = flipped(message, steps[1])
+    token_grad, came = lax.optimization_barrier((token_grad, came))
+    for bit in steps[2:]:
         keep, sums, message = fold(bit, keep, sums, came)
         came = flipped(message, bit)
     ta, tb = chan_terms(twiddle_rows)

time: 249 us -> 234 us (0.940)
  starting transfers between devices: 142 us -> 133 us
  waiting for transfers between devices: 58.3 us -> 53.4 us
    ppermute x4 -> x5, waiting for transfers between devices: 14.3 us -> 7.23 us  [flipped(): return lax.ppermute(x, 'seq', [(i, i ^ bit) for i in range(n)])]
    ppermute x60, starting transfers between devices: 131 us -> 125 us  [exchange(): out[k] = lax.ppermute(blocks[k], 'seq', pairs(n, k))]
    ppermute x4 -> x5, starting transfers between devices: 9.37 us -> 7.47 us  [flipped(): return lax.ppermute(x, 'seq', [(i, i ^ bit) for i in range(n)])]
  transfers between devices with their start and end apart: 71 -> 72, of which waited for: 19 -> 20; matrix products, arithmetic and copies ran while one was open for 0% -> 0% of each run, Pallas kernels for 11% -> 15%
where the time goes in v3:
time: 234 us
  starting transfers between devices  133 us (57%)
  waiting for transfers between devices  53.4 us (23%)
  Pallas kernels  40.7 us (17%)
  local copies, waits for them, and re-layouts  3.79 us (2%)
    ppermute x60, starting transfers between devices, exchange(): out[k] = lax.ppermute(blocks[k], 'seq', pairs(n, k))  125 us
    ppermute x60, waiting for transfers between devices, exchange(): out[k] = lax.ppermute(blocks[k], 'seq', pairs(n, k))  42.6 us
    pallas_call x2, Pallas kernels, second_factor(): pl.pallas_call(functools.partial(second_kernel, n, group), in_specs=[VMEM...  8.48 us
    ppermute x5, starting transfers between devices, flipped(): return lax.ppermute(x, 'seq', [(i, i ^ bit) for i in range(n)])  7.47 us
    pallas_call x1, Pallas kernels, finish(): pl.pallas_call(functools.partial(finish_kernel, n), in_specs=[VMEM] * 8 +...  7.43 us
    ppermute x5, waiting for transfers between devices, flipped(): return lax.ppermute(x, 'seq', [(i, i ^ bit) for i in range(n)])  7.23 us
    pallas_call x1, Pallas kernels, left_gradient(): pl.pallas_call(functools.partial(left_kernel, n, group), in_specs=[HBM] *...  5.82 us
    pallas_call x1, Pallas kernels, back_first(): pl.pallas_call(functools.partial(back_kernel, n), in_specs=[VMEM] * 4 + [...  5.72 us
  transfers between devices with their start and end apart: 72, of which 20 were waited for; matrix products, arithmetic and copies ran while one was open for 0% of the time, Pallas kernels for 15%

profile of v3, /device:TPU:0, one launch (start us, length us, event | category | flops | bytes accessed | tf_op | source)
XLA Modules:
  0.0 234.0 jit_solution(11251812684263522081)
XLA Ops:
  32.4 10.3 %collective-permute-start.13 = (bf16[4,32,512]{2,1,0:T(8,128)(2,1)S(1)}, bf16[4,32,512]{2,1,0:T(8,128)(2,1)S(1)}, u32[]{:S(2)}, u32[]{:S(2)}) collective-permute-start(bf16[4,32,512]{2,1,0:T(8,128)(2,1)S(1)} %get-tuple-element.207), channel_id=1, source_target_pairs={{0,22},{2,20},{4,18},{6,16},{8,30},{10,28},{12,26},{14,24},{16,6},... | collective-permute-start | bytes 393224 | tf_op jit(solution)/shard_map/ppermute | solution.py:78
  44.5 3.2 %collective-permute-done.11.rest_9_ = bf16[4,32,512]{2,1,0:T(8,128)(2,1)} collective-permute-done((bf16[4,32,512]{2,1,0:T(8,128)(2,1)S(1)}, bf16[4,32,512]{2,1,0:T(8,128)(2,1)}, u32[]{:S(2)}, u32[]{:S(2)}) %collective-permute-start.11) | collective-permute-done | bytes 131104 | tf_op jit(solution)/shard_map/ppermute | solution.py:78
  50.6 7.5 %collective-permute-start.16 = (bf16[4,32,512]{2,1,0:T(8,128)(2,1)S(1)}, bf16[4,32,512]{2,1,0:T(8,128)(2,1)S(1)}, u32[]{:S(2)}, u32[]{:S(2)}) collective-permute-start(bf16[4,32,512]{2,1,0:T(8,128)(2,1)S(1)} %get-tuple-element.210), channel_id=1, source_target_pairs={{0,28},{2,30},{4,24},{6,26},{8,4},{10,6},{12,0},{14,2},{16,12},{18... | collective-permute-start | bytes 393224 | tf_op jit(solution)/shard_map/ppermute | solution.py:78
  71.3 7.5 %collective-permute-done.19.rest_24_.rest_8_ = bf16[4,32,512]{2,1,0:T(8,128)(2,1)S(1)} collective-permute-done((bf16[4,32,512]{2,1,0:T(8,128)(2,1)S(1)}, bf16[4,32,512]{2,1,0:T(8,128)(2,1)S(1)}, u32[]{:S(2)}, u32[]{:S(2)}) %collective-permute-start.19) | collective-permute-done | bytes 131104 | tf_op jit(solution)/shard_map/ppermute | solution.py:78
  78.9 4.7 %collective-permute-start.25 = (bf16[4,32,512]{2,1,0:T(8,128)(2,1)S(1)}, bf16[4,32,512]{2,1,0:T(8,128)(2,1)S(1)}, u32[]{:S(2)}, u32[]{:S(2)}) collective-permute-start(bf16[4,32,512]{2,1,0:T(8,128)(2,1)S(1)} %get-tuple-element.219), channel_id=1, source_target_pairs={{0,26},{2,24},{4,30},{6,28},{8,2},{10,0},{12,6},{14,4},{16,10},{18... | collective-permute-start | bytes 393224 | tf_op jit(solution)/shard_map/ppermute | solution.py:78
  83.6 2.9 %collective-permute-start.26 = (bf16[4,32,512]{2,1,0:T(8,128)(2,1)S(1)}, bf16[4,32,512]{2,1,0:T(8,128)(2,1)S(1)}, u32[]{:S(2)}, u32[]{:S(2)}) collective-permute-start(bf16[4,32,512]{2,1,0:T(8,128)(2,1)S(1)} %get-tuple-element.240), channel_id=1, source_target_pairs={{0,6},{2,4},{4,2},{6,0},{8,14},{10,12},{12,10},{14,8},{16,22},{18,... | collective-permute-start | bytes 393224 | tf_op jit(solution)/shard_map/ppermute | solution.py:78
  86.5 3.1 %collective-permute-done.23.rest_25_.rest_9_ = bf16[4,32,512]{2,1,0:T(8,128)(2,1)S(1)} collective-permute-done((bf16[4,32,512]{2,1,0:T(8,128)(2,1)S(1)}, bf16[4,32,512]{2,1,0:T(8,128)(2,1)S(1)}, u32[]{:S(2)}, u32[]{:S(2)}) %collective-permute-start.23) | collective-permute-done | bytes 131104 | tf_op jit(solution)/shard_map/ppermute | solution.py:78
  91.3 6.9 %collective-permute-start.30 = (bf16[4,32,512]{2,1,0:T(8,128)(2,1)S(1)}, bf16[4,32,512]{2,1,0:T(8,128)(2,1)S(1)}, u32[]{:S(2)}, u32[]{:S(2)}) collective-permute-start(bf16[4,32,512]{2,1,0:T(8,128)(2,1)S(1)} %get-tuple-element.248), channel_id=1, source_target_pairs={{0,22},{2,20},{4,18},{6,16},{8,30},{10,28},{12,26},{14,24},{16,6},... | collective-permute-start | bytes 393224 | tf_op jit(solution)/shard_map/ppermute | solution.py:78
  98.2 6.6 %collective-permute-start.31 = (bf16[4,32,512]{2,1,0:T(8,128)(2,1)S(1)}, bf16[4,32,512]{2,1,0:T(8,128)(2,1)S(1)}, u32[]{:S(2)}, u32[]{:S(2)}) collective-permute-start(bf16[4,32,512]{2,1,0:T(8,128)(2,1)S(1)} %get-tuple-element.251), channel_id=1, source_target_pairs={{0,28},{2,30},{4,24},{6,26},{8,4},{10,6},{12,0},{14,2},{16,12},{18... | collective-permute-start | bytes 393224 | tf_op jit(solution)/shard_map/ppermute | solution.py:78
  107.8 4.2 %spread_grad.1 = (bf16[4,32,512]{2,1,0:T(8,128)(2,1)S(1)}, bf16[4,32,512]{2,1,0:T(8,128)(2,1)S(1)}, bf16[4,32,512]{2,1,0:T(8,128)(2,1)S(1)}, bf16[4,32,512]{2,1,...) custom-call(bf16[1024,1024]{1,0:T(8,128)(2,1)S(1)} %get-tuple-elemen, ...), custom_call_target="tpu_custom_call" | custom-call | flops 2147483 | bytes 8388 | tf_op jit(solution)/shard_map/spread_grad/pallas_call | solution.py:448
  120.2 6.3 %collective-permute-done.34.rest_8_ = bf16[4,32,512]{2,1,0:T(8,128)(2,1)S(1)} collective-permute-done((bf16[4,32,512]{2,1,0:T(8,128)(2,1)S(1)}, bf16[4,32,512]{2,1,0:T(8,128)(2,1)S(1)}, u32[]{:S(2)}, u32[]{:S(2)}) %collective-permute-start.34) | collective-permute-done | bytes 131104 | tf_op jit(solution)/shard_map/ppermute | solution.py:78
  126.5 4.7 %collective-permute-start.40 = (bf16[4,32,512]{2,1,0:T(8,128)(2,1)S(1)}, bf16[4,32,512]{2,1,0:T(8,128)(2,1)S(1)}, u32[]{:S(2)}, u32[]{:S(2)}) collective-permute-start(bf16[4,32,512]{2,1,0:T(8,128)(2,1)S(1)} %get-tuple-element.260), channel_id=1, source_target_pairs={{0,26},{2,24},{4,30},{6,28},{8,2},{10,0},{12,6},{14,4},{16,10},{18... | collective-permute-start | bytes 393224 | tf_op jit(solution)/shard_map/ppermute | solution.py:78
  131.2 3.1 %collective-permute-start.42 = (bf16[4,32,512]{2,1,0:T(8,128)(2,1)S(1)}, bf16[4,32,512]{2,1,0:T(8,128)(2,1)S(1)}, u32[]{:S(2)}, u32[]{:S(2)}) collective-permute-start(bf16[4,32,512]{2,1,0:T(8,128)(2,1)S(1)} %get-tuple-element.266), channel_id=1, source_target_pairs={{0,12},{2,14},{4,8},{6,10},{8,20},{10,22},{12,16},{14,18},{16,28},... | collective-permute-start | bytes 393224 | tf_op jit(solution)/shard_map/ppermute | solution.py:78
  136.5 3.6 %collective-permute-start.44 = (bf16[4,32,512]{2,1,0:T(8,128)(2,1)S(1)}, bf16[4,32,512]{2,1,0:T(8,128)(2,1)S(1)}, u32[]{:S(2)}, u32[]{:S(2)}) collective-permute-start(bf16[4,32,512]{2,1,0:T(8,128)(2,1)S(1)} %get-tuple-element.270), channel_id=1, source_target_pairs={{0,20},{2,22},{4,16},{6,18},{8,28},{10,30},{12,24},{14,26},{16,4},... | collective-permute-start | bytes 393224 | tf_op jit(solution)/shard_map/ppermute | solution.py:78
  140.1 5.4 %collective-permute-start.45 = (bf16[4,32,512]{2,1,0:T(8,128)(2,1)S(1)}, bf16[4,32,512]{2,1,0:T(8,128)(2,1)S(1)}, u32[]{:S(2)}, u32[]{:S(2)}) collective-permute-start(bf16[4,32,512]{2,1,0:T(8,128)(2,1)S(1)} %get-tuple-element.271), channel_id=1, source_target_pairs={{0,22},{2,20},{4,18},{6,16},{8,30},{10,28},{12,26},{14,24},{16,6},... | collective-permute-start | bytes 393224 | tf_op jit(solution)/shard_map/ppermute | solution.py:78
  145.5 4.2 %collective-permute-start.46 = (bf16[4,32,512]{2,1,0:T(8,128)(2,1)S(1)}, bf16[4,32,512]{2,1,0:T(8,128)(2,1)S(1)}, u32[]{:S(2)}, u32[]{:S(2)}) collective-permute-start(bf16[4,32,512]{2,1,0:T(8,128)(2,1)S(1)} %get-tuple-element.274), channel_id=1, source_target_pairs={{0,28},{2,30},{4,24},{6,26},{8,4},{10,6},{12,0},{14,2},{16,12},{18... | collective-permute-start | bytes 393224 | tf_op jit(solution)/shard_map/ppermute | solution.py:78
  149.7 3.0 %collective-permute-start.47 = (bf16[4,32,512]{2,1,0:T(8,128)(2,1)S(1)}, bf16[4,32,512]{2,1,0:T(8,128)(2,1)S(1)}, u32[]{:S(2)}, u32[]{:S(2)}) collective-permute-start(bf16[4,32,512]{2,1,0:T(8,128)(2,1)S(1)} %get-tuple-element.275), channel_id=1, source_target_pairs={{0,30},{2,28},{4,26},{6,24},{8,6},{10,4},{12,2},{14,0},{16,14},{18... | collective-permute-start | bytes 393224 | tf_op jit(solution)/shard_map/ppermute | solution.py:78
  152.7 5.8 %left_gradient.1 = (f32[64,32]{1,0:T(8,128)S(1)}, f32[64,32]{1,0:T(8,128)S(1)}) custom-call(bf16[4,32,512]{2,1,0:T(8,128)(2,1)} %copy-done.4, bf16[4,32,512]{2,1,0:T(8,128)(2,1)} %copy-done.12, bf16[4,32,512]{2,1,0:T(8,128)(2,1)} %copy-done.13, bf16[4,32,512]{2,1,0:T(8,128)(2,1)} %copy-done.14, bf16[4,32,512]{2,1,0:T(8,128)(2,1)} %copy-done.15, ...), custom_call_target="tpu_custom_call" | custom-call | flops 2147483 | bytes 8388 | tf_op jit(solution)/shard_map/left_gradient/pallas_call | solution.py:516
  158.6 4.2 %second_mix.1 = (bf16[4,32,512]{2,1,0:T(8,128)(2,1)S(1)}, bf16[4,32,512]{2,1,0:T(8,128)(2,1)S(1)}, bf16[4,32,512]{2,1,0:T(8,128)(2,1)S(1)}, bf16[4,32,512]{2,1,0...) custom-call(bf16[1024,1024]{1,0:T(8,128)(2,1)S(1)} %get-tuple-elemen, ...), custom_call_target="tpu_custom_call" | custom-call | flops 2147483 | bytes 8388 | tf_op jit(solution)/shard_map/second_mix/pallas_call | solution.py:448
  171.3 9.3 %collective-permute-done.49.rest_8_ = bf16[4,32,512]{2,1,0:T(8,128)(2,1)S(1)} collective-permute-done((bf16[4,32,512]{2,1,0:T(8,128)(2,1)S(1)}, bf16[4,32,512]{2,1,0:T(8,128)(2,1)S(1)}, u32[]{:S(2)}, u32[]{:S(2)}) %collective-permute-start.49) | collective-permute-done | bytes 131104 | tf_op jit(solution)/shard_map/ppermute | solution.py:78
  180.7 5.1 %collective-permute-start.56 = (bf16[4,32,512]{2,1,0:T(8,128)(2,1)S(1)}, bf16[4,32,512]{2,1,0:T(8,128)(2,1)S(1)}, u32[]{:S(2)}, u32[]{:S(2)}) collective-permute-start(bf16[4,32,512]{2,1,0:T(8,128)(2,1)S(1)} %get-tuple-element.339), channel_id=1, source_target_pairs={{0,12},{2,14},{4,8},{6,10},{8,20},{10,22},{12,16},{14,18},{16,28},... | collective-permute-start | bytes 393224 | tf_op jit(solution)/shard_map/ppermute | solution.py:78
  198.7 5.7 %back_first.1 = (f32[4,8,512]{2,1,0:T(8,128)S(1)}, f32[4,512,512]{2,1,0:T(8,128)S(1)}, f32[512,256]{1,0:T(8,128)S(1)}, f32[512,256]{1,0:T(8,128)S(1)}) custom-call(f32[4,512,512]{2,1,0:T(8,128)S(1)} %get-tuple-element.194.first_ref, bf16[4,512,512]{2,1,0:T(8,128)(2,1)S(1)} %get-tuple-element.193.nb_ref, bf16[512,512]{1,0:T(8,128)(2,1)S(1)} %pad_maximum_fusion.right_ref, ...), custom_call_target="tpu_custom_call" | custom-call | flops 2147483 | bytes 12582 | tf_op jit(solution)/shard_map/back_first/pallas_call | solution.py:562
  207.0 7.4 %finish.1 = (bf16[2048,512]{1,0:T(8,128)(2,1)}, f32[2048,512]{1,0:T(8,128)S(1)}, f32[8,2048]{1,0:T(8,128)S(1)}, f32[8,256]{1,0:T(8,128)S(1)}) custom-call(bf16[2048,512]{1,0:T(8,128)(2,1)S(1)} %copy-done.1, bf16[2048,512]{1,0:T(8,128)(2,1)S(1)} %copy-done.3, f32[8,2048]{1,0:T(8,128)S(1)} %squares.1.sa_ref, f32[8,2048]{1,0:T(8,128)S(1)} %collective-permute-done.sb_ref, ...), custom_call_target="tpu_custom_call" | custom-call | flops 41943 | bytes 16777 | tf_op jit(solution)/shard_map/finish/pallas_call | solution.py:614
  220.2 3.0 %token_gradient.1 = bf16[2048,512]{1,0:T(8,128)(2,1)} custom-call(bf16[2048,512]{1,0:T(8,128)(2,1)S(1)} %copy-done.1, f32[2048,512]{1,0:T(8,128)S(1)} %get-tuple-element.350.scaled_ref, f32[8,2048]{1,0:T(8,128)S(1)} %squares.1.sa_ref, f32[8,2048]{1,0:T(8,128)S(1)} %collective-permute-done.sb_ref, f32[8,2048]{1,0:T(8,128)S(1)} %get-tuple-element.351.ia_ref, ...), custom_call_target="tpu_custom_call" | custom-call | flops 5242 | bytes 8388 | tf_op jit(solution)/shard_map/token_gradient/pallas_call | solution.py:638
  (277 shorter events, 104.7 us)
Async XLA Ops:
  20.4 37.7 %collective-permute-start.1 = (bf16[256,512]{1,0:T(8,128)(2,1)}, bf16[256,512]{1,0:T(8,128)(2,1)}, u32[]{:S(2)}, u32[]{:S(2)}) collective-permute-start(bf16[256,512]{1,0:T(8,128)(2,1)} %param.13), channel_id=1, source_target_pairs={{0,1},{1,0},{2,3},{3,2},{4,5},{5,4},{6,7},{7,6},{8,9},{9,8},{10,11... | collective-permute-start | bytes 786440 | tf_op jit(solution)/shard_map/ppermute | solution.py:106
  22.4 20.2 %collective-permute-start.10 = (bf16[4,32,512]{2,1,0:T(8,128)(2,1)S(1)}, bf16[4,32,512]{2,1,0:T(8,128)(2,1)}, u32[]{:S(2)}, u32[]{:S(2)}) collective-permute-start(bf16[4,32,512]{2,1,0:T(8,128)(2,1)S(1)} %get-tuple-element.204), channel_id=1, source_target_pairs={{0,16},{2,18},{4,20},{6,22},{8,24},{10,26},{12,28},{14,30},{16,0},... | collective-permute-start | bytes 393224 | tf_op jit(solution)/shard_map/ppermute | solution.py:78
  25.6 22.1 %collective-permute-start.11 = (bf16[4,32,512]{2,1,0:T(8,128)(2,1)S(1)}, bf16[4,32,512]{2,1,0:T(8,128)(2,1)}, u32[]{:S(2)}, u32[]{:S(2)}) collective-permute-start(bf16[4,32,512]{2,1,0:T(8,128)(2,1)S(1)} %get-tuple-element.205), channel_id=1, source_target_pairs={{0,18},{2,16},{4,22},{6,20},{8,26},{10,24},{12,30},{14,28},{16,2},... | collective-permute-start | bytes 393224 | tf_op jit(solution)/shard_map/ppermute | solution.py:78
  28.5 22.0 %collective-permute-start.12 = (bf16[4,32,512]{2,1,0:T(8,128)(2,1)S(1)}, bf16[4,32,512]{2,1,0:T(8,128)(2,1)}, u32[]{:S(2)}, u32[]{:S(2)}) collective-permute-start(bf16[4,32,512]{2,1,0:T(8,128)(2,1)S(1)} %get-tuple-element.206), channel_id=1, source_target_pairs={{0,20},{2,22},{4,16},{6,18},{8,28},{10,30},{12,24},{14,26},{16,4},... | collective-permute-start | bytes 393224 | tf_op jit(solution)/shard_map/ppermute | solution.py:78
  32.4 30.9 %collective-permute-start.13 = (bf16[4,32,512]{2,1,0:T(8,128)(2,1)S(1)}, bf16[4,32,512]{2,1,0:T(8,128)(2,1)S(1)}, u32[]{:S(2)}, u32[]{:S(2)}) collective-permute-start(bf16[4,32,512]{2,1,0:T(8,128)(2,1)S(1)} %get-tuple-element.207), channel_id=1, source_target_pairs={{0,22},{2,20},{4,18},{6,16},{8,30},{10,28},{12,26},{14,24},{16,6},... | collective-permute-start | bytes 393224 | tf_op jit(solution)/shard_map/ppermute | solution.py:78
  42.6 21.3 %collective-permute-start.14 = (bf16[4,32,512]{2,1,0:T(8,128)(2,1)S(1)}, bf16[4,32,512]{2,1,0:T(8,128)(2,1)S(1)}, u32[]{:S(2)}, u32[]{:S(2)}) collective-permute-start(bf16[4,32,512]{2,1,0:T(8,128)(2,1)S(1)} %get-tuple-element.208), channel_id=1, source_target_pairs={{0,24},{2,26},{4,28},{6,30},{8,0},{10,2},{12,4},{14,6},{16,8},{18,... | collective-permute-start | bytes 393224 | tf_op jit(solution)/shard_map/ppermute | solution.py:78
  66.6 17.0 %collective-permute-start.21 = (bf16[4,32,512]{2,1,0:T(8,128)(2,1)S(1)}, bf16[4,32,512]{2,1,0:T(8,128)(2,1)S(1)}, u32[]{:S(2)}, u32[]{:S(2)}) collective-permute-start(bf16[4,32,512]{2,1,0:T(8,128)(2,1)S(1)} %get-tuple-element.215), channel_id=1, source_target_pairs={{0,24},{2,26},{4,28},{6,30},{8,0},{10,2},{12,4},{14,6},{16,8},{18,... | collective-permute-start | bytes 393224 | tf_op jit(solution)/shard_map/ppermute | solution.py:78
  69.0 17.5 %collective-permute-start.22 = (bf16[4,32,512]{2,1,0:T(8,128)(2,1)S(1)}, bf16[4,32,512]{2,1,0:T(8,128)(2,1)S(1)}, u32[]{:S(2)}, u32[]{:S(2)}) collective-permute-start(bf16[4,32,512]{2,1,0:T(8,128)(2,1)S(1)} %get-tuple-element.216), channel_id=1, source_target_pairs={{0,4},{2,6},{4,0},{6,2},{8,12},{10,14},{12,8},{14,10},{16,20},{18,... | collective-permute-start | bytes 393224 | tf_op jit(solution)/shard_map/ppermute | solution.py:78
  69.5 20.1 %collective-permute-start.23 = (bf16[4,32,512]{2,1,0:T(8,128)(2,1)S(1)}, bf16[4,32,512]{2,1,0:T(8,128)(2,1)S(1)}, u32[]{:S(2)}, u32[]{:S(2)}) collective-permute-start(bf16[4,32,512]{2,1,0:T(8,128)(2,1)S(1)} %get-tuple-element.217), channel_id=1, source_target_pairs={{0,18},{2,16},{4,22},{6,20},{8,26},{10,24},{12,30},{14,28},{16,2},... | collective-permute-start | bytes 393224 | tf_op jit(solution)/shard_map/ppermute | solution.py:78
  86.5 18.3 %collective-permute-start.27 = (bf16[4,32,512]{2,1,0:T(8,128)(2,1)S(1)}, bf16[4,32,512]{2,1,0:T(8,128)(2,1)S(1)}, u32[]{:S(2)}, u32[]{:S(2)}) collective-permute-start(bf16[4,32,512]{2,1,0:T(8,128)(2,1)S(1)} %get-tuple-element.243), channel_id=1, source_target_pairs={{0,12},{2,14},{4,8},{6,10},{8,20},{10,22},{12,16},{14,18},{16,28},... | collective-permute-start | bytes 393224 | tf_op jit(solution)/shard_map/ppermute | solution.py:78
  89.6 22.6 %collective-permute-start.28 = (bf16[4,32,512]{2,1,0:T(8,128)(2,1)S(1)}, bf16[4,32,512]{2,1,0:T(8,128)(2,1)S(1)}, u32[]{:S(2)}, u32[]{:S(2)}) collective-permute-start(bf16[4,32,512]{2,1,0:T(8,128)(2,1)S(1)} %get-tuple-element.244), channel_id=1, source_target_pairs={{0,14},{2,12},{4,10},{6,8},{8,22},{10,20},{12,18},{14,16},{16,30},... | collective-permute-start | bytes 393224 | tf_op jit(solution)/shard_map/ppermute | solution.py:78
  89.6 24.0 %collective-permute-start.29 = (bf16[4,32,512]{2,1,0:T(8,128)(2,1)S(1)}, bf16[4,32,512]{2,1,0:T(8,128)(2,1)S(1)}, u32[]{:S(2)}, u32[]{:S(2)}) collective-permute-start(bf16[4,32,512]{2,1,0:T(8,128)(2,1)S(1)} %get-tuple-element.247), channel_id=1, source_target_pairs={{0,20},{2,22},{4,16},{6,18},{8,28},{10,30},{12,24},{14,26},{16,4},... | collective-permute-start | bytes 393224 | tf_op jit(solution)/shard_map/ppermute | solution.py:78
  91.3 22.3 %collective-permute-start.30 = (bf16[4,32,512]{2,1,0:T(8,128)(2,1)S(1)}, bf16[4,32,512]{2,1,0:T(8,128)(2,1)S(1)}, u32[]{:S(2)}, u32[]{:S(2)}) collective-permute-start(bf16[4,32,512]{2,1,0:T(8,128)(2,1)S(1)} %get-tuple-element.248), channel_id=1, source_target_pairs={{0,22},{2,20},{4,18},{6,16},{8,30},{10,28},{12,26},{14,24},{16,6},... | collective-permute-start | bytes 393224 | tf_op jit(solution)/shard_map/ppermute | solution.py:78
  119.4 17.0 %collective-permute-start.38 = (bf16[4,32,512]{2,1,0:T(8,128)(2,1)S(1)}, bf16[4,32,512]{2,1,0:T(8,128)(2,1)S(1)}, u32[]{:S(2)}, u32[]{:S(2)}) collective-permute-start(bf16[4,32,512]{2,1,0:T(8,128)(2,1)S(1)} %get-tuple-element.258), channel_id=1, source_target_pairs={{0,18},{2,16},{4,22},{6,20},{8,26},{10,24},{12,30},{14,28},{16,2},... | collective-permute-start | bytes 393224 | tf_op jit(solution)/shard_map/ppermute | solution.py:78
  131.2 18.5 %collective-permute-start.42 = (bf16[4,32,512]{2,1,0:T(8,128)(2,1)S(1)}, bf16[4,32,512]{2,1,0:T(8,128)(2,1)S(1)}, u32[]{:S(2)}, u32[]{:S(2)}) collective-permute-start(bf16[4,32,512]{2,1,0:T(8,128)(2,1)S(1)} %get-tuple-element.266), channel_id=1, source_target_pairs={{0,12},{2,14},{4,8},{6,10},{8,20},{10,22},{12,16},{14,18},{16,28},... | collective-permute-start | bytes 393224 | tf_op jit(solution)/shard_map/ppermute | solution.py:78
  136.4 27.1 %collective-permute-start.43 = (bf16[4,32,512]{2,1,0:T(8,128)(2,1)S(1)}, bf16[4,32,512]{2,1,0:T(8,128)(2,1)S(1)}, u32[]{:S(2)}, u32[]{:S(2)}) collective-permute-start(bf16[4,32,512]{2,1,0:T(8,128)(2,1)S(1)} %get-tuple-element.267), channel_id=1, source_target_pairs={{0,14},{2,12},{4,10},{6,8},{8,22},{10,20},{12,18},{14,16},{16,30},... | collective-permute-start | bytes 393224 | tf_op jit(solution)/shard_map/ppermute | solution.py:78
  136.5 27.4 %collective-permute-start.44 = (bf16[4,32,512]{2,1,0:T(8,128)(2,1)S(1)}, bf16[4,32,512]{2,1,0:T(8,128)(2,1)S(1)}, u32[]{:S(2)}, u32[]{:S(2)}) collective-permute-start(bf16[4,32,512]{2,1,0:T(8,128)(2,1)S(1)} %get-tuple-element.270), channel_id=1, source_target_pairs={{0,20},{2,22},{4,16},{6,18},{8,28},{10,30},{12,24},{14,26},{16,4},... | collective-permute-start | bytes 393224 | tf_op jit(solution)/shard_map/ppermute | solution.py:78
  140.1 23.8 %collective-permute-start.45 = (bf16[4,32,512]{2,1,0:T(8,128)(2,1)S(1)}, bf16[4,32,512]{2,1,0:T(8,128)(2,1)S(1)}, u32[]{:S(2)}, u32[]{:S(2)}) collective-permute-start(bf16[4,32,512]{2,1,0:T(8,128)(2,1)S(1)} %get-tuple-element.271), channel_id=1, source_target_pairs={{0,22},{2,20},{4,18},{6,16},{8,30},{10,28},{12,26},{14,24},{16,6},... | collective-permute-start | bytes 393224 | tf_op jit(solution)/shard_map/ppermute | solution.py:78
  145.5 19.6 %collective-permute-start.46 = (bf16[4,32,512]{2,1,0:T(8,128)(2,1)S(1)}, bf16[4,32,512]{2,1,0:T(8,128)(2,1)S(1)}, u32[]{:S(2)}, u32[]{:S(2)}) collective-permute-start(bf16[4,32,512]{2,1,0:T(8,128)(2,1)S(1)} %get-tuple-element.274), channel_id=1, source_target_pairs={{0,28},{2,30},{4,24},{6,26},{8,4},{10,6},{12,0},{14,2},{16,12},{18... | collective-permute-start | bytes 393224 | tf_op jit(solution)/shard_map/ppermute | solution.py:78
  149.7 18.1 %collective-permute-start.47 = (bf16[4,32,512]{2,1,0:T(8,128)(2,1)S(1)}, bf16[4,32,512]{2,1,0:T(8,128)(2,1)S(1)}, u32[]{:S(2)}, u32[]{:S(2)}) collective-permute-start(bf16[4,32,512]{2,1,0:T(8,128)(2,1)S(1)} %get-tuple-element.275), channel_id=1, source_target_pairs={{0,30},{2,28},{4,26},{6,24},{8,6},{10,4},{12,2},{14,0},{16,14},{18... | collective-permute-start | bytes 393224 | tf_op jit(solution)/shard_map/ppermute | solution.py:78
  163.9 16.7 %collective-permute-start.49 = (bf16[4,32,512]{2,1,0:T(8,128)(2,1)S(1)}, bf16[4,32,512]{2,1,0:T(8,128)(2,1)S(1)}, u32[]{:S(2)}, u32[]{:S(2)}) collective-permute-start(bf16[4,32,512]{2,1,0:T(8,128)(2,1)S(1)} %get-tuple-element.311), channel_id=1, source_target_pairs={{0,16},{2,18},{4,20},{6,22},{8,24},{10,26},{12,28},{14,30},{16,0},... | collective-permute-start | bytes 393224 | tf_op jit(solution)/shard_map/ppermute | solution.py:78
  163.9 16.7 %collective-permute-start.50 = (bf16[4,32,512]{2,1,0:T(8,128)(2,1)S(1)}, bf16[4,32,512]{2,1,0:T(8,128)(2,1)S(1)}, u32[]{:S(2)}, u32[]{:S(2)}) collective-permute-start(bf16[4,32,512]{2,1,0:T(8,128)(2,1)S(1)} %get-tuple-element.312), channel_id=1, source_target_pairs={{0,8},{2,10},{4,12},{6,14},{8,16},{10,18},{12,20},{14,22},{16,24},... | collective-permute-start | bytes 393224 | tf_op jit(solution)/shard_map/ppermute | solution.py:78
  167.8 18.0 %collective-permute-start.52 = (bf16[4,32,512]{2,1,0:T(8,128)(2,1)S(1)}, bf16[4,32,512]{2,1,0:T(8,128)(2,1)S(1)}, u32[]{:S(2)}, u32[]{:S(2)}) collective-permute-start(bf16[4,32,512]{2,1,0:T(8,128)(2,1)S(1)} %get-tuple-element.314), channel_id=1, source_target_pairs={{0,4},{2,6},{4,0},{6,2},{8,12},{10,14},{12,8},{14,10},{16,20},{18,... | collective-permute-start | bytes 393224 | tf_op jit(solution)/shard_map/ppermute | solution.py:78
  186.3 18.3 %collective-permute-start.58 = (bf16[4,32,512]{2,1,0:T(8,128)(2,1)S(1)}, bf16[4,32,512]{2,1,0:T(8,128)(2,1)S(1)}, u32[]{:S(2)}, u32[]{:S(2)}) collective-permute-start(bf16[4,32,512]{2,1,0:T(8,128)(2,1)S(1)} %get-tuple-element.343), channel_id=1, source_target_pairs={{0,20},{2,22},{4,16},{6,18},{8,28},{10,30},{12,24},{14,26},{16,4},... | collective-permute-start | bytes 393224 | tf_op jit(solution)/shard_map/ppermute | solution.py:78
  (117 other events, 1935.3 us)

commit v4 on v3

--- a/solution.py
+++ b/solution.py
@@ -60,7 +60,7 @@
 
 def send_order(n):
     if n == 16:
-        return [1, 8, 4, 12, 2, 9, 5, 13, 3, 10, 6, 14, 11, 7, 15]
+        return [1, 8, 4, 12, 2, 9, 5, 13, 3, 10, 6, 14, 7, 11, 15]
     high = n // 4
     far_first = sorted(range(1, high), key=lambda d: (abs(d - high / 2), d))
     order = []

time: 234 us -> 234 us (level)
  no operation moved by 1% of the time
where the time goes in v4:
time: 234 us
  starting transfers between devices  133 us (57%)
  waiting for transfers between devices  53.4 us (23%)
  Pallas kernels  40.7 us (17%)
  local copies, waits for them, and re-layouts  3.79 us (2%)
    ppermute x60, starting transfers between devices, exchange(): out[k] = lax.ppermute(blocks[k], 'seq', pairs(n, k))  125 us
    ppermute x60, waiting for transfers between devices, exchange(): out[k] = lax.ppermute(blocks[k], 'seq', pairs(n, k))  42.6 us
    pallas_call x2, Pallas kernels, second_factor(): pl.pallas_call(functools.partial(second_kernel, n, group), in_specs=[VMEM...  8.48 us
    ppermute x5, starting transfers between devices, flipped(): return lax.ppermute(x, 'seq', [(i, i ^ bit) for i in range(n)])  7.47 us
    pallas_call x1, Pallas kernels, finish(): pl.pallas_call(functools.partial(finish_kernel, n), in_specs=[VMEM] * 8 +...  7.43 us
    ppermute x5, waiting for transfers between devices, flipped(): return lax.ppermute(x, 'seq', [(i, i ^ bit) for i in range(n)])  7.23 us
    pallas_call x1, Pallas kernels, left_gradient(): pl.pallas_call(functools.partial(left_kernel, n, group), in_specs=[HBM] *...  5.82 us
    pallas_call x1, Pallas kernels, back_first(): pl.pallas_call(functools.partial(back_kernel, n), in_specs=[VMEM] * 4 + [...  5.72 us
  transfers between devices with their start and end apart: 72, of which 20 were waited for; matrix products, arithmetic and copies ran while one was open for 0% of the time, Pallas kernels for 15%

profile of v4, /device:TPU:0, one launch (start us, length us, event | category | flops | bytes accessed | tf_op | source)
XLA Modules:
  0.0 234.0 jit_solution(11251812684263522081)
XLA Ops:
  32.4 10.3 %collective-permute-start.13 = (bf16[4,32,512]{2,1,0:T(8,128)(2,1)S(1)}, bf16[4,32,512]{2,1,0:T(8,128)(2,1)S(1)}, u32[]{:S(2)}, u32[]{:S(2)}) collective-permute-start(bf16[4,32,512]{2,1,0:T(8,128)(2,1)S(1)} %get-tuple-element.207), channel_id=1, source_target_pairs={{0,22},{2,20},{4,18},{6,16},{8,30},{10,28},{12,26},{14,24},{16,6},... | collective-permute-start | bytes 393224 | tf_op jit(solution)/shard_map/ppermute | solution.py:78
  44.5 3.2 %collective-permute-done.11.rest_9_ = bf16[4,32,512]{2,1,0:T(8,128)(2,1)} collective-permute-done((bf16[4,32,512]{2,1,0:T(8,128)(2,1)S(1)}, bf16[4,32,512]{2,1,0:T(8,128)(2,1)}, u32[]{:S(2)}, u32[]{:S(2)}) %collective-permute-start.11) | collective-permute-done | bytes 131104 | tf_op jit(solution)/shard_map/ppermute | solution.py:78
  50.6 7.5 %collective-permute-start.16 = (bf16[4,32,512]{2,1,0:T(8,128)(2,1)S(1)}, bf16[4,32,512]{2,1,0:T(8,128)(2,1)S(1)}, u32[]{:S(2)}, u32[]{:S(2)}) collective-permute-start(bf16[4,32,512]{2,1,0:T(8,128)(2,1)S(1)} %get-tuple-element.210), channel_id=1, source_target_pairs={{0,28},{2,30},{4,24},{6,26},{8,4},{10,6},{12,0},{14,2},{16,12},{18... | collective-permute-start | bytes 393224 | tf_op jit(solution)/shard_map/ppermute | solution.py:78
  71.3 7.5 %collective-permute-done.19.rest_24_.rest_8_ = bf16[4,32,512]{2,1,0:T(8,128)(2,1)S(1)} collective-permute-done((bf16[4,32,512]{2,1,0:T(8,128)(2,1)S(1)}, bf16[4,32,512]{2,1,0:T(8,128)(2,1)S(1)}, u32[]{:S(2)}, u32[]{:S(2)}) %collective-permute-start.19) | collective-permute-done | bytes 131104 | tf_op jit(solution)/shard_map/ppermute | solution.py:78
  78.9 4.7 %collective-permute-start.25 = (bf16[4,32,512]{2,1,0:T(8,128)(2,1)S(1)}, bf16[4,32,512]{2,1,0:T(8,128)(2,1)S(1)}, u32[]{:S(2)}, u32[]{:S(2)}) collective-permute-start(bf16[4,32,512]{2,1,0:T(8,128)(2,1)S(1)} %get-tuple-element.219), channel_id=1, source_target_pairs={{0,26},{2,24},{4,30},{6,28},{8,2},{10,0},{12,6},{14,4},{16,10},{18... | collective-permute-start | bytes 393224 | tf_op jit(solution)/shard_map/ppermute | solution.py:78
  83.6 2.9 %collective-permute-start.26 = (bf16[4,32,512]{2,1,0:T(8,128)(2,1)S(1)}, bf16[4,32,512]{2,1,0:T(8,128)(2,1)S(1)}, u32[]{:S(2)}, u32[]{:S(2)}) collective-permute-start(bf16[4,32,512]{2,1,0:T(8,128)(2,1)S(1)} %get-tuple-element.240), channel_id=1, source_target_pairs={{0,6},{2,4},{4,2},{6,0},{8,14},{10,12},{12,10},{14,8},{16,22},{18,... | collective-permute-start | bytes 393224 | tf_op jit(solution)/shard_map/ppermute | solution.py:78
  86.5 3.1 %collective-permute-done.23.rest_25_.rest_9_ = bf16[4,32,512]{2,1,0:T(8,128)(2,1)S(1)} collective-permute-done((bf16[4,32,512]{2,1,0:T(8,128)(2,1)S(1)}, bf16[4,32,512]{2,1,0:T(8,128)(2,1)S(1)}, u32[]{:S(2)}, u32[]{:S(2)}) %collective-permute-start.23) | collective-permute-done | bytes 131104 | tf_op jit(solution)/shard_map/ppermute | solution.py:78
  91.3 6.9 %collective-permute-start.30 = (bf16[4,32,512]{2,1,0:T(8,128)(2,1)S(1)}, bf16[4,32,512]{2,1,0:T(8,128)(2,1)S(1)}, u32[]{:S(2)}, u32[]{:S(2)}) collective-permute-start(bf16[4,32,512]{2,1,0:T(8,128)(2,1)S(1)} %get-tuple-element.248), channel_id=1, source_target_pairs={{0,22},{2,20},{4,18},{6,16},{8,30},{10,28},{12,26},{14,24},{16,6},... | collective-permute-start | bytes 393224 | tf_op jit(solution)/shard_map/ppermute | solution.py:78
  98.2 6.6 %collective-permute-start.31 = (bf16[4,32,512]{2,1,0:T(8,128)(2,1)S(1)}, bf16[4,32,512]{2,1,0:T(8,128)(2,1)S(1)}, u32[]{:S(2)}, u32[]{:S(2)}) collective-permute-start(bf16[4,32,512]{2,1,0:T(8,128)(2,1)S(1)} %get-tuple-element.251), channel_id=1, source_target_pairs={{0,28},{2,30},{4,24},{6,26},{8,4},{10,6},{12,0},{14,2},{16,12},{18... | collective-permute-start | bytes 393224 | tf_op jit(solution)/shard_map/ppermute | solution.py:78
  107.8 4.2 %spread_grad.1 = (bf16[4,32,512]{2,1,0:T(8,128)(2,1)S(1)}, bf16[4,32,512]{2,1,0:T(8,128)(2,1)S(1)}, bf16[4,32,512]{2,1,0:T(8,128)(2,1)S(1)}, bf16[4,32,512]{2,1,...) custom-call(bf16[1024,1024]{1,0:T(8,128)(2,1)S(1)} %get-tuple-elemen, ...), custom_call_target="tpu_custom_call" | custom-call | flops 2147483 | bytes 8388 | tf_op jit(solution)/shard_map/spread_grad/pallas_call | solution.py:448
  120.2 6.3 %collective-permute-done.34.rest_8_ = bf16[4,32,512]{2,1,0:T(8,128)(2,1)S(1)} collective-permute-done((bf16[4,32,512]{2,1,0:T(8,128)(2,1)S(1)}, bf16[4,32,512]{2,1,0:T(8,128)(2,1)S(1)}, u32[]{:S(2)}, u32[]{:S(2)}) %collective-permute-start.34) | collective-permute-done | bytes 131104 | tf_op jit(solution)/shard_map/ppermute | solution.py:78
  126.5 4.7 %collective-permute-start.40 = (bf16[4,32,512]{2,1,0:T(8,128)(2,1)S(1)}, bf16[4,32,512]{2,1,0:T(8,128)(2,1)S(1)}, u32[]{:S(2)}, u32[]{:S(2)}) collective-permute-start(bf16[4,32,512]{2,1,0:T(8,128)(2,1)S(1)} %get-tuple-element.260), channel_id=1, source_target_pairs={{0,26},{2,24},{4,30},{6,28},{8,2},{10,0},{12,6},{14,4},{16,10},{18... | collective-permute-start | bytes 393224 | tf_op jit(solution)/shard_map/ppermute | solution.py:78
  131.2 3.1 %collective-permute-start.42 = (bf16[4,32,512]{2,1,0:T(8,128)(2,1)S(1)}, bf16[4,32,512]{2,1,0:T(8,128)(2,1)S(1)}, u32[]{:S(2)}, u32[]{:S(2)}) collective-permute-start(bf16[4,32,512]{2,1,0:T(8,128)(2,1)S(1)} %get-tuple-element.266), channel_id=1, source_target_pairs={{0,12},{2,14},{4,8},{6,10},{8,20},{10,22},{12,16},{14,18},{16,28},... | collective-permute-start | bytes 393224 | tf_op jit(solution)/shard_map/ppermute | solution.py:78
  136.5 3.6 %collective-permute-start.44 = (bf16[4,32,512]{2,1,0:T(8,128)(2,1)S(1)}, bf16[4,32,512]{2,1,0:T(8,128)(2,1)S(1)}, u32[]{:S(2)}, u32[]{:S(2)}) collective-permute-start(bf16[4,32,512]{2,1,0:T(8,128)(2,1)S(1)} %get-tuple-element.270), channel_id=1, source_target_pairs={{0,20},{2,22},{4,16},{6,18},{8,28},{10,30},{12,24},{14,26},{16,4},... | collective-permute-start | bytes 393224 | tf_op jit(solution)/shard_map/ppermute | solution.py:78
  140.1 5.4 %collective-permute-start.45 = (bf16[4,32,512]{2,1,0:T(8,128)(2,1)S(1)}, bf16[4,32,512]{2,1,0:T(8,128)(2,1)S(1)}, u32[]{:S(2)}, u32[]{:S(2)}) collective-permute-start(bf16[4,32,512]{2,1,0:T(8,128)(2,1)S(1)} %get-tuple-element.271), channel_id=1, source_target_pairs={{0,22},{2,20},{4,18},{6,16},{8,30},{10,28},{12,26},{14,24},{16,6},... | collective-permute-start | bytes 393224 | tf_op jit(solution)/shard_map/ppermute | solution.py:78
  145.5 4.2 %collective-permute-start.46 = (bf16[4,32,512]{2,1,0:T(8,128)(2,1)S(1)}, bf16[4,32,512]{2,1,0:T(8,128)(2,1)S(1)}, u32[]{:S(2)}, u32[]{:S(2)}) collective-permute-start(bf16[4,32,512]{2,1,0:T(8,128)(2,1)S(1)} %get-tuple-element.274), channel_id=1, source_target_pairs={{0,28},{2,30},{4,24},{6,26},{8,4},{10,6},{12,0},{14,2},{16,12},{18... | collective-permute-start | bytes 393224 | tf_op jit(solution)/shard_map/ppermute | solution.py:78
  149.7 3.0 %collective-permute-start.47 = (bf16[4,32,512]{2,1,0:T(8,128)(2,1)S(1)}, bf16[4,32,512]{2,1,0:T(8,128)(2,1)S(1)}, u32[]{:S(2)}, u32[]{:S(2)}) collective-permute-start(bf16[4,32,512]{2,1,0:T(8,128)(2,1)S(1)} %get-tuple-element.275), channel_id=1, source_target_pairs={{0,30},{2,28},{4,26},{6,24},{8,6},{10,4},{12,2},{14,0},{16,14},{18... | collective-permute-start | bytes 393224 | tf_op jit(solution)/shard_map/ppermute | solution.py:78
  152.7 5.8 %left_gradient.1 = (f32[64,32]{1,0:T(8,128)S(1)}, f32[64,32]{1,0:T(8,128)S(1)}) custom-call(bf16[4,32,512]{2,1,0:T(8,128)(2,1)} %copy-done.4, bf16[4,32,512]{2,1,0:T(8,128)(2,1)} %copy-done.12, bf16[4,32,512]{2,1,0:T(8,128)(2,1)} %copy-done.13, bf16[4,32,512]{2,1,0:T(8,128)(2,1)} %copy-done.14, bf16[4,32,512]{2,1,0:T(8,128)(2,1)} %copy-done.15, ...), custom_call_target="tpu_custom_call" | custom-call | flops 2147483 | bytes 8388 | tf_op jit(solution)/shard_map/left_gradient/pallas_call | solution.py:516
  158.6 4.2 %second_mix.1 = (bf16[4,32,512]{2,1,0:T(8,128)(2,1)S(1)}, bf16[4,32,512]{2,1,0:T(8,128)(2,1)S(1)}, bf16[4,32,512]{2,1,0:T(8,128)(2,1)S(1)}, bf16[4,32,512]{2,1,0...) custom-call(bf16[1024,1024]{1,0:T(8,128)(2,1)S(1)} %get-tuple-elemen, ...), custom_call_target="tpu_custom_call" | custom-call | flops 2147483 | bytes 8388 | tf_op jit(solution)/shard_map/second_mix/pallas_call | solution.py:448
  171.3 9.3 %collective-permute-done.49.rest_8_ = bf16[4,32,512]{2,1,0:T(8,128)(2,1)S(1)} collective-permute-done((bf16[4,32,512]{2,1,0:T(8,128)(2,1)S(1)}, bf16[4,32,512]{2,1,0:T(8,128)(2,1)S(1)}, u32[]{:S(2)}, u32[]{:S(2)}) %collective-permute-start.49) | collective-permute-done | bytes 131104 | tf_op jit(solution)/shard_map/ppermute | solution.py:78
  180.7 5.1 %collective-permute-start.56 = (bf16[4,32,512]{2,1,0:T(8,128)(2,1)S(1)}, bf16[4,32,512]{2,1,0:T(8,128)(2,1)S(1)}, u32[]{:S(2)}, u32[]{:S(2)}) collective-permute-start(bf16[4,32,512]{2,1,0:T(8,128)(2,1)S(1)} %get-tuple-element.339), channel_id=1, source_target_pairs={{0,12},{2,14},{4,8},{6,10},{8,20},{10,22},{12,16},{14,18},{16,28},... | collective-permute-start | bytes 393224 | tf_op jit(solution)/shard_map/ppermute | solution.py:78
  198.7 5.7 %back_first.1 = (f32[4,8,512]{2,1,0:T(8,128)S(1)}, f32[4,512,512]{2,1,0:T(8,128)S(1)}, f32[512,256]{1,0:T(8,128)S(1)}, f32[512,256]{1,0:T(8,128)S(1)}) custom-call(f32[4,512,512]{2,1,0:T(8,128)S(1)} %get-tuple-element.194.first_ref, bf16[4,512,512]{2,1,0:T(8,128)(2,1)S(1)} %get-tuple-element.193.nb_ref, bf16[512,512]{1,0:T(8,128)(2,1)S(1)} %pad_maximum_fusion.right_ref, ...), custom_call_target="tpu_custom_call" | custom-call | flops 2147483 | bytes 12582 | tf_op jit(solution)/shard_map/back_first/pallas_call | solution.py:562
  207.0 7.4 %finish.1 = (bf16[2048,512]{1,0:T(8,128)(2,1)}, f32[2048,512]{1,0:T(8,128)S(1)}, f32[8,2048]{1,0:T(8,128)S(1)}, f32[8,256]{1,0:T(8,128)S(1)}) custom-call(bf16[2048,512]{1,0:T(8,128)(2,1)S(1)} %copy-done.1, bf16[2048,512]{1,0:T(8,128)(2,1)S(1)} %copy-done.3, f32[8,2048]{1,0:T(8,128)S(1)} %squares.1.sa_ref, f32[8,2048]{1,0:T(8,128)S(1)} %collective-permute-done.sb_ref, ...), custom_call_target="tpu_custom_call" | custom-call | flops 41943 | bytes 16777 | tf_op jit(solution)/shard_map/finish/pallas_call | solution.py:614
  220.2 3.0 %token_gradient.1 = bf16[2048,512]{1,0:T(8,128)(2,1)} custom-call(bf16[2048,512]{1,0:T(8,128)(2,1)S(1)} %copy-done.1, f32[2048,512]{1,0:T(8,128)S(1)} %get-tuple-element.350.scaled_ref, f32[8,2048]{1,0:T(8,128)S(1)} %squares.1.sa_ref, f32[8,2048]{1,0:T(8,128)S(1)} %collective-permute-done.sb_ref, f32[8,2048]{1,0:T(8,128)S(1)} %get-tuple-element.351.ia_ref, ...), custom_call_target="tpu_custom_call" | custom-call | flops 5242 | bytes 8388 | tf_op jit(solution)/shard_map/token_gradient/pallas_call | solution.py:638
  (277 shorter events, 104.7 us)
Async XLA Ops:
  20.4 37.7 %collective-permute-start.1 = (bf16[256,512]{1,0:T(8,128)(2,1)}, bf16[256,512]{1,0:T(8,128)(2,1)}, u32[]{:S(2)}, u32[]{:S(2)}) collective-permute-start(bf16[256,512]{1,0:T(8,128)(2,1)} %param.13), channel_id=1, source_target_pairs={{0,1},{1,0},{2,3},{3,2},{4,5},{5,4},{6,7},{7,6},{8,9},{9,8},{10,11... | collective-permute-start | bytes 786440 | tf_op jit(solution)/shard_map/ppermute | solution.py:106
  22.4 20.2 %collective-permute-start.10 = (bf16[4,32,512]{2,1,0:T(8,128)(2,1)S(1)}, bf16[4,32,512]{2,1,0:T(8,128)(2,1)}, u32[]{:S(2)}, u32[]{:S(2)}) collective-permute-start(bf16[4,32,512]{2,1,0:T(8,128)(2,1)S(1)} %get-tuple-element.204), channel_id=1, source_target_pairs={{0,16},{2,18},{4,20},{6,22},{8,24},{10,26},{12,28},{14,30},{16,0},... | collective-permute-start | bytes 393224 | tf_op jit(solution)/shard_map/ppermute | solution.py:78
  25.6 22.1 %collective-permute-start.11 = (bf16[4,32,512]{2,1,0:T(8,128)(2,1)S(1)}, bf16[4,32,512]{2,1,0:T(8,128)(2,1)}, u32[]{:S(2)}, u32[]{:S(2)}) collective-permute-start(bf16[4,32,512]{2,1,0:T(8,128)(2,1)S(1)} %get-tuple-element.205), channel_id=1, source_target_pairs={{0,18},{2,16},{4,22},{6,20},{8,26},{10,24},{12,30},{14,28},{16,2},... | collective-permute-start | bytes 393224 | tf_op jit(solution)/shard_map/ppermute | solution.py:78
  28.5 22.0 %collective-permute-start.12 = (bf16[4,32,512]{2,1,0:T(8,128)(2,1)S(1)}, bf16[4,32,512]{2,1,0:T(8,128)(2,1)}, u32[]{:S(2)}, u32[]{:S(2)}) collective-permute-start(bf16[4,32,512]{2,1,0:T(8,128)(2,1)S(1)} %get-tuple-element.206), channel_id=1, source_target_pairs={{0,20},{2,22},{4,16},{6,18},{8,28},{10,30},{12,24},{14,26},{16,4},... | collective-permute-start | bytes 393224 | tf_op jit(solution)/shard_map/ppermute | solution.py:78
  32.4 30.9 %collective-permute-start.13 = (bf16[4,32,512]{2,1,0:T(8,128)(2,1)S(1)}, bf16[4,32,512]{2,1,0:T(8,128)(2,1)S(1)}, u32[]{:S(2)}, u32[]{:S(2)}) collective-permute-start(bf16[4,32,512]{2,1,0:T(8,128)(2,1)S(1)} %get-tuple-element.207), channel_id=1, source_target_pairs={{0,22},{2,20},{4,18},{6,16},{8,30},{10,28},{12,26},{14,24},{16,6},... | collective-permute-start | bytes 393224 | tf_op jit(solution)/shard_map/ppermute | solution.py:78
  42.6 21.3 %collective-permute-start.14 = (bf16[4,32,512]{2,1,0:T(8,128)(2,1)S(1)}, bf16[4,32,512]{2,1,0:T(8,128)(2,1)S(1)}, u32[]{:S(2)}, u32[]{:S(2)}) collective-permute-start(bf16[4,32,512]{2,1,0:T(8,128)(2,1)S(1)} %get-tuple-element.208), channel_id=1, source_target_pairs={{0,24},{2,26},{4,28},{6,30},{8,0},{10,2},{12,4},{14,6},{16,8},{18,... | collective-permute-start | bytes 393224 | tf_op jit(solution)/shard_map/ppermute | solution.py:78
  66.6 17.0 %collective-permute-start.21 = (bf16[4,32,512]{2,1,0:T(8,128)(2,1)S(1)}, bf16[4,32,512]{2,1,0:T(8,128)(2,1)S(1)}, u32[]{:S(2)}, u32[]{:S(2)}) collective-permute-start(bf16[4,32,512]{2,1,0:T(8,128)(2,1)S(1)} %get-tuple-element.215), channel_id=1, source_target_pairs={{0,24},{2,26},{4,28},{6,30},{8,0},{10,2},{12,4},{14,6},{16,8},{18,... | collective-permute-start | bytes 393224 | tf_op jit(solution)/shard_map/ppermute | solution.py:78
  69.0 17.5 %collective-permute-start.22 = (bf16[4,32,512]{2,1,0:T(8,128)(2,1)S(1)}, bf16[4,32,512]{2,1,0:T(8,128)(2,1)S(1)}, u32[]{:S(2)}, u32[]{:S(2)}) collective-permute-start(bf16[4,32,512]{2,1,0:T(8,128)(2,1)S(1)} %get-tuple-element.216), channel_id=1, source_target_pairs={{0,4},{2,6},{4,0},{6,2},{8,12},{10,14},{12,8},{14,10},{16,20},{18,... | collective-permute-start | bytes 393224 | tf_op jit(solution)/shard_map/ppermute | solution.py:78
  69.5 20.1 %collective-permute-start.23 = (bf16[4,32,512]{2,1,0:T(8,128)(2,1)S(1)}, bf16[4,32,512]{2,1,0:T(8,128)(2,1)S(1)}, u32[]{:S(2)}, u32[]{:S(2)}) collective-permute-start(bf16[4,32,512]{2,1,0:T(8,128)(2,1)S(1)} %get-tuple-element.217), channel_id=1, source_target_pairs={{0,18},{2,16},{4,22},{6,20},{8,26},{10,24},{12,30},{14,28},{16,2},... | collective-permute-start | bytes 393224 | tf_op jit(solution)/shard_map/ppermute | solution.py:78
  86.5 18.3 %collective-permute-start.27 = (bf16[4,32,512]{2,1,0:T(8,128)(2,1)S(1)}, bf16[4,32,512]{2,1,0:T(8,128)(2,1)S(1)}, u32[]{:S(2)}, u32[]{:S(2)}) collective-permute-start(bf16[4,32,512]{2,1,0:T(8,128)(2,1)S(1)} %get-tuple-element.243), channel_id=1, source_target_pairs={{0,12},{2,14},{4,8},{6,10},{8,20},{10,22},{12,16},{14,18},{16,28},... | collective-permute-start | bytes 393224 | tf_op jit(solution)/shard_map/ppermute | solution.py:78
  89.6 22.6 %collective-permute-start.28 = (bf16[4,32,512]{2,1,0:T(8,128)(2,1)S(1)}, bf16[4,32,512]{2,1,0:T(8,128)(2,1)S(1)}, u32[]{:S(2)}, u32[]{:S(2)}) collective-permute-start(bf16[4,32,512]{2,1,0:T(8,128)(2,1)S(1)} %get-tuple-element.244), channel_id=1, source_target_pairs={{0,14},{2,12},{4,10},{6,8},{8,22},{10,20},{12,18},{14,16},{16,30},... | collective-permute-start | bytes 393224 | tf_op jit(solution)/shard_map/ppermute | solution.py:78
  89.6 24.0 %collective-permute-start.29 = (bf16[4,32,512]{2,1,0:T(8,128)(2,1)S(1)}, bf16[4,32,512]{2,1,0:T(8,128)(2,1)S(1)}, u32[]{:S(2)}, u32[]{:S(2)}) collective-permute-start(bf16[4,32,512]{2,1,0:T(8,128)(2,1)S(1)} %get-tuple-element.247), channel_id=1, source_target_pairs={{0,20},{2,22},{4,16},{6,18},{8,28},{10,30},{12,24},{14,26},{16,4},... | collective-permute-start | bytes 393224 | tf_op jit(solution)/shard_map/ppermute | solution.py:78
  91.3 22.3 %collective-permute-start.30 = (bf16[4,32,512]{2,1,0:T(8,128)(2,1)S(1)}, bf16[4,32,512]{2,1,0:T(8,128)(2,1)S(1)}, u32[]{:S(2)}, u32[]{:S(2)}) collective-permute-start(bf16[4,32,512]{2,1,0:T(8,128)(2,1)S(1)} %get-tuple-element.248), channel_id=1, source_target_pairs={{0,22},{2,20},{4,18},{6,16},{8,30},{10,28},{12,26},{14,24},{16,6},... | collective-permute-start | bytes 393224 | tf_op jit(solution)/shard_map/ppermute | solution.py:78
  119.4 17.0 %collective-permute-start.38 = (bf16[4,32,512]{2,1,0:T(8,128)(2,1)S(1)}, bf16[4,32,512]{2,1,0:T(8,128)(2,1)S(1)}, u32[]{:S(2)}, u32[]{:S(2)}) collective-permute-start(bf16[4,32,512]{2,1,0:T(8,128)(2,1)S(1)} %get-tuple-element.258), channel_id=1, source_target_pairs={{0,18},{2,16},{4,22},{6,20},{8,26},{10,24},{12,30},{14,28},{16,2},... | collective-permute-start | bytes 393224 | tf_op jit(solution)/shard_map/ppermute | solution.py:78
  131.2 18.5 %collective-permute-start.42 = (bf16[4,32,512]{2,1,0:T(8,128)(2,1)S(1)}, bf16[4,32,512]{2,1,0:T(8,128)(2,1)S(1)}, u32[]{:S(2)}, u32[]{:S(2)}) collective-permute-start(bf16[4,32,512]{2,1,0:T(8,128)(2,1)S(1)} %get-tuple-element.266), channel_id=1, source_target_pairs={{0,12},{2,14},{4,8},{6,10},{8,20},{10,22},{12,16},{14,18},{16,28},... | collective-permute-start | bytes 393224 | tf_op jit(solution)/shard_map/ppermute | solution.py:78
  136.4 27.1 %collective-permute-start.43 = (bf16[4,32,512]{2,1,0:T(8,128)(2,1)S(1)}, bf16[4,32,512]{2,1,0:T(8,128)(2,1)S(1)}, u32[]{:S(2)}, u32[]{:S(2)}) collective-permute-start(bf16[4,32,512]{2,1,0:T(8,128)(2,1)S(1)} %get-tuple-element.267), channel_id=1, source_target_pairs={{0,14},{2,12},{4,10},{6,8},{8,22},{10,20},{12,18},{14,16},{16,30},... | collective-permute-start | bytes 393224 | tf_op jit(solution)/shard_map/ppermute | solution.py:78
  136.5 27.4 %collective-permute-start.44 = (bf16[4,32,512]{2,1,0:T(8,128)(2,1)S(1)}, bf16[4,32,512]{2,1,0:T(8,128)(2,1)S(1)}, u32[]{:S(2)}, u32[]{:S(2)}) collective-permute-start(bf16[4,32,512]{2,1,0:T(8,128)(2,1)S(1)} %get-tuple-element.270), channel_id=1, source_target_pairs={{0,20},{2,22},{4,16},{6,18},{8,28},{10,30},{12,24},{14,26},{16,4},... | collective-permute-start | bytes 393224 | tf_op jit(solution)/shard_map/ppermute | solution.py:78
  140.1 23.8 %collective-permute-start.45 = (bf16[4,32,512]{2,1,0:T(8,128)(2,1)S(1)}, bf16[4,32,512]{2,1,0:T(8,128)(2,1)S(1)}, u32[]{:S(2)}, u32[]{:S(2)}) collective-permute-start(bf16[4,32,512]{2,1,0:T(8,128)(2,1)S(1)} %get-tuple-element.271), channel_id=1, source_target_pairs={{0,22},{2,20},{4,18},{6,16},{8,30},{10,28},{12,26},{14,24},{16,6},... | collective-permute-start | bytes 393224 | tf_op jit(solution)/shard_map/ppermute | solution.py:78
  145.5 19.6 %collective-permute-start.46 = (bf16[4,32,512]{2,1,0:T(8,128)(2,1)S(1)}, bf16[4,32,512]{2,1,0:T(8,128)(2,1)S(1)}, u32[]{:S(2)}, u32[]{:S(2)}) collective-permute-start(bf16[4,32,512]{2,1,0:T(8,128)(2,1)S(1)} %get-tuple-element.274), channel_id=1, source_target_pairs={{0,28},{2,30},{4,24},{6,26},{8,4},{10,6},{12,0},{14,2},{16,12},{18... | collective-permute-start | bytes 393224 | tf_op jit(solution)/shard_map/ppermute | solution.py:78
  149.7 18.1 %collective-permute-start.47 = (bf16[4,32,512]{2,1,0:T(8,128)(2,1)S(1)}, bf16[4,32,512]{2,1,0:T(8,128)(2,1)S(1)}, u32[]{:S(2)}, u32[]{:S(2)}) collective-permute-start(bf16[4,32,512]{2,1,0:T(8,128)(2,1)S(1)} %get-tuple-element.275), channel_id=1, source_target_pairs={{0,30},{2,28},{4,26},{6,24},{8,6},{10,4},{12,2},{14,0},{16,14},{18... | collective-permute-start | bytes 393224 | tf_op jit(solution)/shard_map/ppermute | solution.py:78
  163.9 16.7 %collective-permute-start.49 = (bf16[4,32,512]{2,1,0:T(8,128)(2,1)S(1)}, bf16[4,32,512]{2,1,0:T(8,128)(2,1)S(1)}, u32[]{:S(2)}, u32[]{:S(2)}) collective-permute-start(bf16[4,32,512]{2,1,0:T(8,128)(2,1)S(1)} %get-tuple-element.311), channel_id=1, source_target_pairs={{0,16},{2,18},{4,20},{6,22},{8,24},{10,26},{12,28},{14,30},{16,0},... | collective-permute-start | bytes 393224 | tf_op jit(solution)/shard_map/ppermute | solution.py:78
  163.9 16.7 %collective-permute-start.50 = (bf16[4,32,512]{2,1,0:T(8,128)(2,1)S(1)}, bf16[4,32,512]{2,1,0:T(8,128)(2,1)S(1)}, u32[]{:S(2)}, u32[]{:S(2)}) collective-permute-start(bf16[4,32,512]{2,1,0:T(8,128)(2,1)S(1)} %get-tuple-element.312), channel_id=1, source_target_pairs={{0,8},{2,10},{4,12},{6,14},{8,16},{10,18},{12,20},{14,22},{16,24},... | collective-permute-start | bytes 393224 | tf_op jit(solution)/shard_map/ppermute | solution.py:78
  167.8 18.0 %collective-permute-start.52 = (bf16[4,32,512]{2,1,0:T(8,128)(2,1)S(1)}, bf16[4,32,512]{2,1,0:T(8,128)(2,1)S(1)}, u32[]{:S(2)}, u32[]{:S(2)}) collective-permute-start(bf16[4,32,512]{2,1,0:T(8,128)(2,1)S(1)} %get-tuple-element.314), channel_id=1, source_target_pairs={{0,4},{2,6},{4,0},{6,2},{8,12},{10,14},{12,8},{14,10},{16,20},{18,... | collective-permute-start | bytes 393224 | tf_op jit(solution)/shard_map/ppermute | solution.py:78
  186.3 18.3 %collective-permute-start.58 = (bf16[4,32,512]{2,1,0:T(8,128)(2,1)S(1)}, bf16[4,32,512]{2,1,0:T(8,128)(2,1)S(1)}, u32[]{:S(2)}, u32[]{:S(2)}) collective-permute-start(bf16[4,32,512]{2,1,0:T(8,128)(2,1)S(1)} %get-tuple-element.343), channel_id=1, source_target_pairs={{0,20},{2,22},{4,16},{6,18},{8,28},{10,30},{12,24},{14,26},{16,4},... | collective-permute-start | bytes 393224 | tf_op jit(solution)/shard_map/ppermute | solution.py:78
  (117 other events, 1935.3 us)
